TPU v7x, 32 devices: a whole 2x2x4 slice. The times are simulated.
32 devices in a mesh: grp: 8 (over z, x), band: 4 (over y, core).
Axes of the slice: x: 2, y: 2, z: 4, core: 2. Of those that a mesh axis runs over, the one named last changes fastest.
Arguments:
- state: float32 [80, 384, 1280], P('grp', 'band'), may hold values from -6 to 6
- pair_of_slot: int32 [256], replicated, may hold values from 0 to 255, each once
- legendre: float32 [256, 513, 384], P(('grp', 'band')), may hold values from -0.3125 to 0.3125
- diffusion: float32 [80], replicated, may hold values from 0.5 to 8
- w_in: bfloat16 [80, 1024], replicated, may hold values from -0.625 to 0.625
- w_out: bfloat16 [1024, 80], replicated, may hold values from -0.1875 to 0.1875
Outputs:
- new_state: float32 [80, 384, 1280], P('grp', 'band')
Inputs may be any that keep to these rules, and one draw needn't show every extreme that they name: `pair_of_slot`: each pair index appears in exactly one slot.
All inputs are finite; a program needn't handle non-finite values.
Results may differ from a plain program's by a relative error of at most 0.004.
Values may be sent and summed in bfloat16 or wider, within the bound.
No kernel may reach another device: no remote copies, remote signals or barrier semaphores. Data moves between devices by JAX's collectives and lax.ppermute only.
A program may use at most 128 MiB of HBM per device.

v0:
```python
import math

import jax
import jax.numpy as jnp
from jax import lax
from jax.sharding import PartitionSpec as P

NLON = 1280
M = 512


def fourier_basis(pair_index, points):
    upper_wave = M - 1 - pair_index
    wavenums = jnp.stack([pair_index, pair_index, upper_wave, upper_wave], axis=1)
    longitude = jnp.arange(points, dtype=jnp.int32)
    phases = wavenums[:, :, None] * longitude[None, None, :] % points
    angles = phases.astype(jnp.float32) * jnp.float32(2.0 * math.pi / points)
    cosine = jnp.cos(angles)
    sine_part = jnp.sin(angles)
    parity = (jnp.arange(4, dtype=jnp.int32) % 2 == 0)[None, :, None]
    forward = jnp.where(parity, cosine, -sine_part) / jnp.float32(points)
    weights = jnp.where(wavenums == 0, jnp.float32(1.0), jnp.float32(2.0))[:, :, None]
    inverse = jnp.where(parity, cosine, -sine_part) * weights
    return (forward, inverse)


def spectral_step(fields, legendre, pair_index, diffusion):
    projected = jnp.einsum("kjcl,krl->kjcr", fields, legendre, precision=lax.Precision.HIGHEST)
    row_index = jnp.arange(legendre.shape[1], dtype=jnp.int32)
    first_part = row_index[None, :] < (M - pair_index)[:, None]
    degree = jnp.where(
        first_part, pair_index[:, None] + row_index[None, :], row_index[None, :] - 1
    ).astype(jnp.float32)
    scaled = degree * (degree + 1.0) / jnp.float32(M * (M + 1))
    damping = jnp.exp(-diffusion[None, :, None] * scaled[:, None, :])
    keep_first = first_part[:, None, None, :]
    filtered = jnp.where(keep_first, projected[:, 0:2], projected[:, 2:4]) * damping[:, None]
    nothing = jnp.zeros_like(filtered)
    coeffs = jnp.concatenate(
        [jnp.where(keep_first, filtered, nothing), jnp.where(keep_first, nothing, filtered)], axis=1
    )
    return jnp.einsum("kjcr,krl->kjcl", coeffs, legendre, precision=lax.Precision.HIGHEST)


def shards(state, pair_of_slot, legendre, diffusion, w_in, w_out):
    groups = lax.axis_size("grp")
    bands = lax.axis_size("band")
    part_chans, lat_rows, lon_total = state.shape
    slot_count = legendre.shape[0]
    lat_total = legendre.shape[2]
    column_block = lax.all_to_all(
        state.astype(jnp.bfloat16), "grp", split_axis=2, concat_axis=0, tiled=True
    )
    channels = column_block.shape[0]
    lon_cols = column_block.shape[2]
    columns = column_block.reshape(channels, lat_rows * lon_cols)
    hidden = lax.dot_general(
        w_in, columns, (((0,), (0,)), ((), ())), preferred_element_type=jnp.float32
    )
    hidden = jax.nn.silu(hidden).astype(jnp.bfloat16)
    tendency = lax.dot_general(
        w_out, hidden, (((0,), (0,)), ((), ())), preferred_element_type=jnp.float32
    )
    tendency = tendency.reshape(channels, lat_rows, lon_cols)
    forward, inverse = fourier_basis(pair_of_slot, NLON)
    total_slots = forward.shape[0]
    flat_rows = state.reshape(part_chans * lat_rows, lon_total)
    spectra = lax.dot_general(
        forward.reshape(total_slots * 4, NLON),
        flat_rows,
        (((1,), (1,)), ((), ())),
        precision=lax.Precision.HIGHEST,
    )
    spectra = spectra.reshape(groups, bands, slot_count, 4, part_chans, lat_rows)
    gathered = lax.all_to_all(
        lax.all_to_all(spectra, "grp", split_axis=0, concat_axis=4, tiled=True),
        "band",
        split_axis=1,
        concat_axis=5,
        tiled=True,
    )
    device = lax.axis_index("grp") * bands + lax.axis_index("band")
    own_pairs = lax.dynamic_slice_in_dim(pair_of_slot, device * slot_count, slot_count)
    solved = spectral_step(
        gathered.reshape(slot_count, 4, channels, lat_total), legendre, own_pairs, diffusion
    )
    solved = solved.reshape(1, 1, slot_count, 4, channels, lat_total)
    returned = lax.all_to_all(
        lax.all_to_all(solved, "grp", split_axis=4, concat_axis=0, tiled=True),
        "band",
        split_axis=5,
        concat_axis=1,
        tiled=True,
    )
    coef_flat = returned.reshape(total_slots * 4, part_chans * lat_rows)
    dynamics = lax.dot_general(
        coef_flat,
        inverse.reshape(total_slots * 4, NLON),
        (((0,), (0,)), ((), ())),
        precision=lax.Precision.HIGHEST,
    )
    dynamics = dynamics.reshape(part_chans, lat_rows, lon_total)
    tendency_rows = lax.all_to_all(
        tendency.astype(jnp.bfloat16), "grp", split_axis=0, concat_axis=2, tiled=True
    ).astype(tendency.dtype)
    return dynamics + tendency_rows


def solution(mesh):
    return jax.shard_map(
        shards,
        mesh=mesh,
        in_specs=(P("grp", "band", None), P(), P(("grp", "band"), None, None), P(), P(), P()),
        out_specs=P("grp", "band", None),
        check_vma=False,
    )
```

profile of v0, /device:TPU:0, one launch (start us, length us, event | category | flops | bytes accessed | tf_op | source)
XLA Modules:
  0.0 802.2 jit_solution(14345487638428045147)
XLA Ops:
  0.0 0.0 copy-start
  0.0 0.7 broadcast_subtract_fusion
  0.7 0.8 stack.23
  1.5 0.0 copy-start.8
  1.5 0.1 stack.24
  1.6 0.1 pad_add_fusion
  1.7 46.9 %fusion.16 = f32[8,4,8,4,10,96]{5,2,4,3,1,0:T(8,128)} fusion(f32[10,96,1280]{2,1,0:T(8,128)} %param.6, s32[8,4,8,4]{2,3,1,0:T(4,128)S(1)} %pad_add_fusion, pred[4]{0:T(512)(128)(4,1)S(1)} %fusion.63), kind=kOutput, calls=%fused_computation.19 | convolution fusion | flops 15115223040 | bytes 8851460 | tf_op jit(solution)/shard_map/dot_general | solution.py:68
  48.6 0.0 copy-done.6
  48.6 0.0 copy-done.8
  48.6 7.6 all-to-all-start
  56.2 2.7 convert_element_type.49
  58.8 5.8 copy.76
  64.6 9.3 %reshape.204 = bf16[8,2,76800]{2,1,0:T(2,128)(2,1)} reshape(bf16[1280,10,96]{2,1,0:T(8,128)(2,1)} %bitcast.83) | data formatting | bytes 4915200
  73.9 97.9 %all-to-all-done = f32[8,4,8,4,10,96]{5,2,4,3,1,0:T(8,128)} async-done(((f32[8,4,8,4,10,96]{5,2,4,3,1,0:T(8,128)}), f32[8,4,8,4,10,96]{5,2,4,3,1,0:T(8,128)}, u32[]{:S(2)}, u32[]{:S(2)}) %all-to-all-start) | async-done | bytes 3932192 | tf_op jit(solution)/shard_map/all_to_all | solution.py:76
  171.8 3.6 all-to-all-start.4
  175.5 5.5 copy.63
  181.0 50.6 %all-to-all-done.4 = bf16[8,2,76800]{2,1,0:T(2,128)(2,1)S(1)} async-done(((bf16[8,2,76800]{2,1,0:T(2,128)(2,1)}), bf16[8,2,76800]{2,1,0:T(2,128)(2,1)S(1)}, u32[]{:S(2)}, u32[]{:S(2)}) %all-to-all-start.4) | async-done | bytes 2457632 | tf_op jit(solution)/shard_map/all_to_all | solution.py:51
  231.6 5.2 all-to-all-start.1
  236.8 0.0 copy-done.11
  236.9 0.1 broadcast_subtract_fusion.1
  236.9 0.1 iota_compare_fusion
  237.0 0.1 fusion.62
  237.1 1.5 multiply_exponential_fusion
  238.6 6.8 reshape.205
  245.4 7.9 copy.78
  253.3 8.8 %reshape.196 = bf16[80,15360]{1,0:T(8,128)(2,1)} reshape(bf16[8,10,96,160]{3,2,1,0:T(8,128)(2,1)} %copy.78) | data formatting | bytes 4915200 | tf_op jit(solution)/shard_map/reshape | solution.py:56
  262.1 34.2 %all-to-all-done.1 = f32[1,4,8,4,80,96]{5,2,4,3,0,1:T(8,128)} async-done(((f32[1,4,8,4,80,96]{5,2,4,3,0,1:T(8,128)}), f32[1,4,8,4,80,96]{5,2,4,3,0,1:T(8,128)}, u32[]{:S(2)}, u32[]{:S(2)}) %all-to-all-start.1) | async-done | bytes 3932192 | tf_op jit(solution)/shard_map/all_to_all | solution.py:75
  296.3 8.2 %copy.65 = f32[1,1,8,4,80,4,96]{6,5,4,3,2,1,0:T(4,128)} copy(f32[1,1,8,4,80,4,96]{6,2,4,3,5,1,0:T(8,128)} %bitcast.9) | data formatting | bytes 7864320 | tf_op jit(solution)/shard_map/all_to_all | solution.py:75
  304.5 7.1 reshape.193
  311.6 0.0 slice-start.1
  311.6 17.2 %fusion.10 = f32[8,4,80,513]{3,2,1,0:T(8,128)S(1)} fusion(f32[8,4,80,384]{3,2,1,0:T(8,128)} %reshape.193, f32[8,513,384,1]{2,0,1,3:T(8,128)} %bitcast.77), kind=kOutput, calls=%fused_computation.13 | convolution fusion | flops 6051594240 | bytes 15489024 | tf_op jit(solution)/shard_map/kjcl,krl->kjcr/dot_general | solution.py:28
  328.9 0.6 broadcast_select_fusion.1
  329.5 12.2 %fusion.57 = f32[1,1,8,4,80,384]{5,4,3,2,1,0:T(8,128)S(1)} fusion(f32[8,513,384,1]{2,0,1,3:T(8,128)S(1)} %bitcast.80, f32[8,2,80,513]{3,2,1,0:T(8,128)S(1)} %get-tuple-element.8, f32[8,2,80,513]{3,2,1,0:T(8,128)S(1)} %get-tuple-element.7), kind=kOutput, calls=%fused_computation.57 | convolution fusion | flops 6052907520 | bytes 15489024 | tf_op jit(solution)/shard_map/kjcr,krl->kjcl/dot_general | solution.py:42
  341.7 3.4 copy.68
  345.1 5.2 all-to-all-start.2
  350.3 25.4 %fusion.2 = bf16[80,15360]{1,0:T(8,128)(2,1)} fusion(bf16[1024,80]{0,1:T(8,128)(2,1)S(1)} %copy-done, bf16[80,1024]{1,0:T(8,128)(2,1)S(1)} %copy-done.10, bf16[80,15360]{1,0:T(8,128)(2,1)S(1)} %copy-done.3), kind=kOutput, calls=%fused_computation.3 | convolution fusion | flops 5113036800 | bytes 5242880 | tf_op jit(solution)/shard_map/dot_general | solution.py:61
  375.7 7.4 convert_element_type.53
  383.1 6.0 copy.79
  389.1 48.7 %all-to-all-done.2 = f32[1,1,8,4,80,384]{5,3,2,1,0,4:T(4,128)} async-done(((f32[1,1,8,4,80,384]{5,3,2,1,0,4:T(4,128)}), f32[1,1,8,4,80,384]{5,3,2,1,0,4:T(4,128)}, u32[]{:S(2)}, u32[]{:S(2)}) %all-to-all-start.2) | async-done | bytes 3932192 | tf_op jit(solution)/shard_map/all_to_all | solution.py:89
  437.8 3.7 all-to-all-start.5
  441.5 4.3 copy.69
  445.8 39.6 %copy.70 = f32[8,1,8,4,10,384]{4,2,3,1,0,5:T(8,128)} copy(f32[8,1,8,4,10,384]{5,2,4,0,3,1:T(8,128)} %bitcast.87) | data formatting | bytes 7864320 | tf_op jit(solution)/shard_map/all_to_all | solution.py:89
  485.4 75.6 %reshape.206 = f32[4,1,245760]{2,1,0:T(1,128)} reshape(f32[384,8,1,4,8,10]{5,4,3,2,1,0:T(8,128)} %bitcast.74) | data formatting | bytes 7864320
  560.9 0.0 copy-start.5
  561.0 0.0 all-to-all-done.5
  561.0 4.8 all-to-all-start.3
  565.8 0.1 copy.74
  566.0 0.1 mul.109
  566.1 0.1 copy.75
  566.2 0.1 select_n.85
  566.4 0.1 broadcast_in_dim.68
  566.5 24.2 %fusion.84 = f32[1024,1280,1]{1,0,2:T(8,128)} fusion(f32[1024]{0:T(1024)S(1)} %select_n.85, s32[1024]{0:T(1024)S(1)} %mul.109, pred[1024]{0:T(1024)(128)(4,1)S(1)} %broadcast_in_dim.68), kind=kLoop, calls=%fused_computation.22.clone.clone.clone.1 | loop fusion | flops 15728640 | bytes 5252096 | tf_op jit(solution)/shard_map/dot_general | solution.py:96
  590.8 0.9 convert_bitcast_fusion
  591.7 3.3 copy.80
  594.9 6.3 copy.81
  601.3 9.9 %all-to-all-done.3 = f32[4,1,245760]{2,1,0:T(1,128)} async-done(((f32[4,1,245760]{2,1,0:T(1,128)}), f32[4,1,245760]{2,1,0:T(1,128)}, u32[]{:S(2)}, u32[]{:S(2)}) %all-to-all-start.3) | async-done | bytes 3932192 | tf_op jit(solution)/shard_map/all_to_all | solution.py:88
  611.2 0.6 broadcast.186
  611.8 33.5 %reduce = f32[4,245760]{1,0:T(4,128)} reduce(f32[4,1,245760]{2,1,0:T(1,128)} %all-to-all-done.3, f32[]{:T(128)} %broadcast.186), dimensions={1}, to_apply=%all_to_all.77.reduce_sub_computation | reduce | bytes 7864324 | tf_op jit(solution)/shard_map/all_to_all | solution.py:88
  645.3 77.4 %reshape.207 = f32[384,8,1,4,8,10]{5,4,3,2,1,0:T(8,128)} reshape(f32[4,245760]{1,0:T(4,128)} %reduce) | data formatting | bytes 7864320
  722.7 34.6 %copy.90 = f32[8,1,8,4,10,4,96]{6,5,2,4,3,0,1:T(4,128)} copy(f32[8,1,8,4,10,4,96]{4,2,3,0,6,5,1:T(8,128)} %bitcast.75) | data formatting | bytes 7864320 | tf_op jit(solution)/shard_map/all_to_all | solution.py:88
  757.3 8.9 %copy.72 = f32[8,4,1,8,4,10,96]{6,5,4,3,1,0,2:T(8,128)} copy(f32[8,4,1,8,4,10,96]{6,1,3,5,4,0,2:T(4,128)} %bitcast.84) | data formatting | bytes 7864320 | tf_op jit(solution)/shard_map/all_to_all | solution.py:88
  766.1 7.8 reshape.195
  773.9 5.6 copy.73
  779.5 22.2 %fusion.41 = f32[10,96,1280]{2,1,0:T(8,128)} fusion(f32[10,96,1280]{2,1,0:T(8,128)} %copy.81, f32[10,96,1024]{2,1,0:T(8,128)} %bitcast.86, f32[1024,1280,1]{1,0,2:T(8,128)} %fusion.84), kind=kOutput, calls=%fused_computation.42 | convolution fusion | flops 15100723200 | bytes 19005440 | tf_op jit(solution)/shard_map/dot_general | solution.py:96
  (28 shorter events, 0.1 us)
Async XLA Ops:
  0.0 350.3 %copy-start = (bf16[1024,80]{0,1:T(8,128)(2,1)S(1)}, bf16[1024,80]{0,1:T(8,128)(2,1)}, u32[]{:S(2)}) copy-start(bf16[1024,80]{0,1:T(8,128)(2,1)} %param.11) | copy-start | bytes 491524
  0.7 47.9 %copy-start.6 = (s32[256]{0:T(256)}, s32[256]{0:T(256)S(1)}, u32[]{:S(2)}) copy-start(s32[256]{0:T(256)S(1)} %broadcast_subtract_fusion) | copy-start | bytes 3076
  1.5 47.1 %copy-start.8 = (pred[4]{0:T(512)(128)(4,1)}, pred[4]{0:T(512)(128)(4,1)S(1)}, u32[]{:S(2)}) copy-start(pred[4]{0:T(512)(128)(4,1)S(1)} %fusion.63) | copy-start | bytes 16
  48.6 123.3 %all-to-all-start = ((f32[8,4,8,4,10,96]{5,2,4,3,1,0:T(8,128)}), f32[8,4,8,4,10,96]{5,2,4,3,1,0:T(8,128)}, u32[]{:S(2)}, u32[]{:S(2)}) async-start(f32[8,4,8,4,10,96]{5,2,4,3,1,0:T(8,128)} %fusion.16), calls=%async_computation | async-start | bytes 10485760 | tf_op jit(solution)/shard_map/all_to_all | solution.py:76
  171.8 59.8 %all-to-all-start.4 = ((bf16[8,2,76800]{2,1,0:T(2,128)(2,1)}), bf16[8,2,76800]{2,1,0:T(2,128)(2,1)S(1)}, u32[]{:S(2)}, u32[]{:S(2)}) async-start(bf16[8,2,76800]{2,1,0:T(2,128)(2,1)} %reshape.204), calls=%async_computation.4 | async-start | bytes 4915200 | tf_op jit(solution)/shard_map/all_to_all | solution.py:51
  231.6 5.2 copy-start.11
  231.6 5.2 copy-start.4
  231.6 64.6 %all-to-all-start.1 = ((f32[1,4,8,4,80,96]{5,2,4,3,0,1:T(8,128)}), f32[1,4,8,4,80,96]{5,2,4,3,0,1:T(8,128)}, u32[]{:S(2)}, u32[]{:S(2)}) async-start(f32[1,4,8,4,80,96]{5,2,4,3,0,1:T(8,128)} %bitcast.81), calls=%async_computation.1 | async-start | bytes 10485760 | tf_op jit(solution)/shard_map/all_to_all | solution.py:75
  304.5 25.0 %slice-start = ((s8[6303744]{0:T(1024)(128)(4,1)}), s8[2109440]{0:T(1024)(128)(4,1)S(1)}, s32[]{:S(2)}) async-start(s8[6303744]{0:T(1024)(128)(4,1)} %bitcast.78), calls=%async_computation.6 | async-start | bytes 4218880
  311.6 17.3 %copy-start.2 = (f32[8,80,513]{2,1,0:T(8,128)S(1)}, f32[8,80,513]{2,1,0:T(8,128)}, u32[]{:S(2)}) copy-start(f32[8,80,513]{2,1,0:T(8,128)} %multiply_exponential_fusion) | copy-start | bytes 3939844
  311.6 17.9 %slice-start.1 = ((s8[6303744]{0:T(1024)(128)(4,1)}), s8[4194304]{0:T(1024)(128)(4,1)S(1)}, s32[]{:S(2)}) async-start(s8[6303744]{0:T(1024)(128)(4,1)} %bitcast.78), calls=%async_computation.7 | async-start | bytes 8388608
  345.1 5.2 copy-start.3
  345.1 5.2 copy-start.10
  345.1 92.7 %all-to-all-start.2 = ((f32[1,1,8,4,80,384]{5,3,2,1,0,4:T(4,128)}), f32[1,1,8,4,80,384]{5,3,2,1,0,4:T(4,128)}, u32[]{:S(2)}, u32[]{:S(2)}) async-start(f32[1,1,8,4,80,384]{5,3,2,1,0,4:T(4,128)} %copy.68), calls=%async_computation.2 | async-start | bytes 7864320 | tf_op jit(solution)/shard_map/all_to_all | solution.py:89
  437.8 123.2 %all-to-all-start.5 = ((bf16[80,96,160]{1,2,0:T(8,128)(2,1)}), bf16[80,96,160]{1,2,0:T(8,128)(2,1)S(1)}, u32[]{:S(2)}, u32[]{:S(2)}) async-start(bf16[80,96,160]{1,2,0:T(8,128)(2,1)} %copy.79), calls=%async_computation.5 | async-start | bytes 6553600 | tf_op jit(solution)/shard_map/all_to_all | solution.py:103
  560.9 4.8 copy-start.5
  561.0 4.8 copy-start.7
  561.0 5.4 copy-start.9
  561.0 50.2 %all-to-all-start.3 = ((f32[4,1,245760]{2,1,0:T(1,128)}), f32[4,1,245760]{2,1,0:T(1,128)}, u32[]{:S(2)}, u32[]{:S(2)}) async-start(f32[4,1,245760]{2,1,0:T(1,128)} %reshape.206), calls=%async_computation.3 | async-start | bytes 7864320 | tf_op jit(solution)/shard_map/all_to_all | solution.py:88
  779.5 22.2 %copy-start.1 = (bf16[1024,80]{0,1:T(8,128)(2,1)S(1)}, bf16[1024,80]{0,1:T(8,128)(2,1)}, u32[]{:S(2)}) copy-start(bf16[1024,80]{0,1:T(8,128)(2,1)} %param.11) | copy-start | bytes 491524
where the time goes:
time: 813 us; the launch traced here: 802 us
  local copies, waits for them, and re-layouts  342 us (42%)
  waiting for transfers between devices  241 us (30%)
  matrix products  124 us (15%)
  other arithmetic  64.4 us (8%)
  starting transfers between devices  30 us (4%)
    unnamed x32, local copies, waits for them, and re-layouts  169 us
    all_to_all x1, waiting for transfers between devices, shards(): lax.all_to_all(spectra, 'grp', split_axis=0, concat_axis=4, tiled=True)  97.9 us
    all_to_all x1, waiting for transfers between devices, shards(): lax.all_to_all(state.astype(jnp.bfloat16), 'grp', split_axis=2, concat_ax...  50.6 us
    all_to_all x1, waiting for transfers between devices, shards(): lax.all_to_all(solved, 'grp', split_axis=4, concat_axis=0, tiled=True)  48.7 us
    dot_general x1, matrix products, shards(): lax.dot_general(forward.reshape(total_slots * 4, NLON), flat_rows, (((1,)...  46.9 us
    all_to_all x3, local copies, waits for them, and re-layouts, shards(): lax.all_to_all(lax.all_to_all(solved, 'grp', split_axis=4, concat_axis=0,...  44 us
    all_to_all x2, local copies, waits for them, and re-layouts, shards(): lax.all_to_all(solved, 'grp', split_axis=4, concat_axis=0, tiled=True)  43.9 us
    all_to_all x1, waiting for transfers between devices, shards(): lax.all_to_all(lax.all_to_all(spectra, 'grp', split_axis=0, concat_axis=4...  34.2 us
  transfers between devices with their start and end apart: 6, of which 5 were waited for; matrix products, arithmetic and copies ran while one was open for 30% of the time, Pallas kernels for 0%

commit v1 on v0

--- a/solution.py
+++ b/solution.py
@@ -1,16 +1,384 @@
+import functools
 import math
 
 import jax
 import jax.numpy as jnp
 from jax import lax
+from jax.experimental import pallas as pl
+from jax.experimental.pallas import tpu as pltpu
 from jax.sharding import PartitionSpec as P
 
-NLON = 1280
-M = 512
-
-
-def fourier_basis(pair_index, points):
-    upper_wave = M - 1 - pair_index
+LANES = 128
+ROWS = 8
+F32 = jnp.float32
+BF16 = jnp.bfloat16
+NT = (((1,), (1,)), ((), ()))
+NN = (((1,), (0,)), ((), ()))
+
+
+def mm(a, b, dims=NN):
+    return lax.dot_general(a, b, dims, preferred_element_type=F32)
+
+
+def halves(value):
+    high = value.astype(BF16)
+    return high, (value - high.astype(F32)).astype(BF16)
+
+
+def cost(flops, moved, special=0):
+    return pl.CostEstimate(flops=int(flops), bytes_accessed=int(moved), transcendentals=int(special))
+
+
+def params(mib):
+    return pltpu.CompilerParams(dimension_semantics=("arbitrary",), vmem_limit_bytes=mib << 20)
+
+
+def cut_kernel(tiles, state_ref, out_ref):
+    for tile in range(tiles):
+        out_ref[0, :, tile] = state_ref[:, :, tile * LANES : (tile + 1) * LANES].astype(BF16)
+
+
+def cut_columns(state, lat_cuts, lon_cuts):
+    chans, lats, lons = state.shape
+    rows, tiles = lats // lat_cuts, lons // lon_cuts // LANES
+    groups = lat_cuts * lon_cuts
+    return pl.pallas_call(
+        functools.partial(cut_kernel, tiles),
+        grid=(groups,),
+        in_specs=[
+            pl.BlockSpec((chans, rows, tiles * LANES), lambda g: (0, g // lon_cuts, g % lon_cuts))
+        ],
+        out_specs=pl.BlockSpec((1, chans, tiles, rows, LANES), lambda g: (g, 0, 0, 0, 0)),
+        out_shape=jax.ShapeDtypeStruct((groups, chans, tiles, rows, LANES), BF16),
+        compiler_params=params(32),
+        cost_estimate=cost(0, state.size * 6),
+        name="cut_columns",
+    )(state)
+
+
+def basis_tables(pair_index, points, waves):
+    upper = waves - 1 - pair_index
+    wavenums = jnp.stack([pair_index, pair_index, upper, upper], axis=1).reshape(-1, 1)
+    odd = (jnp.arange(wavenums.shape[0], dtype=jnp.int32) % 2 == 1)[:, None]
+    unit = jnp.float32(2.0 * math.pi / points)
+
+    def angles(at):
+        return (wavenums * at[None, :] % points).astype(F32) * unit
+
+    fine = angles(jnp.arange(LANES, dtype=jnp.int32))
+    coarse = angles(jnp.arange(points // LANES, dtype=jnp.int32) * LANES)
+    cosine, sine = jnp.cos(coarse), jnp.sin(coarse)
+    by_cos = jnp.where(odd, -sine, cosine)
+    by_sin = jnp.where(odd, -cosine, -sine)
+    return jnp.cos(fine), jnp.sin(fine), by_cos, by_sin
+
+
+def forward_kernel(owners, width, folds, state_ref, cos_ref, sin_ref, by_cos_ref, by_sin_ref,
+                   out_ref, high_ref, low_ref, state_high, state_low):
+    @pl.when(pl.program_id(0) == 0)
+    def _():
+        state_high[...], state_low[...] = halves(state_ref[...])
+
+    cosine, sine = cos_ref[...], sin_ref[...]
+    for tile in range(by_cos_ref.shape[1]):
+        at = slice(tile * LANES, (tile + 1) * LANES)
+        wave = by_cos_ref[:, tile : tile + 1] * cosine + by_sin_ref[:, tile : tile + 1] * sine
+        high_ref[:, at], low_ref[:, at] = halves(wave)
+    found = mm(high_ref[...], state_low[...], NT)
+    found += mm(low_ref[...], state_high[...], NT)
+    found += mm(high_ref[...], state_high[...], NT)
+    rows = out_ref.shape[1]
+    for owner in range(owners):
+        for fold in range(folds):
+            start = (owner * folds + fold) * rows
+            out_ref[owner, :, fold * width : (fold + 1) * width] = found[start : start + rows].astype(BF16)
+
+
+def forward_transform(flat, tables, devices, folds, step_rows):
+    width, points = flat.shape
+    total = tables[0].shape[0]
+    per_owner = total // devices
+    rows = per_owner // folds
+    owners = step_rows // per_owner
+    coarse = points // LANES
+    return pl.pallas_call(
+        functools.partial(forward_kernel, owners, width, folds),
+        grid=(total // step_rows,),
+        in_specs=[
+            pl.BlockSpec((width, points), lambda i: (0, 0)),
+            pl.BlockSpec((step_rows, LANES), lambda i: (i, 0)),
+            pl.BlockSpec((step_rows, LANES), lambda i: (i, 0)),
+            pl.BlockSpec((step_rows, coarse), lambda i: (i, 0)),
+            pl.BlockSpec((step_rows, coarse), lambda i: (i, 0)),
+        ],
+        out_specs=[
+            pl.BlockSpec((owners, rows, folds * width), lambda i: (i, 0, 0)),
+            pl.BlockSpec((step_rows, points), lambda i: (i, 0)),
+            pl.BlockSpec((step_rows, points), lambda i: (i, 0)),
+        ],
+        out_shape=[
+            jax.ShapeDtypeStruct((devices, rows, folds * width), BF16),
+            jax.ShapeDtypeStruct((total, points), BF16),
+            jax.ShapeDtypeStruct((total, points), BF16),
+        ],
+        scratch_shapes=[pltpu.VMEM((width, points), BF16), pltpu.VMEM((width, points), BF16)],
+        compiler_params=params(56),
+        cost_estimate=cost(6 * total * width * points, width * points * 4 + total * (points * 4 + width * 2)),
+        name="forward_transform",
+    )(flat, *tables)
+
+
+def physics_kernel(chans, rows, columns_ref, w_in_ref, w_out_ref, out_ref, spread, found):
+    spread[...] = columns_ref[...].astype(F32).reshape(chans * rows, LANES)
+    for group in range(rows // ROWS):
+        at = [pl.ds(group * ROWS + row, chans, stride=rows) for row in range(ROWS)]
+        columns = jnp.concatenate([spread[where, :].astype(BF16) for where in at], axis=1)
+        half = mm(w_in_ref[...], columns)
+        hidden = (half + half * jnp.tanh(half)).astype(BF16)
+        tendency = mm(w_out_ref[...], hidden)
+        for row in range(ROWS):
+            found[at[row], :] = tendency[:, row * LANES : (row + 1) * LANES]
+    out_ref[...] = found[...].astype(BF16).reshape(out_ref.shape)
+
+
+def physics(columns, w_in, w_out):
+    groups, per_group, tiles, rows, _ = columns.shape
+    chans, hidden = w_in.shape
+    spec = pl.BlockSpec((groups, per_group, 1, rows, LANES), lambda i: (0, 0, i, 0, 0))
+    count = tiles * rows * LANES
+    return pl.pallas_call(
+        functools.partial(physics_kernel, chans, rows),
+        grid=(tiles,),
+        in_specs=[
+            spec,
+            pl.BlockSpec((hidden, chans), lambda i: (0, 0)),
+            pl.BlockSpec((chans, hidden), lambda i: (0, 0)),
+        ],
+        out_specs=spec,
+        out_shape=jax.ShapeDtypeStruct(columns.shape, BF16),
+        scratch_shapes=[pltpu.VMEM((chans * rows, LANES), F32), pltpu.VMEM((chans * rows, LANES), F32)],
+        compiler_params=params(48),
+        cost_estimate=cost(4 * count * chans * hidden, count * chans * 4, count * hidden),
+        name="physics",
+    )(columns, w_in.T * jnp.asarray(0.5, BF16), w_out.T)
+
+
+def spectral_kernel(geometry, points, pairs_ref, got_ref, legendre_ref, diffusion_ref, out_ref,
+                    rows_ref, block_ref, high_ref, low_ref):
+    groups, bands, slots, per_group, lats, folds = geometry
+    devices = groups * bands
+    per_device = 4 * slots
+    fold_rows = per_device // folds
+    width = per_group * lats
+    degrees = legendre_ref.shape[1]
+    waves = degrees - 1
+    padded = high_ref.shape[0]
+    slot = pl.program_id(0)
+    chans = groups * per_group
+    spans = [(tile, tile * LANES, min(LANES, width - tile * LANES)) for tile in range(rows_ref.shape[0])]
+    fill = rows_ref.shape[0] * LANES - width
+
+    @pl.when(slot == 0)
+    def _():
+        for device in range(devices):
+            for fold in range(folds):
+                start = device * per_device + fold * fold_rows
+                for tile, at, lanes in spans:
+                    rows_ref[tile, start : start + fold_rows, 0:lanes] = got_ref[
+                        device, :, fold * width + at : fold * width + at + lanes
+                    ].astype(F32)
+        high_ref[...] = jnp.zeros_like(high_ref)
+        low_ref[...] = jnp.zeros_like(low_ref)
+
+    def rows_of(band, wave):
+        return pl.ds(band * per_device + 4 * slot + wave, groups, stride=bands * per_device)
+
+    for wave in range(4):
+        for band in range(bands):
+            piece = jnp.concatenate([rows_ref[tile, rows_of(band, wave), :] for tile, _, _ in spans], axis=1)
+            for chan in range(per_group):
+                row = (wave * per_group + chan) * groups
+                block_ref[row : row + groups, band * lats : (band + 1) * lats] = piece[
+                    :, chan * lats : (chan + 1) * lats
+                ]
+    high, low = halves(legendre_ref[0])
+    high_ref[0:degrees, :] = high
+    low_ref[0:degrees, :] = low
+    fields = block_ref[...].astype(BF16)
+    projected = mm(fields, low_ref[...], NT) + mm(fields, high_ref[...], NT)
+    pair = pairs_ref[slot]
+    row = lax.broadcasted_iota(jnp.int32, (1, padded), 1)
+    first = row < waves - pair
+    degree = jnp.where(first, pair + row, row - 1).astype(F32)
+    scaled = degree * (degree + 1.0) / F32(waves * (waves + 1))
+    wavenum = jnp.where(first, pair, waves - 1 - pair)
+    weight = jnp.where(wavenum == 0, F32(1.0 / points), F32(2.0 / points))
+    damping = jnp.exp(-diffusion_ref[...] * scaled) * weight
+    upper, lower = [], []
+    for part in range(2):
+        one = projected[part * chans : (part + 1) * chans]
+        two = projected[(2 + part) * chans : (3 + part) * chans]
+        kept = jnp.where(first, one, two) * damping
+        upper.append(jnp.where(first, kept, 0.0))
+        lower.append(jnp.where(first, 0.0, kept))
+    spec_high, spec_low = halves(jnp.concatenate(upper + lower, axis=0))
+    back = mm(spec_low, high_ref[...]) + mm(spec_high, low_ref[...]) + mm(spec_high, high_ref[...])
+    for wave in range(4):
+        for band in range(bands):
+            starts = [(wave * per_group + chan) * groups for chan in range(per_group)]
+            pieces = [back[start : start + groups, band * lats : (band + 1) * lats] for start in starts]
+            if fill:
+                pieces.append(jnp.zeros((groups, fill), F32))
+            line = jnp.concatenate(pieces, axis=1)
+            for tile, at, _ in spans:
+                rows_ref[tile, rows_of(band, wave), :] = line[:, at : at + LANES]
+
+    @pl.when(slot == slots - 1)
+    def _():
+        for device in range(devices):
+            for fold in range(folds):
+                start = device * per_device + fold * fold_rows
+                for tile, at, lanes in spans:
+                    out_ref[device, :, fold * width + at : fold * width + at + lanes] = rows_ref[
+                        tile, start : start + fold_rows, 0:lanes
+                    ].astype(BF16)
+
+
+def spectral_step(got, legendre, own_pairs, diffusion, groups, bands, folds, points):
+    slots, degrees, lat_total = legendre.shape
+    lats = lat_total // bands
+    chans = diffusion.shape[0]
+    per_group = chans // groups
+    padded = -(-degrees // LANES) * LANES
+    by_row = diffusion.reshape(groups, per_group).T.reshape(chans, 1)
+    geometry = (groups, bands, slots, per_group, lats, folds)
+    whole = lambda i, pairs: (0, 0, 0)
+    return pl.pallas_call(
+        functools.partial(spectral_kernel, geometry, points),
+        grid_spec=pltpu.PrefetchScalarGridSpec(
+            num_scalar_prefetch=1,
+            grid=(slots,),
+            in_specs=[
+                pl.BlockSpec(got.shape, whole),
+                pl.BlockSpec((1, degrees, lat_total), lambda i, pairs: (i, 0, 0)),
+                pl.BlockSpec((chans, 1), lambda i, pairs: (0, 0)),
+            ],
+            out_specs=pl.BlockSpec(got.shape, whole),
+            scratch_shapes=[
+                pltpu.VMEM((-(-per_group * lats // LANES), groups * bands * 4 * slots, LANES), F32),
+                pltpu.VMEM((4 * chans, lat_total), F32),
+                pltpu.VMEM((padded, lat_total), BF16),
+                pltpu.VMEM((padded, lat_total), BF16),
+            ],
+        ),
+        out_shape=jax.ShapeDtypeStruct(got.shape, BF16),
+        compiler_params=params(48),
+        cost_estimate=cost(40 * slots * chans * degrees * lat_total, slots * degrees * lat_total * 4),
+        name="spectral_step",
+    )(own_pairs, got, legendre, by_row)
+
+
+def inverse_kernel(geometry, back_ref, high_ref, low_ref, tendency_ref, out_ref, rows_ref, turned):
+    devices, fold_rows, folds, width, lat_cuts, lon_cuts, tiles = geometry
+    chans, lats, step_lons = out_ref.shape
+    rows = lats // lat_cuts
+
+    @pl.when(pl.program_id(0) == 0)
+    def _():
+        rows_ref[...] = jnp.zeros_like(rows_ref)
+        for device in range(devices):
+            for fold in range(folds):
+                start = (device * folds + fold) * fold_rows
+                rows_ref[start : start + fold_rows, 0:width] = back_ref[
+                    device, :, fold * width : (fold + 1) * width
+                ]
+        turned[...] = rows_ref[...].T
+
+    waves = turned[0:width, :]
+    found = mm(waves, low_ref[...]) + mm(waves, high_ref[...])
+    found = found.reshape(chans, lats, step_lons)
+    for part in range(step_lons // LANES):
+        tile = pl.program_id(0) * (step_lons // LANES) + part
+        for cut in range(lat_cuts):
+            at = slice(cut * rows, (cut + 1) * rows)
+            lanes = slice(part * LANES, (part + 1) * LANES)
+            out_ref[:, at, lanes] = found[:, at, lanes] + tendency_ref[
+                cut * lon_cuts + tile // tiles, :, tile % tiles
+            ].astype(F32)
+
+
+def inverse_transform(back, high, low, tendency, shape, lat_cuts, lon_cuts, step_lons):
+    chans, lats, lons = shape
+    devices, fold_rows, wide = back.shape
+    width = chans * lats
+    folds = wide // width
+    total = high.shape[0]
+    tiles = tendency.shape[2]
+    padded = -(-width // LANES) * LANES
+    geometry = (devices, fold_rows, folds, width, lat_cuts, lon_cuts, tiles)
+    return pl.pallas_call(
+        functools.partial(inverse_kernel, geometry),
+        grid=(lons // step_lons,),
+        in_specs=[
+            pl.BlockSpec(back.shape, lambda i: (0, 0, 0)),
+            pl.BlockSpec((total, step_lons), lambda i: (0, i)),
+            pl.BlockSpec((total, step_lons), lambda i: (0, i)),
+            pl.BlockSpec(tendency.shape, lambda i: (0, 0, 0, 0, 0)),
+        ],
+        out_specs=pl.BlockSpec((chans, lats, step_lons), lambda i: (0, 0, i)),
+        out_shape=jax.ShapeDtypeStruct(shape, F32),
+        scratch_shapes=[pltpu.VMEM((total, padded), BF16), pltpu.VMEM((padded, total), BF16)],
+        compiler_params=params(56),
+        cost_estimate=cost(4 * total * width * lons, total * lons * 4 + width * lons * 6),
+        name="inverse_transform",
+    )(back, high, low, tendency)
+
+
+def cuts_of(lats, lons, groups):
+    for lon_cuts in range(1, groups + 1):
+        if groups % lon_cuts or lons % (lon_cuts * LANES):
+            continue
+        lat_cuts = groups // lon_cuts
+        if lats % (lat_cuts * ROWS) == 0:
+            return lat_cuts, lon_cuts
+    return None
+
+
+def folds_of(width, per_device):
+    folds = LANES // math.gcd(width, LANES)
+    return folds if per_device % (folds * 2 * ROWS) == 0 else None
+
+
+def fast(state, pair_of_slot, legendre, diffusion, w_in, w_out):
+    groups = lax.axis_size("grp")
+    bands = lax.axis_size("band")
+    devices = groups * bands
+    chans, lats, lons = state.shape
+    slots, degrees, _ = legendre.shape
+    waves = degrees - 1
+    lat_cuts, lon_cuts = cuts_of(lats, lons, groups)
+    folds = folds_of(chans * lats, 4 * slots)
+    cut = cut_columns(state, lat_cuts, lon_cuts)
+    cut, pairs = lax.optimization_barrier((cut, pair_of_slot))
+    columns = lax.all_to_all(cut, "grp", 0, 0, tiled=True)
+    tables = basis_tables(pairs, lons, waves)
+    step_rows = min(8, devices) * 4 * slots
+    spectra, high, low = forward_transform(state.reshape(chans * lats, lons), tables, devices, folds, step_rows)
+    columns, spectra = lax.optimization_barrier((columns, spectra))
+    got = lax.all_to_all(spectra, ("grp", "band"), 0, 0, tiled=True)
+    tendency = physics(columns, w_in, w_out)
+    got, tendency = lax.optimization_barrier((got, tendency))
+    tendency = lax.all_to_all(tendency, "grp", 0, 0, tiled=True)
+    device = lax.axis_index("grp") * bands + lax.axis_index("band")
+    own_pairs = lax.dynamic_slice_in_dim(pairs, device * slots, slots)
+    solved = spectral_step(got, legendre, own_pairs, diffusion, groups, bands, folds, lons)
+    tendency, solved = lax.optimization_barrier((tendency, solved))
+    back = lax.all_to_all(solved, ("grp", "band"), 0, 0, tiled=True)
+    return inverse_transform(back, high, low, tendency, state.shape, lat_cuts, lon_cuts, 2 * LANES)
+
+
+def plain_basis(pair_index, points, waves):
+    upper_wave = waves - 1 - pair_index
     wavenums = jnp.stack([pair_index, pair_index, upper_wave, upper_wave], axis=1)
     longitude = jnp.arange(points, dtype=jnp.int32)
     phases = wavenums[:, :, None] * longitude[None, None, :] % points
@@ -24,14 +392,15 @@
     return (forward, inverse)
 
 
-def spectral_step(fields, legendre, pair_index, diffusion):
+def plain_spectral_step(fields, legendre, pair_index, diffusion):
+    waves = legendre.shape[1] - 1
     projected = jnp.einsum("kjcl,krl->kjcr", fields, legendre, precision=lax.Precision.HIGHEST)
     row_index = jnp.arange(legendre.shape[1], dtype=jnp.int32)
-    first_part = row_index[None, :] < (M - pair_index)[:, None]
+    first_part = row_index[None, :] < (waves - pair_index)[:, None]
     degree = jnp.where(
         first_part, pair_index[:, None] + row_index[None, :], row_index[None, :] - 1
     ).astype(jnp.float32)
-    scaled = degree * (degree + 1.0) / jnp.float32(M * (M + 1))
+    scaled = degree * (degree + 1.0) / jnp.float32(waves * (waves + 1))
     damping = jnp.exp(-diffusion[None, :, None] * scaled[:, None, :])
     keep_first = first_part[:, None, None, :]
     filtered = jnp.where(keep_first, projected[:, 0:2], projected[:, 2:4]) * damping[:, None]
@@ -42,7 +411,7 @@
     return jnp.einsum("kjcr,krl->kjcl", coeffs, legendre, precision=lax.Precision.HIGHEST)
 
 
-def shards(state, pair_of_slot, legendre, diffusion, w_in, w_out):
+def plain(state, pair_of_slot, legendre, diffusion, w_in, w_out):
     groups = lax.axis_size("grp")
     bands = lax.axis_size("band")
     part_chans, lat_rows, lon_total = state.shape
@@ -62,11 +431,11 @@
         w_out, hidden, (((0,), (0,)), ((), ())), preferred_element_type=jnp.float32
     )
     tendency = tendency.reshape(channels, lat_rows, lon_cols)
-    forward, inverse = fourier_basis(pair_of_slot, NLON)
+    forward, inverse = plain_basis(pair_of_slot, lon_total, legendre.shape[1] - 1)
     total_slots = forward.shape[0]
     flat_rows = state.reshape(part_chans * lat_rows, lon_total)
     spectra = lax.dot_general(
-        forward.reshape(total_slots * 4, NLON),
+        forward.reshape(total_slots * 4, lon_total),
         flat_rows,
         (((1,), (1,)), ((), ())),
         precision=lax.Precision.HIGHEST,
@@ -81,7 +450,7 @@
     )
     device = lax.axis_index("grp") * bands + lax.axis_index("band")
     own_pairs = lax.dynamic_slice_in_dim(pair_of_slot, device * slot_count, slot_count)
-    solved = spectral_step(
+    solved = plain_spectral_step(
         gathered.reshape(slot_count, 4, channels, lat_total), legendre, own_pairs, diffusion
     )
     solved = solved.reshape(1, 1, slot_count, 4, channels, lat_total)
@@ -95,7 +464,7 @@
     coef_flat = returned.reshape(total_slots * 4, part_chans * lat_rows)
     dynamics = lax.dot_general(
         coef_flat,
-        inverse.reshape(total_slots * 4, NLON),
+        inverse.reshape(total_slots * 4, lon_total),
         (((0,), (0,)), ((), ())),
         precision=lax.Precision.HIGHEST,
     )
@@ -104,6 +473,14 @@
         tendency.astype(jnp.bfloat16), "grp", split_axis=0, concat_axis=2, tiled=True
     ).astype(tendency.dtype)
     return dynamics + tendency_rows
+
+
+def shards(state, pair_of_slot, legendre, diffusion, w_in, w_out):
+    chans, lats, lons = state.shape
+    fits = lats % ROWS == 0 and lons % (2 * LANES) == 0
+    fits = fits and cuts_of(lats, lons, lax.axis_size("grp")) is not None
+    fits = fits and folds_of(chans * lats, 4 * legendre.shape[0]) is not None
+    return (fast if fits else plain)(state, pair_of_slot, legendre, diffusion, w_in, w_out)
 
 
 def solution(mesh):

time: 813 us -> 240 us (0.30); the launches traced: 802 us -> 240 us
  local copies, waits for them, and re-layouts: 342 us -> 9.87 us
  waiting for transfers between devices: 241 us -> 87.3 us
  matrix products: 124 us -> 0 us
  Pallas kernels: 0 us -> 70.4 us
  other arithmetic: 64.4 us -> 6.91 us
  blocking collectives: 0 us -> 49.4 us
  starting transfers between devices: 30 us -> 15.8 us
    unnamed x32 -> x12, local copies, waits for them, and re-layouts: 169 us -> 9.29 us
    all_to_all x6 -> x3, waiting for transfers between devices: 241 us -> 87.3 us  [the longest x1 31.8 us: fast(): columns = lax.all_to_all(cut, 'grp', 0, 0, tiled=True)]
    dot_general x5 -> x0, matrix products: 124 us -> none  [the longest x1 46.9 us: shards(): lax.dot_general(forward.reshape(total_slots * 4, NLON), flat_rows, (((1,)...]
    all_to_all x8 -> x0, local copies, waits for them, and re-layouts: 110 us -> none  [the longest x3 44 us: shards(): lax.all_to_all(lax.all_to_all(solved, 'grp', split_axis=4, concat_axis=0,...]
    pallas_call x0 -> x5, Pallas kernels: none -> 70.4 us  [the longest x1 22.6 us: spectral_step(): pl.pallas_call(functools.partial(spectral_kernel, geometry, points), grid...]
    all_to_all x0 -> x1, blocking collectives: none -> 49.4 us  [fast(): back = lax.all_to_all(solved, ('grp', 'band'), 0, 0, tiled=True)]
    all_to_all x1 -> x0, other arithmetic: 33.5 us -> none  [shards(): lax.all_to_all(lax.all_to_all(solved, 'grp', split_axis=4, concat_axis=0,...]
    convert_element_type x5 -> x0, local copies, waits for them, and re-layouts: 28.8 us -> none  [the longest x2 13.4 us: shards(): tendency.astype(jnp.bfloat16)]
  transfers between devices with their start and end apart: 6 -> 3, of which waited for: 5 -> 3; matrix products, arithmetic and copies ran while one was open for 30% -> 6% of each run, Pallas kernels for 0% -> 23%
where the time goes in v1:
time: 240 us
  waiting for transfers between devices  87.3 us (36%)
  Pallas kernels  70.4 us (29%)
  blocking collectives  49.4 us (21%)
  starting transfers between devices  15.8 us (7%)
  local copies, waits for them, and re-layouts  9.87 us (4%)
  other arithmetic  6.91 us (3%)
    all_to_all x1, blocking collectives, fast(): back = lax.all_to_all(solved, ('grp', 'band'), 0, 0, tiled=True)  49.4 us
    all_to_all x1, waiting for transfers between devices, fast(): columns = lax.all_to_all(cut, 'grp', 0, 0, tiled=True)  31.8 us
    all_to_all x1, waiting for transfers between devices, fast(): got = lax.all_to_all(spectra, ('grp', 'band'), 0, 0, tiled=True)  29.4 us
    all_to_all x1, waiting for transfers between devices, fast(): tendency = lax.all_to_all(tendency, 'grp', 0, 0, tiled=True)  26.1 us
    pallas_call x1, Pallas kernels, spectral_step(): pl.pallas_call(functools.partial(spectral_kernel, geometry, points), grid...  22.6 us
    pallas_call x1, Pallas kernels, forward_transform(): pl.pallas_call(functools.partial(forward_kernel, owners, width, folds), g...  17 us
    pallas_call x1, Pallas kernels, physics(): pl.pallas_call(functools.partial(physics_kernel, chans, rows), grid=(tile...  16.3 us
    pallas_call x1, Pallas kernels, inverse_transform(): pl.pallas_call(functools.partial(inverse_kernel, geometry), grid=(lons //...  11.3 us
  transfers between devices with their start and end apart: 3, of which 3 were waited for; matrix products, arithmetic and copies ran while one was open for 6% of the time, Pallas kernels for 23%

profile of v1, /device:TPU:0, one launch (start us, length us, event | category | flops | bytes accessed | tf_op | source)
XLA Modules:
  0.0 239.8 jit_solution(11730293767700502461)
XLA Ops:
  0.0 0.0 copy-start
  0.0 2.4 copy-done
  2.4 3.3 %cut_columns.1 = bf16[8,10,5,24,128]{4,3,2,1,0:T(8,128)(2,1)} custom-call(f32[10,96,1280]{2,1,0:T(8,128)S(1)} %copy-done), custom_call_target="tpu_custom_call" | custom-call | bytes 7372800 | tf_op jit(solution)/shard_map/cut_columns/pallas_call | solution.py:45
  5.7 0.0 copy-start.3
  5.7 7.4 %all-to-all-start = ((bf16[8,10,5,24,128]{4,3,2,1,0:T(8,128)(2,1)}), bf16[8,10,5,24,128]{4,3,2,1,0:T(8,128)(2,1)S(1)}, u32[]{:S(2)}, u32[]{:S(2)}) async-start(bf16[8,10,5,24,128]{4,3,2,1,0:T(8,128)(2,1)} %cut_columns.1), calls=%async_computation | async-start | bytes 4915200 | tf_op jit(solution)/shard_map/all_to_all | solution.py:363
  13.1 0.0 copy-done.3
  13.2 0.1 copy.16
  13.3 0.1 mul.61
  13.5 3.3 %fusion.10 = (f32[1024,128]{1,0:T(8,128)}, f32[1024,128]{1,0:T(8,128)}) fusion(s32[1024]{0:T(1024)S(1)} %mul.61), kind=kLoop, calls=%fused_computation.16 | loop fusion | flops 1179648 | bytes 1052672 | tf_op jit(solution)/shard_map/sin | solution.py:73
  16.8 3.5 %negate_select_fusion = (f32[1024,10]{1,0:T(8,128)}, f32[1024,10]{1,0:T(8,128)}) fusion(s32[10]{0:T(128)S(1)} %iota_multiply_fusion, s32[1024]{0:T(1024)S(1)} %mul.61, pred[1024]{0:T(1024)(128)(4,1)S(1)} %fusion.14), kind=kLoop, calls=%fused_computation.6 | loop fusion | flops 133120 | bytes 87080 | tf_op jit(solution)/shard_map/jit(_where)/select_n | solution.py:72
  20.3 17.0 %forward_transform.1 = (bf16[32,16,1920]{2,1,0:T(8,128)(2,1)}, bf16[1024,1280]{1,0:T(8,128)(2,1)}, bf16[1024,1280]{1,0:T(8,128)(2,1)}) custom-call(f32[960,1280]{1,0:T(8,128)} %bitcast.7, f32[1024,128]{1,0:T(8,128)} %get-tuple-element.30.cos_ref, f32[1024,128]{1,0:T(8,128)} %get-tuple-element.29.sin_ref, f32[1024,10]{1,0:T(8,128)} %get-tuple-element.28.by_cos_ref, ...), custom_call_target="tpu_custom_call" | custom-call | flops 7549747200 | bytes 12124160 | tf_op jit(solution)/shard_map/forward_transform/pallas_call | solution.py:104
  37.3 0.0 copy-start.2
  37.3 0.0 copy-start.1
  37.3 31.8 %all-to-all-done.columns_ref = bf16[8,10,5,24,128]{4,3,2,1,0:T(8,128)(2,1)S(1)} async-done(((bf16[8,10,5,24,128]{4,3,2,1,0:T(8,128)(2,1)}), bf16[8,10,5,24,128]{4,3,2,1,0:T(8,128)(2,1)S(1)}, u32[]{:S(2)}, u32[]{:S(2)}) %all-to-all-start) | async-done | bytes 2457632 | tf_op jit(solution)/shard_map/all_to_all | solution.py:363
  69.1 3.8 %all-to-all-start.1 = ((bf16[32,16,1920]{2,1,0:T(8,128)(2,1)}), bf16[32,16,1920]{2,1,0:T(8,128)(2,1)}, u32[]{:S(2)}, u32[]{:S(2)}) async-start(bf16[32,16,1920]{2,1,0:T(8,128)(2,1)} %get-tuple-element.19), calls=%async_computation.1 | async-start | bytes 3932160 | tf_op jit(solution)/shard_map/all_to_all | solution.py:368
  72.9 0.0 copy-done.2
  72.9 0.2 copy.17
  73.1 0.0 copy-done.1
  73.1 16.3 %physics.1 = bf16[8,10,5,24,128]{4,3,2,1,0:T(8,128)(2,1)} custom-call(bf16[8,10,5,24,128]{4,3,2,1,0:T(8,128)(2,1)S(1)} %all-to-all-done.columns_ref, bf16[1024,80]{1,0:T(8,128)(2,1)S(1)} %multiply_bitcast_fusion.w_in_ref, bf16[80,1024]{1,0:T(8,128)(2,1)S(1)} %bitcast.8), custom_call_target="tpu_custom_call" | custom-call | flops 5033164800 | bytes 4915200 | tf_op jit(solution)/shard_map/physics/pallas_call | solution.py:149
  89.4 0.0 copy-start.4
  89.4 29.4 %all-to-all-done.1.got_ref = bf16[32,16,1920]{2,1,0:T(8,128)(2,1)} async-done(((bf16[32,16,1920]{2,1,0:T(8,128)(2,1)}), bf16[32,16,1920]{2,1,0:T(8,128)(2,1)}, u32[]{:S(2)}, u32[]{:S(2)}) %all-to-all-start.1) | async-done | bytes 1966112 | tf_op jit(solution)/shard_map/all_to_all | solution.py:368
  118.8 4.6 %all-to-all-start.2 = ((bf16[8,10,5,24,128]{4,3,2,1,0:T(8,128)(2,1)}), bf16[8,10,5,24,128]{4,3,2,1,0:T(8,128)(2,1)}, u32[]{:S(2)}, u32[]{:S(2)}) async-start(bf16[8,10,5,24,128]{4,3,2,1,0:T(8,128)(2,1)} %physics.1), calls=%async_computation.2 | async-start | bytes 4915200 | tf_op jit(solution)/shard_map/all_to_all | solution.py:371
  123.4 0.0 copy-done.4
  123.4 0.1 reshape.26
  123.5 0.1 copy.19
  123.6 0.1 reshape.28.diffusion_ref
  123.6 0.1 dynamic_slice.3.pairs_ref
  123.7 6.7 %copy.20.legendre_ref = f32[8,513,384]{2,1,0:T(8,128)} copy(f32[8,513,384]{2,0,1:T(8,128)} %param.8) | data formatting | bytes 12607488 | tf_op args[2]
  130.4 22.6 %spectral_step.1 = bf16[32,16,1920]{2,1,0:T(8,128)(2,1)S(1)} custom-call(s32[8]{0:T(128)S(1)} %dynamic_slice.3.pairs_ref, bf16[32,16,1920]{2,1,0:T(8,128)(2,1)} %all-to-all-done.1.got_ref, f32[8,513,384]{2,1,0:T(8,128)} %copy.20.legendre_ref, f32[80,1]{1,0:T(8,128)S(1)} %reshape.28.diffusion_ref), custom_call_target="tpu_custom_call" | custom-call | flops 5042995200 | bytes 6303744 | tf_op jit(solution)/shard_map/spectral_step/pallas_call | solution.py:256
  153.0 26.1 %all-to-all-done.2.tendency_ref = bf16[8,10,5,24,128]{4,3,2,1,0:T(8,128)(2,1)} async-done(((bf16[8,10,5,24,128]{4,3,2,1,0:T(8,128)(2,1)}), bf16[8,10,5,24,128]{4,3,2,1,0:T(8,128)(2,1)}, u32[]{:S(2)}, u32[]{:S(2)}) %all-to-all-start.2) | async-done | bytes 2457632 | tf_op jit(solution)/shard_map/all_to_all | solution.py:371
  179.1 49.4 %all_to_all.20.back_ref = bf16[32,16,1920]{2,1,0:T(8,128)(2,1)} all-to-all(bf16[32,16,1920]{2,1,0:T(8,128)(2,1)S(1)} %spectral_step.1), channel_id=1, replica_groups=mesh['grp'=8,'band'=4] {'grp','band'}, dimensions={0} | all-to-all | bytes 3932160 | tf_op jit(solution)/shard_map/all_to_all | solution.py:376
  228.5 11.3 %inverse_transform.1 = f32[10,96,1280]{2,1,0:T(8,128)} custom-call(bf16[32,16,1920]{2,1,0:T(8,128)(2,1)} %all_to_all.20.back_ref, bf16[1024,1280]{1,0:T(8,128)(2,1)} %get-tuple-element.24.high_ref, bf16[1024,1280]{1,0:T(8,128)(2,1)} %get-tuple-element.25.low_ref, bf16[8,10,5,24,128]{4,3,2,1,0:T(8,128)(2,1)} %all-to-all-done.2.tendency_ref), custom_call_target="tpu_custom_call" | custom-call | flops 5033164800 | bytes 12615680 | tf_op jit(solution)/shard_map/inverse_transform/pallas_call | solution.py:319
  (5 shorter events, 0.1 us)
Async XLA Ops:
  0.0 2.4 copy-start
  5.7 7.4 %copy-start.3 = (s32[256]{0:T(256)S(1)}, s32[256]{0:T(256)}, u32[]{:S(2)}) copy-start(s32[256]{0:T(256)} %param.7) | copy-start | bytes 3076
  5.7 63.4 %all-to-all-start = ((bf16[8,10,5,24,128]{4,3,2,1,0:T(8,128)(2,1)}), bf16[8,10,5,24,128]{4,3,2,1,0:T(8,128)(2,1)S(1)}, u32[]{:S(2)}, u32[]{:S(2)}) async-start(bf16[8,10,5,24,128]{4,3,2,1,0:T(8,128)(2,1)} %cut_columns.1), calls=%async_computation | async-start | bytes 4915200 | tf_op jit(solution)/shard_map/all_to_all | solution.py:363
  37.3 35.6 %copy-start.2 = (bf16[80,1024]{1,0:T(8,128)(2,1)S(1)}, bf16[80,1024]{1,0:T(8,128)(2,1)}, u32[]{:S(2)}) copy-start(bf16[80,1024]{1,0:T(8,128)(2,1)} %param.10) | copy-start | bytes 491524
  37.3 35.8 %copy-start.1 = (bf16[1024,80]{0,1:T(8,128)(2,1)S(1)}, bf16[1024,80]{0,1:T(8,128)(2,1)}, u32[]{:S(2)}) copy-start(bf16[1024,80]{0,1:T(8,128)(2,1)} %param.11) | copy-start | bytes 491524
  69.1 49.7 %all-to-all-start.1 = ((bf16[32,16,1920]{2,1,0:T(8,128)(2,1)}), bf16[32,16,1920]{2,1,0:T(8,128)(2,1)}, u32[]{:S(2)}, u32[]{:S(2)}) async-start(bf16[32,16,1920]{2,1,0:T(8,128)(2,1)} %get-tuple-element.19), calls=%async_computation.1 | async-start | bytes 3932160 | tf_op jit(solution)/shard_map/all_to_all | solution.py:368
  89.4 34.0 %copy-start.4 = (f32[80]{0:T(128)S(1)}, f32[80]{0:T(128)}, u32[]{:S(2)}) copy-start(f32[80]{0:T(128)} %param.9) | copy-start | bytes 964
  118.8 60.3 %all-to-all-start.2 = ((bf16[8,10,5,24,128]{4,3,2,1,0:T(8,128)(2,1)}), bf16[8,10,5,24,128]{4,3,2,1,0:T(8,128)(2,1)}, u32[]{:S(2)}, u32[]{:S(2)}) async-start(bf16[8,10,5,24,128]{4,3,2,1,0:T(8,128)(2,1)} %physics.1), calls=%async_computation.2 | async-start | bytes 4915200 | tf_op jit(solution)/shard_map/all_to_all | solution.py:371

commit v2 on v1

--- a/solution.py
+++ b/solution.py
@@ -8,6 +8,7 @@
 from jax.experimental.pallas import tpu as pltpu
 from jax.sharding import PartitionSpec as P
 
+
 LANES = 128
 ROWS = 8
 F32 = jnp.float32
@@ -33,27 +34,47 @@
     return pltpu.CompilerParams(dimension_semantics=("arbitrary",), vmem_limit_bytes=mib << 20)
 
 
-def cut_kernel(tiles, state_ref, out_ref):
-    for tile in range(tiles):
-        out_ref[0, :, tile] = state_ref[:, :, tile * LANES : (tile + 1) * LANES].astype(BF16)
-
-
-def cut_columns(state, lat_cuts, lon_cuts):
+def cut_kernel(mine_ref, state_ref, *out_refs):
+    tiles = out_refs[0].shape[1]
+    for offset, out_ref in enumerate(out_refs):
+
+        @pl.when(pl.program_id(0) == offset)
+        def _():
+            for tile in range(tiles):
+                out_ref[:, tile] = state_ref[:, :, tile * LANES : (tile + 1) * LANES].astype(BF16)
+
+
+def cut_columns(state, mine, lat_cuts, lon_cuts):
     chans, lats, lons = state.shape
     rows, tiles = lats // lat_cuts, lons // lon_cuts // LANES
     groups = lat_cuts * lon_cuts
+    block = (chans, tiles, rows, LANES)
+
+    def source(offset, mine):
+        group = offset ^ mine[0]
+        return (0, group // lon_cuts, group % lon_cuts)
+
     return pl.pallas_call(
-        functools.partial(cut_kernel, tiles),
-        grid=(groups,),
-        in_specs=[
-            pl.BlockSpec((chans, rows, tiles * LANES), lambda g: (0, g // lon_cuts, g % lon_cuts))
-        ],
-        out_specs=pl.BlockSpec((1, chans, tiles, rows, LANES), lambda g: (g, 0, 0, 0, 0)),
-        out_shape=jax.ShapeDtypeStruct((groups, chans, tiles, rows, LANES), BF16),
-        compiler_params=params(32),
+        cut_kernel,
+        grid_spec=pltpu.PrefetchScalarGridSpec(
+            num_scalar_prefetch=1,
+            grid=(groups,),
+            in_specs=[pl.BlockSpec((chans, rows, tiles * LANES), source)],
+            out_specs=[pl.BlockSpec(block, lambda offset, mine: (0, 0, 0, 0))] * groups,
+        ),
+        out_shape=[jax.ShapeDtypeStruct(block, BF16)] * groups,
+        compiler_params=params(60),
         cost_estimate=cost(0, state.size * 6),
         name="cut_columns",
-    )(state)
+    )(mine, state)
+
+
+def exchange(blocks):
+    groups = len(blocks)
+    got = [blocks[0]] + [None] * (groups - 1)
+    for offset in range(groups - 1, 0, -1):
+        got[offset] = lax.ppermute(blocks[offset], "grp", [(g, g ^ offset) for g in range(groups)])
+    return got
 
 
 def basis_tables(pair_index, points, waves):
@@ -128,39 +149,77 @@
     )(flat, *tables)
 
 
-def physics_kernel(chans, rows, columns_ref, w_in_ref, w_out_ref, out_ref, spread, found):
-    spread[...] = columns_ref[...].astype(F32).reshape(chans * rows, LANES)
+def physics_kernel(groups, mine_ref, *refs):
+    columns, (w_in_ref, w_out_ref) = refs[:groups], refs[groups : groups + 2]
+    outs, (spread, found) = refs[groups + 2 : 2 * groups + 2], refs[2 * groups + 2 :]
+    per_group, _, rows, _ = columns[0].shape
+    chans = groups * per_group
+    span = per_group * rows
+
+    def part(offset):
+        return pl.ds(pl.multiple_of((mine_ref[0] ^ offset) * span, ROWS), span)
+
+    for offset in range(groups):
+        spread[part(offset), :] = columns[offset][:, 0].astype(F32).reshape(span, LANES)
     for group in range(rows // ROWS):
         at = [pl.ds(group * ROWS + row, chans, stride=rows) for row in range(ROWS)]
-        columns = jnp.concatenate([spread[where, :].astype(BF16) for where in at], axis=1)
-        half = mm(w_in_ref[...], columns)
+        block = jnp.concatenate([spread[where, :].astype(BF16) for where in at], axis=1)
+        half = mm(w_in_ref[...], block)
         hidden = (half + half * jnp.tanh(half)).astype(BF16)
         tendency = mm(w_out_ref[...], hidden)
         for row in range(ROWS):
             found[at[row], :] = tendency[:, row * LANES : (row + 1) * LANES]
-    out_ref[...] = found[...].astype(BF16).reshape(out_ref.shape)
-
-
-def physics(columns, w_in, w_out):
-    groups, per_group, tiles, rows, _ = columns.shape
+    for offset in range(groups):
+        outs[offset][:, 0] = found[part(offset), :].astype(BF16).reshape(per_group, rows, LANES)
+
+
+def physics(columns, mine, w_in, w_out):
+    groups = len(columns)
+    per_group, tiles, rows, _ = columns[0].shape
     chans, hidden = w_in.shape
-    spec = pl.BlockSpec((groups, per_group, 1, rows, LANES), lambda i: (0, 0, i, 0, 0))
+    spec = pl.BlockSpec((per_group, 1, rows, LANES), lambda i, mine: (0, i, 0, 0))
     count = tiles * rows * LANES
     return pl.pallas_call(
-        functools.partial(physics_kernel, chans, rows),
-        grid=(tiles,),
-        in_specs=[
-            spec,
-            pl.BlockSpec((hidden, chans), lambda i: (0, 0)),
-            pl.BlockSpec((chans, hidden), lambda i: (0, 0)),
-        ],
-        out_specs=spec,
-        out_shape=jax.ShapeDtypeStruct(columns.shape, BF16),
-        scratch_shapes=[pltpu.VMEM((chans * rows, LANES), F32), pltpu.VMEM((chans * rows, LANES), F32)],
+        functools.partial(physics_kernel, groups),
+        grid_spec=pltpu.PrefetchScalarGridSpec(
+            num_scalar_prefetch=1,
+            grid=(tiles,),
+            in_specs=[spec] * groups
+            + [
+                pl.BlockSpec((hidden, chans), lambda i, mine: (0, 0)),
+                pl.BlockSpec((chans, hidden), lambda i, mine: (0, 0)),
+            ],
+            out_specs=[spec] * groups,
+            scratch_shapes=[pltpu.VMEM((chans * rows, LANES), F32), pltpu.VMEM((chans * rows, LANES), F32)],
+        ),
+        out_shape=[jax.ShapeDtypeStruct(columns[0].shape, BF16)] * groups,
         compiler_params=params(48),
         cost_estimate=cost(4 * count * chans * hidden, count * chans * 4, count * hidden),
         name="physics",
-    )(columns, w_in.T * jnp.asarray(0.5, BF16), w_out.T)
+    )(mine, *columns, w_in.T * jnp.asarray(0.5, BF16), w_out.T)
+
+
+def gather_kernel(mine_ref, *refs):
+    for offset, part in enumerate(refs[:-1]):
+        refs[-1][mine_ref[0] ^ offset] = part[...]
+
+
+def gather_tendency(parts, mine):
+    groups = len(parts)
+    shape = parts[0].shape
+    return pl.pallas_call(
+        gather_kernel,
+        grid_spec=pltpu.PrefetchScalarGridSpec(
+            num_scalar_prefetch=1,
+            grid=(1,),
+            in_specs=[pl.BlockSpec(shape, lambda i, mine: (0, 0, 0, 0))] * groups,
+            out_specs=pl.BlockSpec((groups,) + shape, lambda i, mine: (0, 0, 0, 0, 0)),
+        ),
+        out_shape=jax.ShapeDtypeStruct((groups,) + shape, BF16),
+        compiler_params=params(48),
+        cost_estimate=cost(0, 4 * groups * parts[0].size),
+        name="gather_tendency",
+    )(mine, *parts)
 
 
 def spectral_kernel(geometry, points, pairs_ref, got_ref, legendre_ref, diffusion_ref, out_ref,
@@ -358,22 +417,23 @@
     waves = degrees - 1
     lat_cuts, lon_cuts = cuts_of(lats, lons, groups)
     folds = folds_of(chans * lats, 4 * slots)
-    cut = cut_columns(state, lat_cuts, lon_cuts)
-    cut, pairs = lax.optimization_barrier((cut, pair_of_slot))
-    columns = lax.all_to_all(cut, "grp", 0, 0, tiled=True)
+    mine = lax.axis_index("grp")
+    device = mine * bands + lax.axis_index("band")
+    mine = mine.reshape(1)
+    cut = cut_columns(state, mine, lat_cuts, lon_cuts)
+    *cut, pairs = lax.optimization_barrier((*cut, pair_of_slot))
+    columns = exchange(cut)
     tables = basis_tables(pairs, lons, waves)
     step_rows = min(8, devices) * 4 * slots
     spectra, high, low = forward_transform(state.reshape(chans * lats, lons), tables, devices, folds, step_rows)
-    columns, spectra = lax.optimization_barrier((columns, spectra))
     got = lax.all_to_all(spectra, ("grp", "band"), 0, 0, tiled=True)
-    tendency = physics(columns, w_in, w_out)
-    got, tendency = lax.optimization_barrier((got, tendency))
-    tendency = lax.all_to_all(tendency, "grp", 0, 0, tiled=True)
-    device = lax.axis_index("grp") * bands + lax.axis_index("band")
+    tendency = physics(columns, mine, w_in, w_out)
+    *tendency, pairs = lax.optimization_barrier((*tendency, pairs))
+    tendency = exchange(tendency)
     own_pairs = lax.dynamic_slice_in_dim(pairs, device * slots, slots)
     solved = spectral_step(got, legendre, own_pairs, diffusion, groups, bands, folds, lons)
-    tendency, solved = lax.optimization_barrier((tendency, solved))
     back = lax.all_to_all(solved, ("grp", "band"), 0, 0, tiled=True)
+    tendency = gather_tendency(tendency, mine)
     return inverse_transform(back, high, low, tendency, state.shape, lat_cuts, lon_cuts, 2 * LANES)
 
 
@@ -477,10 +537,13 @@
 
 def shards(state, pair_of_slot, legendre, diffusion, w_in, w_out):
     chans, lats, lons = state.shape
-    fits = lats % ROWS == 0 and lons % (2 * LANES) == 0
-    fits = fits and cuts_of(lats, lons, lax.axis_size("grp")) is not None
+    groups = lax.axis_size("grp")
+    fits = groups & (groups - 1) == 0 and lats % ROWS == 0 and lons % (2 * LANES) == 0
+    fits = fits and cuts_of(lats, lons, groups) is not None
     fits = fits and folds_of(chans * lats, 4 * legendre.shape[0]) is not None
-    return (fast if fits else plain)(state, pair_of_slot, legendre, diffusion, w_in, w_out)
+    if not fits:
+        return plain(state, pair_of_slot, legendre, diffusion, w_in, w_out)
+    return fast(state, pair_of_slot, legendre, diffusion, w_in, w_out)
 
 
 def solution(mesh):

time: 240 us -> 298 us (1.24)
  the two profiles are of different devices: /device:TPU:0 before, /device:TPU:12 now
where the time goes in v2:
time: 298 us; the launch traced here: 297 us
  waiting for transfers between devices  159 us (53%)
  Pallas kernels  73.8 us (25%)
  starting transfers between devices  37.8 us (13%)
  local copies, waits for them, and re-layouts  18.6 us (6%)
  other arithmetic  7.86 us (3%)
    ppermute x14, waiting for transfers between devices, exchange(): lax.ppermute(blocks[offset], 'grp', [(g, g ^ offset) for g in range(group...  159 us
    ppermute x14, starting transfers between devices, exchange(): lax.ppermute(blocks[offset], 'grp', [(g, g ^ offset) for g in range(group...  28.2 us
    pallas_call x1, Pallas kernels, spectral_step(): pl.pallas_call(functools.partial(spectral_kernel, geometry, points), grid...  21.9 us
    unnamed x48, local copies, waits for them, and re-layouts  18 us
    pallas_call x1, Pallas kernels, physics(): pl.pallas_call(functools.partial(physics_kernel, groups), grid_spec=pltpu...  17 us
    pallas_call x1, Pallas kernels, forward_transform(): pl.pallas_call(functools.partial(forward_kernel, owners, width, folds), g...  17 us
    pallas_call x1, Pallas kernels, inverse_transform(): pl.pallas_call(functools.partial(inverse_kernel, geometry), grid=(lons //...  11.3 us
    pallas_call x1, Pallas kernels, cut_columns(): pl.pallas_call(cut_kernel, grid_spec=pltpu.PrefetchScalarGridSpec(num_sca...  6.52 us
  transfers between devices with their start and end apart: 16, of which 13 were waited for; matrix products, arithmetic and copies ran while one was open for 3% of the time, Pallas kernels for 6%

profile of v2, /device:TPU:12, one launch (start us, length us, event | category | flops | bytes accessed | tf_op | source)
XLA Modules:
  0.0 297.1 jit_solution(6732441340399304399)
XLA Ops:
  0.0 6.5 %cut_columns.1 = (bf16[10,5,24,128]{3,2,1,0:T(8,128)(2,1)}, bf16[10,5,24,128]{3,2,1,0:T(8,128)(2,1)}, bf16[10,5,24,128]{3,2,1,0:T(8,128)(2,1)}, bf16[10,5,24,128...) custom-call(s32[1]{0:T(128)} %bitcast.mine_ref, ...), custom_call_target="tpu_custom_call" | custom-call | bytes 7372800 | tf_op jit(solution)/shard_map/cut_columns/pallas_call | solution.py:57
  6.5 0.0 copy-done.21
  6.6 0.1 copy.18
  6.7 0.1 mul.66
  6.8 3.3 %fusion.10 = (f32[1024,128]{1,0:T(8,128)}, f32[1024,128]{1,0:T(8,128)}) fusion(s32[1024]{0:T(1024)S(1)} %mul.66), kind=kLoop, calls=%fused_computation.16 | loop fusion | flops 1179648 | bytes 1052672 | tf_op jit(solution)/shard_map/sin | solution.py:94
  10.1 3.6 %negate_select_fusion = (f32[1024,10]{1,0:T(8,128)}, f32[1024,10]{1,0:T(8,128)}) fusion(s32[10]{0:T(128)S(1)} %iota_multiply_fusion, s32[1024]{0:T(1024)S(1)} %mul.66, pred[1024]{0:T(1024)(128)(4,1)S(1)} %fusion.14), kind=kLoop, calls=%fused_computation.6 | loop fusion | flops 133120 | bytes 87080 | tf_op jit(solution)/shard_map/jit(_where)/select_n | solution.py:93
  13.7 17.0 %forward_transform.1 = (bf16[32,16,1920]{2,1,0:T(8,128)(2,1)}, bf16[1024,1280]{1,0:T(8,128)(2,1)}, bf16[1024,1280]{1,0:T(8,128)(2,1)}) custom-call(f32[960,1280]{1,0:T(8,128)} %bitcast.9, f32[1024,128]{1,0:T(8,128)} %get-tuple-element.82.cos_ref, f32[1024,128]{1,0:T(8,128)} %get-tuple-element.81.sin_ref, f32[1024,10]{1,0:T(8,128)} %get-tuple-element.80.by_cos_ref, ...), custom_call_target="tpu_custom_call" | custom-call | flops 7549747200 | bytes 12124160 | tf_op jit(solution)/shard_map/forward_transform/pallas_call | solution.py:125
  30.7 0.0 copy-start.20
  30.7 6.0 %all-to-all-start = ((bf16[32,16,1920]{2,1,0:T(8,128)(2,1)}), bf16[32,16,1920]{2,1,0:T(8,128)(2,1)S(1)}, u32[]{:S(2)}, u32[]{:S(2)}) async-start(bf16[32,16,1920]{2,1,0:T(8,128)(2,1)} %get-tuple-element.68), calls=%async_computation | async-start | bytes 3932160 | tf_op jit(solution)/shard_map/all_to_all | solution.py:429
  36.7 1.5 collective-permute-start
  38.2 0.6 collective-permute-start.1
  38.8 1.5 collective-permute-start.2
  40.2 2.4 collective-permute-start.3
  42.7 1.4 collective-permute-start.4
  44.1 15.2 %collective-permute-done.refs_1_ = bf16[10,5,24,128]{3,2,1,0:T(8,128)(2,1)S(1)} collective-permute-done((bf16[10,5,24,128]{3,2,1,0:T(8,128)(2,1)}, bf16[10,5,24,128]{3,2,1,0:T(8,128)(2,1)S(1)}, u32[]{:S(2)}, u32[]{:S(2)}) %collective-permute-start) | collective-permute-done | bytes 307232 | tf_op jit(solution)/shard_map/ppermute | solution.py:76
  59.2 3.2 %collective-permute-start.5 = (bf16[10,5,24,128]{3,2,1,0:T(8,128)(2,1)}, bf16[10,5,24,128]{3,2,1,0:T(8,128)(2,1)}, u32[]{:S(2)}, u32[]{:S(2)}) collective-permute-start(bf16[10,5,24,128]{3,2,1,0:T(8,128)(2,1)} %get-tuple-element.56), channel_id=1, source_target_pairs={{0,24},{4,28},{8,16},{12,20},{16,8},{20,12},{24,0},{28,4},{1,25},{... | collective-permute-start | bytes 921608 | tf_op jit(solution)/shard_map/ppermute | solution.py:76
  62.4 14.8 %collective-permute-done.1.refs_2_ = bf16[10,5,24,128]{3,2,1,0:T(8,128)(2,1)S(1)} collective-permute-done((bf16[10,5,24,128]{3,2,1,0:T(8,128)(2,1)}, bf16[10,5,24,128]{3,2,1,0:T(8,128)(2,1)S(1)}, u32[]{:S(2)}, u32[]{:S(2)}) %collective-permute-start.1) | collective-permute-done | bytes 307232 | tf_op jit(solution)/shard_map/ppermute | solution.py:76
  77.2 3.6 %collective-permute-start.6 = (bf16[10,5,24,128]{3,2,1,0:T(8,128)(2,1)}, bf16[10,5,24,128]{3,2,1,0:T(8,128)(2,1)}, u32[]{:S(2)}, u32[]{:S(2)}) collective-permute-start(bf16[10,5,24,128]{3,2,1,0:T(8,128)(2,1)} %get-tuple-element.57), channel_id=1, source_target_pairs={{0,28},{4,24},{8,20},{12,16},{16,12},{20,8},{24,4},{28,0},{1,29},{... | collective-permute-start | bytes 921608 | tf_op jit(solution)/shard_map/ppermute | solution.py:76
  80.8 0.1 reshape.30
  80.9 0.1 copy.19
  81.0 0.1 reshape.32.diffusion_ref
  81.1 0.9 copy.16
  81.9 6.8 %copy.20.legendre_ref = f32[8,513,384]{2,1,0:T(8,128)} copy(f32[8,513,384]{2,0,1:T(8,128)} %param.8) | data formatting | bytes 12607488 | tf_op args[2]
  88.7 1.0 multiply_bitcast_fusion.refs_8_
  89.7 0.0 collective-permute-done.2.refs_3_
  89.7 23.5 %collective-permute-done.3.refs_4_ = bf16[10,5,24,128]{3,2,1,0:T(8,128)(2,1)S(1)} collective-permute-done((bf16[10,5,24,128]{3,2,1,0:T(8,128)(2,1)}, bf16[10,5,24,128]{3,2,1,0:T(8,128)(2,1)S(1)}, u32[]{:S(2)}, u32[]{:S(2)}) %collective-permute-start.3) | collective-permute-done | bytes 307232 | tf_op jit(solution)/shard_map/ppermute | solution.py:76
  113.2 0.7 copy-done.3
  113.9 5.9 %collective-permute-done.4.refs_5_ = bf16[10,5,24,128]{3,2,1,0:T(8,128)(2,1)} collective-permute-done((bf16[10,5,24,128]{3,2,1,0:T(8,128)(2,1)}, bf16[10,5,24,128]{3,2,1,0:T(8,128)(2,1)}, u32[]{:S(2)}, u32[]{:S(2)}) %collective-permute-start.4) | collective-permute-done | bytes 307232 | tf_op jit(solution)/shard_map/ppermute | solution.py:76
  119.8 8.4 %collective-permute-done.5.refs_6_ = bf16[10,5,24,128]{3,2,1,0:T(8,128)(2,1)} collective-permute-done((bf16[10,5,24,128]{3,2,1,0:T(8,128)(2,1)}, bf16[10,5,24,128]{3,2,1,0:T(8,128)(2,1)}, u32[]{:S(2)}, u32[]{:S(2)}) %collective-permute-start.5) | collective-permute-done | bytes 307232 | tf_op jit(solution)/shard_map/ppermute | solution.py:76
  128.2 6.9 %collective-permute-done.6.refs_7_ = bf16[10,5,24,128]{3,2,1,0:T(8,128)(2,1)} collective-permute-done((bf16[10,5,24,128]{3,2,1,0:T(8,128)(2,1)}, bf16[10,5,24,128]{3,2,1,0:T(8,128)(2,1)}, u32[]{:S(2)}, u32[]{:S(2)}) %collective-permute-start.6) | collective-permute-done | bytes 307232 | tf_op jit(solution)/shard_map/ppermute | solution.py:76
  135.1 1.0 copy-done.4
  136.1 0.9 copy-done.19
  137.0 17.0 %physics.1 = (bf16[10,5,24,128]{3,2,1,0:T(8,128)(2,1)S(1)}, bf16[10,5,24,128]{3,2,1,0:T(8,128)(2,1)S(1)}, bf16[10,5,24,128]{3,2,1,0:T(8,128)(2,1)S(1)}, bf16[10,...) custom-call(s32[1]{0:T(128)} %bitcast.mine_ref, ...), custom_call_target="tpu_custom_call" | custom-call | flops 5033164800 | bytes 4915200 | tf_op jit(solution)/shard_map/physics/pallas_call | solution.py:182
  154.0 0.7 copy-done.5
  154.7 0.7 copy-done.7
  155.4 0.7 copy-done.9
  156.2 0.7 copy-done.11
  156.9 0.7 copy-done.13
  157.6 0.7 copy-done.15
  158.3 0.7 copy-done.17
  159.0 0.1 dynamic_slice.3.pairs_ref
  159.1 0.0 all-to-all-done.got_ref
  159.1 21.9 %spectral_step.1 = bf16[32,16,1920]{2,1,0:T(8,128)(2,1)S(1)} custom-call(s32[8]{0:T(128)S(1)} %dynamic_slice.3.pairs_ref, bf16[32,16,1920]{2,1,0:T(8,128)(2,1)S(1)} %all-to-all-done.got_ref, f32[8,513,384]{2,1,0:T(8,128)} %copy.20.legendre_ref, f32[80,1]{1,0:T(8,128)S(1)} %reshape.32.diffusion_ref), custom_call_target="tpu_custom_call" | custom-call | flops 5042995200 | bytes 6303744 | tf_op jit(solution)/shard_map/spectral_step/pallas_call | solution.py:315
  181.0 0.0 copy-start.1
  181.0 1.3 copy-done.1
  182.3 3.5 %all-to-all-start.1 = ((bf16[32,16,1920]{2,1,0:T(8,128)(2,1)}), bf16[32,16,1920]{2,1,0:T(8,128)(2,1)}, u32[]{:S(2)}, u32[]{:S(2)}) async-start(bf16[32,16,1920]{2,1,0:T(8,128)(2,1)} %copy-done.1), calls=%async_computation.1 | async-start | bytes 3932160 | tf_op jit(solution)/shard_map/all_to_all | solution.py:435
  185.9 1.5 collective-permute-start.7
  187.4 0.6 collective-permute-start.8
  188.0 1.5 collective-permute-start.9
  189.4 2.4 collective-permute-start.10
  191.9 1.4 collective-permute-start.11
  193.3 15.1 %collective-permute-done.7.refs_1_ = bf16[10,5,24,128]{3,2,1,0:T(8,128)(2,1)S(1)} collective-permute-done((bf16[10,5,24,128]{3,2,1,0:T(8,128)(2,1)S(1)}, bf16[10,5,24,128]{3,2,1,0:T(8,128)(2,1)S(1)}, u32[]{:S(2)}, u32[]{:S(2)}) %collective-permute-start.7) | collective-permute-done | bytes 307232 | tf_op jit(solution)/shard_map/ppermute | solution.py:76
  208.4 3.2 %collective-permute-start.12 = (bf16[10,5,24,128]{3,2,1,0:T(8,128)(2,1)S(1)}, bf16[10,5,24,128]{3,2,1,0:T(8,128)(2,1)S(1)}, u32[]{:S(2)}, u32[]{:S(2)}) collective-permute-start(bf16[10,5,24,128]{3,2,1,0:T(8,128)(2,1)S(1)} %copy-done.8), channel_id=1, source_target_pairs={{0,24},{4,28},{8,16},{12,20},{16,8},{20,12},{24,0},{28,4},{1,25},{... | collective-permute-start | bytes 921608 | tf_op jit(solution)/shard_map/ppermute | solution.py:76
  211.5 14.8 %collective-permute-done.8.refs_2_ = bf16[10,5,24,128]{3,2,1,0:T(8,128)(2,1)S(1)} collective-permute-done((bf16[10,5,24,128]{3,2,1,0:T(8,128)(2,1)S(1)}, bf16[10,5,24,128]{3,2,1,0:T(8,128)(2,1)S(1)}, u32[]{:S(2)}, u32[]{:S(2)}) %collective-permute-start.8) | collective-permute-done | bytes 307232 | tf_op jit(solution)/shard_map/ppermute | solution.py:76
  226.4 3.6 %collective-permute-start.13 = (bf16[10,5,24,128]{3,2,1,0:T(8,128)(2,1)S(1)}, bf16[10,5,24,128]{3,2,1,0:T(8,128)(2,1)S(1)}, u32[]{:S(2)}, u32[]{:S(2)}) collective-permute-start(bf16[10,5,24,128]{3,2,1,0:T(8,128)(2,1)S(1)} %copy-done.6), channel_id=1, source_target_pairs={{0,28},{4,24},{8,20},{12,16},{16,12},{20,8},{24,4},{28,0},{1,29},{... | collective-permute-start | bytes 921608 | tf_op jit(solution)/shard_map/ppermute | solution.py:76
  230.0 5.1 %collective-permute-done.9.refs_3_ = bf16[10,5,24,128]{3,2,1,0:T(8,128)(2,1)S(1)} collective-permute-done((bf16[10,5,24,128]{3,2,1,0:T(8,128)(2,1)S(1)}, bf16[10,5,24,128]{3,2,1,0:T(8,128)(2,1)S(1)}, u32[]{:S(2)}, u32[]{:S(2)}) %collective-permute-start.9) | collective-permute-done | bytes 307232 | tf_op jit(solution)/shard_map/ppermute | solution.py:76
  235.0 27.2 %collective-permute-done.10.refs_4_ = bf16[10,5,24,128]{3,2,1,0:T(8,128)(2,1)S(1)} collective-permute-done((bf16[10,5,24,128]{3,2,1,0:T(8,128)(2,1)S(1)}, bf16[10,5,24,128]{3,2,1,0:T(8,128)(2,1)S(1)}, u32[]{:S(2)}, u32[]{:S(2)}) %collective-permute-start.10) | collective-permute-done | bytes 307232 | tf_op jit(solution)/shard_map/ppermute | solution.py:76
  262.2 6.6 %collective-permute-done.11.refs_5_ = bf16[10,5,24,128]{3,2,1,0:T(8,128)(2,1)S(1)} collective-permute-done((bf16[10,5,24,128]{3,2,1,0:T(8,128)(2,1)S(1)}, bf16[10,5,24,128]{3,2,1,0:T(8,128)(2,1)S(1)}, u32[]{:S(2)}, u32[]{:S(2)}) %collective-permute-start.11) | collective-permute-done | bytes 307232 | tf_op jit(solution)/shard_map/ppermute | solution.py:76
  268.8 8.4 %collective-permute-done.12.refs_6_ = bf16[10,5,24,128]{3,2,1,0:T(8,128)(2,1)S(1)} collective-permute-done((bf16[10,5,24,128]{3,2,1,0:T(8,128)(2,1)S(1)}, bf16[10,5,24,128]{3,2,1,0:T(8,128)(2,1)S(1)}, u32[]{:S(2)}, u32[]{:S(2)}) %collective-permute-start.12) | collective-permute-done | bytes 307232 | tf_op jit(solution)/shard_map/ppermute | solution.py:76
  277.2 6.9 %collective-permute-done.13.refs_7_ = bf16[10,5,24,128]{3,2,1,0:T(8,128)(2,1)S(1)} collective-permute-done((bf16[10,5,24,128]{3,2,1,0:T(8,128)(2,1)S(1)}, bf16[10,5,24,128]{3,2,1,0:T(8,128)(2,1)S(1)}, u32[]{:S(2)}, u32[]{:S(2)}) %collective-permute-start.13) | collective-permute-done | bytes 307232 | tf_op jit(solution)/shard_map/ppermute | solution.py:76
  284.2 0.2 gather_tendency.1.tendency_ref
  284.3 1.4 copy-done
  285.8 0.0 all-to-all-done.1.back_ref
  285.8 11.3 %inverse_transform.1 = f32[10,96,1280]{2,1,0:T(8,128)} custom-call(bf16[32,16,1920]{2,1,0:T(8,128)(2,1)} %all-to-all-done.1.back_ref, bf16[1024,1280]{1,0:T(8,128)(2,1)} %get-tuple-element.69.high_ref, bf16[1024,1280]{1,0:T(8,128)(2,1)} %get-tuple-element.70.low_ref, bf16[8,10,5,24,128]{4,3,2,1,0:T(8,128)(2,1)} %copy-done), custom_call_target="tpu_custom_call" | custom-call | flops 5033164800 | bytes 12615680 | tf_op jit(solution)/shard_map/inverse_transform/pallas_call | solution.py:378
  (35 shorter events, 0.1 us)
Async XLA Ops:
  0.0 6.5 %copy-start.21 = (s32[256]{0:T(256)S(1)}, s32[256]{0:T(256)}, u32[]{:S(2)}) copy-start(s32[256]{0:T(256)} %param.7) | copy-start | bytes 3076
  30.7 50.2 %copy-start.22 = (f32[80]{0:T(128)S(1)}, f32[80]{0:T(128)}, u32[]{:S(2)}) copy-start(f32[80]{0:T(128)} %param.9) | copy-start | bytes 964
  30.7 50.4 %copy-start.20 = (bf16[80,1024]{1,0:T(8,128)(2,1)S(1)}, bf16[80,1024]{1,0:T(8,128)(2,1)}, u32[]{:S(2)}) copy-start(bf16[80,1024]{1,0:T(8,128)(2,1)} %param.10) | copy-start | bytes 491524
  30.7 128.4 %all-to-all-start = ((bf16[32,16,1920]{2,1,0:T(8,128)(2,1)}), bf16[32,16,1920]{2,1,0:T(8,128)(2,1)S(1)}, u32[]{:S(2)}, u32[]{:S(2)}) async-start(bf16[32,16,1920]{2,1,0:T(8,128)(2,1)} %get-tuple-element.68), calls=%async_computation | async-start | bytes 3932160 | tf_op jit(solution)/shard_map/all_to_all | solution.py:429
  36.7 22.6 %collective-permute-start = (bf16[10,5,24,128]{3,2,1,0:T(8,128)(2,1)}, bf16[10,5,24,128]{3,2,1,0:T(8,128)(2,1)S(1)}, u32[]{:S(2)}, u32[]{:S(2)}) collective-permute-start(bf16[10,5,24,128]{3,2,1,0:T(8,128)(2,1)} %get-tuple-element.51), channel_id=1, source_target_pairs={{0,4},{4,0},{8,12},{12,8},{16,20},{20,16},{24,28},{28,24},{1,5},{5... | collective-permute-start | bytes 921608 | tf_op jit(solution)/shard_map/ppermute | solution.py:76
  38.2 39.0 %collective-permute-start.1 = (bf16[10,5,24,128]{3,2,1,0:T(8,128)(2,1)}, bf16[10,5,24,128]{3,2,1,0:T(8,128)(2,1)S(1)}, u32[]{:S(2)}, u32[]{:S(2)}) collective-permute-start(bf16[10,5,24,128]{3,2,1,0:T(8,128)(2,1)} %get-tuple-element.52), channel_id=1, source_target_pairs={{0,8},{4,12},{8,0},{12,4},{16,24},{20,28},{24,16},{28,20},{1,9},{5... | collective-permute-start | bytes 921608 | tf_op jit(solution)/shard_map/ppermute | solution.py:76
  38.8 50.9 %collective-permute-start.2 = (bf16[10,5,24,128]{3,2,1,0:T(8,128)(2,1)}, bf16[10,5,24,128]{3,2,1,0:T(8,128)(2,1)S(1)}, u32[]{:S(2)}, u32[]{:S(2)}) collective-permute-start(bf16[10,5,24,128]{3,2,1,0:T(8,128)(2,1)} %get-tuple-element.53), channel_id=1, source_target_pairs={{0,12},{4,8},{8,4},{12,0},{16,28},{20,24},{24,20},{28,16},{1,13},{... | collective-permute-start | bytes 921608 | tf_op jit(solution)/shard_map/ppermute | solution.py:76
  40.2 72.9 %collective-permute-start.3 = (bf16[10,5,24,128]{3,2,1,0:T(8,128)(2,1)}, bf16[10,5,24,128]{3,2,1,0:T(8,128)(2,1)S(1)}, u32[]{:S(2)}, u32[]{:S(2)}) collective-permute-start(bf16[10,5,24,128]{3,2,1,0:T(8,128)(2,1)} %get-tuple-element.54), channel_id=1, source_target_pairs={{0,16},{4,20},{8,24},{12,28},{16,0},{20,4},{24,8},{28,12},{1,17},{... | collective-permute-start | bytes 921608 | tf_op jit(solution)/shard_map/ppermute | solution.py:76
  42.7 77.1 %collective-permute-start.4 = (bf16[10,5,24,128]{3,2,1,0:T(8,128)(2,1)}, bf16[10,5,24,128]{3,2,1,0:T(8,128)(2,1)}, u32[]{:S(2)}, u32[]{:S(2)}) collective-permute-start(bf16[10,5,24,128]{3,2,1,0:T(8,128)(2,1)} %get-tuple-element.55), channel_id=1, source_target_pairs={{0,20},{4,16},{8,28},{12,24},{16,4},{20,0},{24,12},{28,8},{1,21},{... | collective-permute-start | bytes 921608 | tf_op jit(solution)/shard_map/ppermute | solution.py:76
  59.2 69.0 %collective-permute-start.5 = (bf16[10,5,24,128]{3,2,1,0:T(8,128)(2,1)}, bf16[10,5,24,128]{3,2,1,0:T(8,128)(2,1)}, u32[]{:S(2)}, u32[]{:S(2)}) collective-permute-start(bf16[10,5,24,128]{3,2,1,0:T(8,128)(2,1)} %get-tuple-element.56), channel_id=1, source_target_pairs={{0,24},{4,28},{8,16},{12,20},{16,8},{20,12},{24,0},{28,4},{1,25},{... | collective-permute-start | bytes 921608 | tf_op jit(solution)/shard_map/ppermute | solution.py:76
  77.2 57.9 %collective-permute-start.6 = (bf16[10,5,24,128]{3,2,1,0:T(8,128)(2,1)}, bf16[10,5,24,128]{3,2,1,0:T(8,128)(2,1)}, u32[]{:S(2)}, u32[]{:S(2)}) collective-permute-start(bf16[10,5,24,128]{3,2,1,0:T(8,128)(2,1)} %get-tuple-element.57), channel_id=1, source_target_pairs={{0,28},{4,24},{8,20},{12,16},{16,12},{20,8},{24,4},{28,0},{1,29},{... | collective-permute-start | bytes 921608 | tf_op jit(solution)/shard_map/ppermute | solution.py:76
  81.9 53.2 %copy-start.2 = (bf16[10,5,24,128]{3,2,1,0:T(8,128)(2,1)S(1)}, bf16[10,5,24,128]{3,2,1,0:T(8,128)(2,1)}, u32[]{:S(2)}) copy-start(bf16[10,5,24,128]{3,2,1,0:T(8,128)(2,1)} %get-tuple-element.50.refs_0_) | copy-start | bytes 921604
  113.2 0.7 copy-start.3
  135.1 1.0 copy-start.4
  136.1 0.9 copy-start.19
  154.0 0.7 copy-start.5
  154.7 0.7 copy-start.7
  155.4 0.7 copy-start.9
  156.2 0.7 copy-start.11
  156.9 0.7 copy-start.13
  157.6 0.7 copy-start.15
  158.3 0.7 copy-start.17
  181.0 1.3 copy-start.1
  182.3 3.6 %copy-start.18 = (bf16[10,5,24,128]{3,2,1,0:T(8,128)(2,1)S(1)}, bf16[10,5,24,128]{3,2,1,0:T(8,128)(2,1)}, u32[]{:S(2)}) copy-start(bf16[10,5,24,128]{3,2,1,0:T(8,128)(2,1)} %copy-done.17) | copy-start | bytes 921604
  182.3 5.1 %copy-start.16 = (bf16[10,5,24,128]{3,2,1,0:T(8,128)(2,1)S(1)}, bf16[10,5,24,128]{3,2,1,0:T(8,128)(2,1)}, u32[]{:S(2)}) copy-start(bf16[10,5,24,128]{3,2,1,0:T(8,128)(2,1)} %copy-done.15) | copy-start | bytes 921604
  182.3 5.7 %copy-start.14 = (bf16[10,5,24,128]{3,2,1,0:T(8,128)(2,1)S(1)}, bf16[10,5,24,128]{3,2,1,0:T(8,128)(2,1)}, u32[]{:S(2)}) copy-start(bf16[10,5,24,128]{3,2,1,0:T(8,128)(2,1)} %copy-done.13) | copy-start | bytes 921604
  182.3 7.1 %copy-start.12 = (bf16[10,5,24,128]{3,2,1,0:T(8,128)(2,1)S(1)}, bf16[10,5,24,128]{3,2,1,0:T(8,128)(2,1)}, u32[]{:S(2)}) copy-start(bf16[10,5,24,128]{3,2,1,0:T(8,128)(2,1)} %copy-done.11) | copy-start | bytes 921604
  182.3 9.6 %copy-start.10 = (bf16[10,5,24,128]{3,2,1,0:T(8,128)(2,1)S(1)}, bf16[10,5,24,128]{3,2,1,0:T(8,128)(2,1)}, u32[]{:S(2)}) copy-start(bf16[10,5,24,128]{3,2,1,0:T(8,128)(2,1)} %copy-done.9) | copy-start | bytes 921604
  182.3 26.1 %copy-start.8 = (bf16[10,5,24,128]{3,2,1,0:T(8,128)(2,1)S(1)}, bf16[10,5,24,128]{3,2,1,0:T(8,128)(2,1)}, u32[]{:S(2)}) copy-start(bf16[10,5,24,128]{3,2,1,0:T(8,128)(2,1)} %copy-done.7) | copy-start | bytes 921604
  182.3 44.0 %copy-start.6 = (bf16[10,5,24,128]{3,2,1,0:T(8,128)(2,1)S(1)}, bf16[10,5,24,128]{3,2,1,0:T(8,128)(2,1)}, u32[]{:S(2)}) copy-start(bf16[10,5,24,128]{3,2,1,0:T(8,128)(2,1)} %copy-done.5) | copy-start | bytes 921604
  182.3 103.4 %all-to-all-start.1 = ((bf16[32,16,1920]{2,1,0:T(8,128)(2,1)}), bf16[32,16,1920]{2,1,0:T(8,128)(2,1)}, u32[]{:S(2)}, u32[]{:S(2)}) async-start(bf16[32,16,1920]{2,1,0:T(8,128)(2,1)} %copy-done.1), calls=%async_computation.1 | async-start | bytes 3932160 | tf_op jit(solution)/shard_map/all_to_all | solution.py:435
  185.9 22.5 %collective-permute-start.7 = (bf16[10,5,24,128]{3,2,1,0:T(8,128)(2,1)S(1)}, bf16[10,5,24,128]{3,2,1,0:T(8,128)(2,1)S(1)}, u32[]{:S(2)}, u32[]{:S(2)}) collective-permute-start(bf16[10,5,24,128]{3,2,1,0:T(8,128)(2,1)S(1)} %copy-done.18), channel_id=1, source_target_pairs={{0,4},{4,0},{8,12},{12,8},{16,20},{20,16},{24,28},{28,24},{1,5},{5... | collective-permute-start | bytes 921608 | tf_op jit(solution)/shard_map/ppermute | solution.py:76
  187.4 39.0 %collective-permute-start.8 = (bf16[10,5,24,128]{3,2,1,0:T(8,128)(2,1)S(1)}, bf16[10,5,24,128]{3,2,1,0:T(8,128)(2,1)S(1)}, u32[]{:S(2)}, u32[]{:S(2)}) collective-permute-start(bf16[10,5,24,128]{3,2,1,0:T(8,128)(2,1)S(1)} %copy-done.16), channel_id=1, source_target_pairs={{0,8},{4,12},{8,0},{12,4},{16,24},{20,28},{24,16},{28,20},{1,9},{5... | collective-permute-start | bytes 921608 | tf_op jit(solution)/shard_map/ppermute | solution.py:76
  188.0 47.1 %collective-permute-start.9 = (bf16[10,5,24,128]{3,2,1,0:T(8,128)(2,1)S(1)}, bf16[10,5,24,128]{3,2,1,0:T(8,128)(2,1)S(1)}, u32[]{:S(2)}, u32[]{:S(2)}) collective-permute-start(bf16[10,5,24,128]{3,2,1,0:T(8,128)(2,1)S(1)} %copy-done.14), channel_id=1, source_target_pairs={{0,12},{4,8},{8,4},{12,0},{16,28},{20,24},{24,20},{28,16},{1,13},{... | collective-permute-start | bytes 921608 | tf_op jit(solution)/shard_map/ppermute | solution.py:76
  189.4 72.8 %collective-permute-start.10 = (bf16[10,5,24,128]{3,2,1,0:T(8,128)(2,1)S(1)}, bf16[10,5,24,128]{3,2,1,0:T(8,128)(2,1)S(1)}, u32[]{:S(2)}, u32[]{:S(2)}) collective-permute-start(bf16[10,5,24,128]{3,2,1,0:T(8,128)(2,1)S(1)} %copy-done.12), channel_id=1, source_target_pairs={{0,16},{4,20},{8,24},{12,28},{16,0},{20,4},{24,8},{28,12},{1,17},{... | collective-permute-start | bytes 921608 | tf_op jit(solution)/shard_map/ppermute | solution.py:76
  191.9 76.9 %collective-permute-start.11 = (bf16[10,5,24,128]{3,2,1,0:T(8,128)(2,1)S(1)}, bf16[10,5,24,128]{3,2,1,0:T(8,128)(2,1)S(1)}, u32[]{:S(2)}, u32[]{:S(2)}) collective-permute-start(bf16[10,5,24,128]{3,2,1,0:T(8,128)(2,1)S(1)} %copy-done.10), channel_id=1, source_target_pairs={{0,20},{4,16},{8,28},{12,24},{16,4},{20,0},{24,12},{28,8},{1,21},{... | collective-permute-start | bytes 921608 | tf_op jit(solution)/shard_map/ppermute | solution.py:76
  208.4 68.8 %collective-permute-start.12 = (bf16[10,5,24,128]{3,2,1,0:T(8,128)(2,1)S(1)}, bf16[10,5,24,128]{3,2,1,0:T(8,128)(2,1)S(1)}, u32[]{:S(2)}, u32[]{:S(2)}) collective-permute-start(bf16[10,5,24,128]{3,2,1,0:T(8,128)(2,1)S(1)} %copy-done.8), channel_id=1, source_target_pairs={{0,24},{4,28},{8,16},{12,20},{16,8},{20,12},{24,0},{28,4},{1,25},{... | collective-permute-start | bytes 921608 | tf_op jit(solution)/shard_map/ppermute | solution.py:76
  226.4 57.8 %collective-permute-start.13 = (bf16[10,5,24,128]{3,2,1,0:T(8,128)(2,1)S(1)}, bf16[10,5,24,128]{3,2,1,0:T(8,128)(2,1)S(1)}, u32[]{:S(2)}, u32[]{:S(2)}) collective-permute-start(bf16[10,5,24,128]{3,2,1,0:T(8,128)(2,1)S(1)} %copy-done.6), channel_id=1, source_target_pairs={{0,28},{4,24},{8,20},{12,16},{16,12},{20,8},{24,4},{28,0},{1,29},{... | collective-permute-start | bytes 921608 | tf_op jit(solution)/shard_map/ppermute | solution.py:76
  284.3 1.4 copy-start

commit v3 on v2

--- a/solution.py
+++ b/solution.py
@@ -34,14 +34,31 @@
     return pltpu.CompilerParams(dimension_semantics=("arbitrary",), vmem_limit_bytes=mib << 20)
 
 
-def cut_kernel(mine_ref, state_ref, *out_refs):
-    tiles = out_refs[0].shape[1]
-    for offset, out_ref in enumerate(out_refs):
-
-        @pl.when(pl.program_id(0) == offset)
-        def _():
-            for tile in range(tiles):
-                out_ref[:, tile] = state_ref[:, :, tile * LANES : (tile + 1) * LANES].astype(BF16)
+def cut_kernel(lon_cuts, mine_ref, state_ref, *refs):
+    groups = len(refs) - 4
+    out_refs, (wide, narrow, arrived, left) = refs[:groups], refs[groups:]
+    _, tiles, rows, _ = out_refs[0].shape
+    lons = tiles * LANES
+
+    def fetch(offset):
+        group = mine_ref[0] ^ offset
+        lat = pl.multiple_of(group // lon_cuts * rows, ROWS)
+        lon = pl.multiple_of(group % lon_cuts * lons, LANES)
+        block = state_ref.at[:, pl.ds(lat, rows), pl.ds(lon, lons)]
+        return pltpu.make_async_copy(block, wide.at[offset], arrived.at[offset])
+
+    def store(offset):
+        return pltpu.make_async_copy(narrow.at[offset], out_refs[offset], left.at[offset])
+
+    for offset in range(groups):
+        fetch(offset).start()
+    for offset in range(groups):
+        fetch(offset).wait()
+        for tile in range(tiles):
+            narrow[offset, :, tile] = wide[offset, :, :, tile * LANES : (tile + 1) * LANES].astype(BF16)
+        store(offset).start()
+    for offset in range(groups):
+        store(offset).wait()
 
 
 def cut_columns(state, mine, lat_cuts, lon_cuts):
@@ -49,18 +66,19 @@
     rows, tiles = lats // lat_cuts, lons // lon_cuts // LANES
     groups = lat_cuts * lon_cuts
     block = (chans, tiles, rows, LANES)
-
-    def source(offset, mine):
-        group = offset ^ mine[0]
-        return (0, group // lon_cuts, group % lon_cuts)
-
     return pl.pallas_call(
-        cut_kernel,
+        functools.partial(cut_kernel, lon_cuts),
         grid_spec=pltpu.PrefetchScalarGridSpec(
             num_scalar_prefetch=1,
-            grid=(groups,),
-            in_specs=[pl.BlockSpec((chans, rows, tiles * LANES), source)],
-            out_specs=[pl.BlockSpec(block, lambda offset, mine: (0, 0, 0, 0))] * groups,
+            grid=(1,),
+            in_specs=[pl.BlockSpec(memory_space=pl.ANY)],
+            out_specs=[pl.BlockSpec(memory_space=pl.ANY)] * groups,
+            scratch_shapes=[
+                pltpu.VMEM((groups, chans, rows, tiles * LANES), F32),
+                pltpu.VMEM((groups,) + block, BF16),
+                pltpu.SemaphoreType.DMA((groups,)),
+                pltpu.SemaphoreType.DMA((groups,)),
+            ],
         ),
         out_shape=[jax.ShapeDtypeStruct(block, BF16)] * groups,
         compiler_params=params(60),
@@ -135,14 +153,16 @@
         out_specs=[
             pl.BlockSpec((owners, rows, folds * width), lambda i: (i, 0, 0)),
             pl.BlockSpec((step_rows, points), lambda i: (i, 0)),
-            pl.BlockSpec((step_rows, points), lambda i: (i, 0)),
         ],
         out_shape=[
             jax.ShapeDtypeStruct((devices, rows, folds * width), BF16),
             jax.ShapeDtypeStruct((total, points), BF16),
-            jax.ShapeDtypeStruct((total, points), BF16),
         ],
-        scratch_shapes=[pltpu.VMEM((width, points), BF16), pltpu.VMEM((width, points), BF16)],
+        scratch_shapes=[
+            pltpu.VMEM((step_rows, points), BF16),
+            pltpu.VMEM((width, points), BF16),
+            pltpu.VMEM((width, points), BF16),
+        ],
         compiler_params=params(56),
         cost_estimate=cost(6 * total * width * points, width * points * 4 + total * (points * 4 + width * 2)),
         name="forward_transform",
@@ -199,25 +219,30 @@
     )(mine, *columns, w_in.T * jnp.asarray(0.5, BF16), w_out.T)
 
 
-def gather_kernel(mine_ref, *refs):
+def gather_kernel(lon_cuts, mine_ref, *refs):
+    out_ref = refs[-1]
+    tiles = refs[0].shape[1]
     for offset, part in enumerate(refs[:-1]):
-        refs[-1][mine_ref[0] ^ offset] = part[...]
-
-
-def gather_tendency(parts, mine):
-    groups = len(parts)
+        group = mine_ref[0] ^ offset
+        for tile in range(tiles):
+            out_ref[group % lon_cuts * tiles + tile, group // lon_cuts] = part[:, tile]
+
+
+def gather_tendency(parts, mine, lat_cuts, lon_cuts):
     shape = parts[0].shape
+    chans, tiles, rows, _ = shape
+    out = (lon_cuts * tiles, lat_cuts, chans, rows, LANES)
     return pl.pallas_call(
-        gather_kernel,
+        functools.partial(gather_kernel, lon_cuts),
         grid_spec=pltpu.PrefetchScalarGridSpec(
             num_scalar_prefetch=1,
             grid=(1,),
-            in_specs=[pl.BlockSpec(shape, lambda i, mine: (0, 0, 0, 0))] * groups,
-            out_specs=pl.BlockSpec((groups,) + shape, lambda i, mine: (0, 0, 0, 0, 0)),
+            in_specs=[pl.BlockSpec(shape, lambda i, mine: (0, 0, 0, 0))] * len(parts),
+            out_specs=pl.BlockSpec(out, lambda i, mine: (0, 0, 0, 0, 0)),
         ),
-        out_shape=jax.ShapeDtypeStruct((groups,) + shape, BF16),
+        out_shape=jax.ShapeDtypeStruct(out, BF16),
         compiler_params=params(48),
-        cost_estimate=cost(0, 4 * groups * parts[0].size),
+        cost_estimate=cost(0, 4 * len(parts) * parts[0].size),
         name="gather_tendency",
     )(mine, *parts)
 
@@ -337,10 +362,10 @@
     )(own_pairs, got, legendre, by_row)
 
 
-def inverse_kernel(geometry, back_ref, high_ref, low_ref, tendency_ref, out_ref, rows_ref, turned):
-    devices, fold_rows, folds, width, lat_cuts, lon_cuts, tiles = geometry
+def inverse_kernel(geometry, back_ref, basis_ref, tendency_ref, out_ref, rows_ref, turned):
+    devices, fold_rows, folds, width = geometry
     chans, lats, step_lons = out_ref.shape
-    rows = lats // lat_cuts
+    _, lat_cuts, _, rows, _ = tendency_ref.shape
 
     @pl.when(pl.program_id(0) == 0)
     def _():
@@ -354,43 +379,38 @@
         turned[...] = rows_ref[...].T
 
     waves = turned[0:width, :]
-    found = mm(waves, low_ref[...]) + mm(waves, high_ref[...])
+    found = mm(waves, basis_ref[...])
     found = found.reshape(chans, lats, step_lons)
     for part in range(step_lons // LANES):
-        tile = pl.program_id(0) * (step_lons // LANES) + part
         for cut in range(lat_cuts):
             at = slice(cut * rows, (cut + 1) * rows)
             lanes = slice(part * LANES, (part + 1) * LANES)
-            out_ref[:, at, lanes] = found[:, at, lanes] + tendency_ref[
-                cut * lon_cuts + tile // tiles, :, tile % tiles
-            ].astype(F32)
-
-
-def inverse_transform(back, high, low, tendency, shape, lat_cuts, lon_cuts, step_lons):
+            out_ref[:, at, lanes] = found[:, at, lanes] + tendency_ref[part, cut].astype(F32)
+
+
+def inverse_transform(back, basis, tendency, shape, step_lons):
     chans, lats, lons = shape
     devices, fold_rows, wide = back.shape
     width = chans * lats
     folds = wide // width
-    total = high.shape[0]
-    tiles = tendency.shape[2]
+    total = basis.shape[0]
     padded = -(-width // LANES) * LANES
-    geometry = (devices, fold_rows, folds, width, lat_cuts, lon_cuts, tiles)
+    geometry = (devices, fold_rows, folds, width)
     return pl.pallas_call(
         functools.partial(inverse_kernel, geometry),
         grid=(lons // step_lons,),
         in_specs=[
-            pl.BlockSpec(back.shape, lambda i: (0, 0, 0)),
+            pl.BlockSpec(back.shape, lambda i: (0, 0, 0), pipeline_mode=pl.Buffered(1)),
             pl.BlockSpec((total, step_lons), lambda i: (0, i)),
-            pl.BlockSpec((total, step_lons), lambda i: (0, i)),
-            pl.BlockSpec(tendency.shape, lambda i: (0, 0, 0, 0, 0)),
+            pl.BlockSpec((step_lons // LANES,) + tendency.shape[1:], lambda i: (i, 0, 0, 0, 0)),
         ],
         out_specs=pl.BlockSpec((chans, lats, step_lons), lambda i: (0, 0, i)),
         out_shape=jax.ShapeDtypeStruct(shape, F32),
         scratch_shapes=[pltpu.VMEM((total, padded), BF16), pltpu.VMEM((padded, total), BF16)],
-        compiler_params=params(56),
-        cost_estimate=cost(4 * total * width * lons, total * lons * 4 + width * lons * 6),
+        compiler_params=params(48),
+        cost_estimate=cost(2 * total * width * lons, total * lons * 2 + width * lons * 6),
         name="inverse_transform",
-    )(back, high, low, tendency)
+    )(back, basis, tendency)
 
 
 def cuts_of(lats, lons, groups):
@@ -425,7 +445,7 @@
     columns = exchange(cut)
     tables = basis_tables(pairs, lons, waves)
     step_rows = min(8, devices) * 4 * slots
-    spectra, high, low = forward_transform(state.reshape(chans * lats, lons), tables, devices, folds, step_rows)
+    spectra, basis = forward_transform(state.reshape(chans * lats, lons), tables, devices, folds, step_rows)
     got = lax.all_to_all(spectra, ("grp", "band"), 0, 0, tiled=True)
     tendency = physics(columns, mine, w_in, w_out)
     *tendency, pairs = lax.optimization_barrier((*tendency, pairs))
@@ -433,8 +453,8 @@
     own_pairs = lax.dynamic_slice_in_dim(pairs, device * slots, slots)
     solved = spectral_step(got, legendre, own_pairs, diffusion, groups, bands, folds, lons)
     back = lax.all_to_all(solved, ("grp", "band"), 0, 0, tiled=True)
-    tendency = gather_tendency(tendency, mine)
-    return inverse_transform(back, high, low, tendency, state.shape, lat_cuts, lon_cuts, 2 * LANES)
+    tendency = gather_tendency(tendency, mine, lat_cuts, lon_cuts)
+    return inverse_transform(back, basis, tendency, state.shape, 2 * LANES)
 
 
 def plain_basis(pair_index, points, waves):

time: 298 us -> 290 us (0.973)
  Pallas kernels: 73.8 us -> 68.5 us
    unnamed x48 -> x46, local copies, waits for them, and re-layouts: 18 us -> 15.7 us
where the time goes in v3:
time: 290 us; the launch traced here: 289 us
  waiting for transfers between devices  159 us (55%)
  Pallas kernels  68.5 us (24%)
  starting transfers between devices  37.8 us (13%)
  local copies, waits for them, and re-layouts  16.3 us (6%)
  other arithmetic  7.86 us (3%)
    ppermute x14, waiting for transfers between devices, exchange(): lax.ppermute(blocks[offset], 'grp', [(g, g ^ offset) for g in range(group...  159 us
    ppermute x14, starting transfers between devices, exchange(): lax.ppermute(blocks[offset], 'grp', [(g, g ^ offset) for g in range(group...  28.2 us
    pallas_call x1, Pallas kernels, spectral_step(): pl.pallas_call(functools.partial(spectral_kernel, geometry, points), grid...  21.9 us
    pallas_call x1, Pallas kernels, physics(): pl.pallas_call(functools.partial(physics_kernel, groups), grid_spec=pltpu...  17 us
    pallas_call x1, Pallas kernels, forward_transform(): pl.pallas_call(functools.partial(forward_kernel, owners, width, folds), g...  17 us
    unnamed x46, local copies, waits for them, and re-layouts  15.7 us
    pallas_call x1, Pallas kernels, inverse_transform(): pl.pallas_call(functools.partial(inverse_kernel, geometry), grid=(lons //...  8.51 us
    all_to_all x1, starting transfers between devices, fast(): got = lax.all_to_all(spectra, ('grp', 'band'), 0, 0, tiled=True)  6 us
  transfers between devices with their start and end apart: 16, of which 13 were waited for; matrix products, arithmetic and copies ran while one was open for 3% of the time, Pallas kernels for 6%

profile of v3, /device:TPU:12, one launch (start us, length us, event | category | flops | bytes accessed | tf_op | source)
XLA Modules:
  0.0 289.5 jit_solution(5865562723986243800)
XLA Ops:
  0.0 3.9 %cut_columns.1 = (bf16[10,5,24,128]{3,2,1,0:T(8,128)(2,1)}, bf16[10,5,24,128]{3,2,1,0:T(8,128)(2,1)}, bf16[10,5,24,128]{3,2,1,0:T(8,128)(2,1)}, bf16[10,5,24,128...) custom-call(s32[1]{0:T(128)} %bitcast.mine_ref, ...), custom_call_target="tpu_custom_call" | custom-call | bytes 7372800 | tf_op jit(solution)/shard_map/cut_columns/pallas_call | solution.py:69
  4.0 0.1 copy.18
  4.1 0.1 mul.66
  4.2 3.3 %fusion.10 = (f32[1024,128]{1,0:T(8,128)}, f32[1024,128]{1,0:T(8,128)}) fusion(s32[1024]{0:T(1024)S(1)} %mul.66), kind=kLoop, calls=%fused_computation.16 | loop fusion | flops 1179648 | bytes 1052672 | tf_op jit(solution)/shard_map/sin | solution.py:112
  7.5 3.6 %negate_select_fusion = (f32[1024,10]{1,0:T(8,128)}, f32[1024,10]{1,0:T(8,128)}) fusion(s32[10]{0:T(128)S(1)} %iota_multiply_fusion, s32[1024]{0:T(1024)S(1)} %mul.66, pred[1024]{0:T(1024)(128)(4,1)S(1)} %fusion.14), kind=kLoop, calls=%fused_computation.6 | loop fusion | flops 133120 | bytes 87080 | tf_op jit(solution)/shard_map/jit(_where)/select_n | solution.py:111
  11.1 17.0 %forward_transform.1 = (bf16[32,16,1920]{2,1,0:T(8,128)(2,1)}, bf16[1024,1280]{1,0:T(8,128)(2,1)}) custom-call(f32[960,1280]{1,0:T(8,128)} %bitcast.9, f32[1024,128]{1,0:T(8,128)} %get-tuple-element.80.cos_ref, f32[1024,128]{1,0:T(8,128)} %get-tuple-element.79.sin_ref, f32[1024,10]{1,0:T(8,128)} %get-tuple-element.78.by_cos_ref, ...), custom_call_target="tpu_custom_call" | custom-call | flops 7549747200 | bytes 12124160 | tf_op jit(solution)/shard_map/forward_transform/pallas_call | solution.py:143
  28.0 0.0 copy-start.19
  28.1 6.0 %all-to-all-start = ((bf16[32,16,1920]{2,1,0:T(8,128)(2,1)}), bf16[32,16,1920]{2,1,0:T(8,128)(2,1)S(1)}, u32[]{:S(2)}, u32[]{:S(2)}) async-start(bf16[32,16,1920]{2,1,0:T(8,128)(2,1)} %get-tuple-element.67), calls=%async_computation | async-start | bytes 3932160 | tf_op jit(solution)/shard_map/all_to_all | solution.py:449
  34.1 1.5 collective-permute-start
  35.6 0.6 collective-permute-start.1
  36.2 1.5 collective-permute-start.2
  37.6 2.4 collective-permute-start.3
  40.1 1.4 collective-permute-start.4
  41.5 15.2 %collective-permute-done.refs_1_ = bf16[10,5,24,128]{3,2,1,0:T(8,128)(2,1)S(1)} collective-permute-done((bf16[10,5,24,128]{3,2,1,0:T(8,128)(2,1)}, bf16[10,5,24,128]{3,2,1,0:T(8,128)(2,1)S(1)}, u32[]{:S(2)}, u32[]{:S(2)}) %collective-permute-start) | collective-permute-done | bytes 307232 | tf_op jit(solution)/shard_map/ppermute | solution.py:94
  56.6 3.2 %collective-permute-start.5 = (bf16[10,5,24,128]{3,2,1,0:T(8,128)(2,1)}, bf16[10,5,24,128]{3,2,1,0:T(8,128)(2,1)}, u32[]{:S(2)}, u32[]{:S(2)}) collective-permute-start(bf16[10,5,24,128]{3,2,1,0:T(8,128)(2,1)} %get-tuple-element.55), channel_id=1, source_target_pairs={{0,24},{4,28},{8,16},{12,20},{16,8},{20,12},{24,0},{28,4},{1,25},{... | collective-permute-start | bytes 921608 | tf_op jit(solution)/shard_map/ppermute | solution.py:94
  59.8 14.8 %collective-permute-done.1.refs_2_ = bf16[10,5,24,128]{3,2,1,0:T(8,128)(2,1)S(1)} collective-permute-done((bf16[10,5,24,128]{3,2,1,0:T(8,128)(2,1)}, bf16[10,5,24,128]{3,2,1,0:T(8,128)(2,1)S(1)}, u32[]{:S(2)}, u32[]{:S(2)}) %collective-permute-start.1) | collective-permute-done | bytes 307232 | tf_op jit(solution)/shard_map/ppermute | solution.py:94
  74.6 3.6 %collective-permute-start.6 = (bf16[10,5,24,128]{3,2,1,0:T(8,128)(2,1)}, bf16[10,5,24,128]{3,2,1,0:T(8,128)(2,1)}, u32[]{:S(2)}, u32[]{:S(2)}) collective-permute-start(bf16[10,5,24,128]{3,2,1,0:T(8,128)(2,1)} %get-tuple-element.56), channel_id=1, source_target_pairs={{0,28},{4,24},{8,20},{12,16},{16,12},{20,8},{24,4},{28,0},{1,29},{... | collective-permute-start | bytes 921608 | tf_op jit(solution)/shard_map/ppermute | solution.py:94
  78.2 0.1 reshape.30
  78.3 0.1 copy.19
  78.4 0.1 reshape.32.diffusion_ref
  78.5 0.0 copy-done.19
  78.5 0.9 copy.16
  79.3 6.8 %copy.20.legendre_ref = f32[8,513,384]{2,1,0:T(8,128)} copy(f32[8,513,384]{2,0,1:T(8,128)} %param.8) | data formatting | bytes 12607488 | tf_op args[2]
  86.1 1.0 multiply_bitcast_fusion.refs_8_
  87.1 0.0 collective-permute-done.2.refs_3_
  87.1 0.7 copy-done.2
  87.8 22.7 %collective-permute-done.3.refs_4_ = bf16[10,5,24,128]{3,2,1,0:T(8,128)(2,1)} collective-permute-done((bf16[10,5,24,128]{3,2,1,0:T(8,128)(2,1)}, bf16[10,5,24,128]{3,2,1,0:T(8,128)(2,1)}, u32[]{:S(2)}, u32[]{:S(2)}) %collective-permute-start.3) | collective-permute-done | bytes 307232 | tf_op jit(solution)/shard_map/ppermute | solution.py:94
  110.6 6.6 %collective-permute-done.4.refs_5_ = bf16[10,5,24,128]{3,2,1,0:T(8,128)(2,1)} collective-permute-done((bf16[10,5,24,128]{3,2,1,0:T(8,128)(2,1)}, bf16[10,5,24,128]{3,2,1,0:T(8,128)(2,1)}, u32[]{:S(2)}, u32[]{:S(2)}) %collective-permute-start.4) | collective-permute-done | bytes 307232 | tf_op jit(solution)/shard_map/ppermute | solution.py:94
  117.2 8.4 %collective-permute-done.5.refs_6_ = bf16[10,5,24,128]{3,2,1,0:T(8,128)(2,1)} collective-permute-done((bf16[10,5,24,128]{3,2,1,0:T(8,128)(2,1)}, bf16[10,5,24,128]{3,2,1,0:T(8,128)(2,1)}, u32[]{:S(2)}, u32[]{:S(2)}) %collective-permute-start.5) | collective-permute-done | bytes 307232 | tf_op jit(solution)/shard_map/ppermute | solution.py:94
  125.6 6.9 %collective-permute-done.6.refs_7_ = bf16[10,5,24,128]{3,2,1,0:T(8,128)(2,1)} collective-permute-done((bf16[10,5,24,128]{3,2,1,0:T(8,128)(2,1)}, bf16[10,5,24,128]{3,2,1,0:T(8,128)(2,1)}, u32[]{:S(2)}, u32[]{:S(2)}) %collective-permute-start.6) | collective-permute-done | bytes 307232 | tf_op jit(solution)/shard_map/ppermute | solution.py:94
  132.5 1.0 copy-done.3
  133.5 17.0 %physics.1 = (bf16[10,5,24,128]{3,2,1,0:T(8,128)(2,1)S(1)}, bf16[10,5,24,128]{3,2,1,0:T(8,128)(2,1)S(1)}, bf16[10,5,24,128]{3,2,1,0:T(8,128)(2,1)S(1)}, bf16[10,...) custom-call(s32[1]{0:T(128)} %bitcast.mine_ref, ...), custom_call_target="tpu_custom_call" | custom-call | flops 5033164800 | bytes 4915200 | tf_op jit(solution)/shard_map/physics/pallas_call | solution.py:202
  150.5 0.7 copy-done.4
  151.2 0.7 copy-done.6
  151.9 0.7 copy-done.8
  152.7 0.7 copy-done.10
  153.4 0.7 copy-done.12
  154.2 0.7 copy-done.14
  154.9 0.7 copy-done.16
  155.6 0.1 dynamic_slice.3.pairs_ref
  155.7 0.0 all-to-all-done.got_ref
  155.7 21.9 %spectral_step.1 = bf16[32,16,1920]{2,1,0:T(8,128)(2,1)S(1)} custom-call(s32[8]{0:T(128)S(1)} %dynamic_slice.3.pairs_ref, bf16[32,16,1920]{2,1,0:T(8,128)(2,1)S(1)} %all-to-all-done.got_ref, f32[8,513,384]{2,1,0:T(8,128)} %copy.20.legendre_ref, f32[80,1]{1,0:T(8,128)S(1)} %reshape.32.diffusion_ref), custom_call_target="tpu_custom_call" | custom-call | flops 5042995200 | bytes 6303744 | tf_op jit(solution)/shard_map/spectral_step/pallas_call | solution.py:340
  177.6 0.0 copy-start
  177.6 1.3 copy-done
  178.9 3.5 %all-to-all-start.1 = ((bf16[32,16,1920]{2,1,0:T(8,128)(2,1)}), bf16[32,16,1920]{2,1,0:T(8,128)(2,1)}, u32[]{:S(2)}, u32[]{:S(2)}) async-start(bf16[32,16,1920]{2,1,0:T(8,128)(2,1)} %copy-done), calls=%async_computation.1 | async-start | bytes 3932160 | tf_op jit(solution)/shard_map/all_to_all | solution.py:455
  182.4 1.5 collective-permute-start.7
  184.0 0.6 collective-permute-start.8
  184.5 1.5 collective-permute-start.9
  186.0 2.4 collective-permute-start.10
  188.5 0.0 copy-done.9
  188.5 1.4 collective-permute-start.11
  189.8 15.1 %collective-permute-done.7.refs_1_ = bf16[10,5,24,128]{3,2,1,0:T(8,128)(2,1)S(1)} collective-permute-done((bf16[10,5,24,128]{3,2,1,0:T(8,128)(2,1)S(1)}, bf16[10,5,24,128]{3,2,1,0:T(8,128)(2,1)S(1)}, u32[]{:S(2)}, u32[]{:S(2)}) %collective-permute-start.7) | collective-permute-done | bytes 307232 | tf_op jit(solution)/shard_map/ppermute | solution.py:94
  204.9 0.0 copy-done.7
  205.0 3.2 %collective-permute-start.12 = (bf16[10,5,24,128]{3,2,1,0:T(8,128)(2,1)S(1)}, bf16[10,5,24,128]{3,2,1,0:T(8,128)(2,1)S(1)}, u32[]{:S(2)}, u32[]{:S(2)}) collective-permute-start(bf16[10,5,24,128]{3,2,1,0:T(8,128)(2,1)S(1)} %copy-done.7), channel_id=1, source_target_pairs={{0,24},{4,28},{8,16},{12,20},{16,8},{20,12},{24,0},{28,4},{1,25},{... | collective-permute-start | bytes 921608 | tf_op jit(solution)/shard_map/ppermute | solution.py:94
  208.1 14.8 %collective-permute-done.8.refs_2_ = bf16[10,5,24,128]{3,2,1,0:T(8,128)(2,1)S(1)} collective-permute-done((bf16[10,5,24,128]{3,2,1,0:T(8,128)(2,1)S(1)}, bf16[10,5,24,128]{3,2,1,0:T(8,128)(2,1)S(1)}, u32[]{:S(2)}, u32[]{:S(2)}) %collective-permute-start.8) | collective-permute-done | bytes 307232 | tf_op jit(solution)/shard_map/ppermute | solution.py:94
  222.9 3.6 %collective-permute-start.13 = (bf16[10,5,24,128]{3,2,1,0:T(8,128)(2,1)S(1)}, bf16[10,5,24,128]{3,2,1,0:T(8,128)(2,1)S(1)}, u32[]{:S(2)}, u32[]{:S(2)}) collective-permute-start(bf16[10,5,24,128]{3,2,1,0:T(8,128)(2,1)S(1)} %copy-done.5), channel_id=1, source_target_pairs={{0,28},{4,24},{8,20},{12,16},{16,12},{20,8},{24,4},{28,0},{1,29},{... | collective-permute-start | bytes 921608 | tf_op jit(solution)/shard_map/ppermute | solution.py:94
  226.5 5.1 %collective-permute-done.9.refs_3_ = bf16[10,5,24,128]{3,2,1,0:T(8,128)(2,1)S(1)} collective-permute-done((bf16[10,5,24,128]{3,2,1,0:T(8,128)(2,1)S(1)}, bf16[10,5,24,128]{3,2,1,0:T(8,128)(2,1)S(1)}, u32[]{:S(2)}, u32[]{:S(2)}) %collective-permute-start.9) | collective-permute-done | bytes 307232 | tf_op jit(solution)/shard_map/ppermute | solution.py:94
  231.6 27.2 %collective-permute-done.10.refs_4_ = bf16[10,5,24,128]{3,2,1,0:T(8,128)(2,1)S(1)} collective-permute-done((bf16[10,5,24,128]{3,2,1,0:T(8,128)(2,1)S(1)}, bf16[10,5,24,128]{3,2,1,0:T(8,128)(2,1)S(1)}, u32[]{:S(2)}, u32[]{:S(2)}) %collective-permute-start.10) | collective-permute-done | bytes 307232 | tf_op jit(solution)/shard_map/ppermute | solution.py:94
  258.8 6.6 %collective-permute-done.11.refs_5_ = bf16[10,5,24,128]{3,2,1,0:T(8,128)(2,1)S(1)} collective-permute-done((bf16[10,5,24,128]{3,2,1,0:T(8,128)(2,1)S(1)}, bf16[10,5,24,128]{3,2,1,0:T(8,128)(2,1)S(1)}, u32[]{:S(2)}, u32[]{:S(2)}) %collective-permute-start.11) | collective-permute-done | bytes 307232 | tf_op jit(solution)/shard_map/ppermute | solution.py:94
  265.4 8.4 %collective-permute-done.12.refs_6_ = bf16[10,5,24,128]{3,2,1,0:T(8,128)(2,1)S(1)} collective-permute-done((bf16[10,5,24,128]{3,2,1,0:T(8,128)(2,1)S(1)}, bf16[10,5,24,128]{3,2,1,0:T(8,128)(2,1)S(1)}, u32[]{:S(2)}, u32[]{:S(2)}) %collective-permute-start.12) | collective-permute-done | bytes 307232 | tf_op jit(solution)/shard_map/ppermute | solution.py:94
  273.8 6.9 %collective-permute-done.13.refs_7_ = bf16[10,5,24,128]{3,2,1,0:T(8,128)(2,1)S(1)} collective-permute-done((bf16[10,5,24,128]{3,2,1,0:T(8,128)(2,1)S(1)}, bf16[10,5,24,128]{3,2,1,0:T(8,128)(2,1)S(1)}, u32[]{:S(2)}, u32[]{:S(2)}) %collective-permute-start.13) | collective-permute-done | bytes 307232 | tf_op jit(solution)/shard_map/ppermute | solution.py:94
  280.7 0.2 gather_tendency.1.tendency_ref
  281.0 0.0 all-to-all-done.1.back_ref
  281.0 8.5 %inverse_transform.1 = f32[10,96,1280]{2,1,0:T(8,128)} custom-call(bf16[32,16,1920]{2,1,0:T(8,128)(2,1)} %all-to-all-done.1.back_ref, bf16[1024,1280]{1,0:T(8,128)(2,1)} %get-tuple-element.68.basis_ref, bf16[10,4,10,24,128]{4,3,2,1,0:T(8,128)(2,1)S(1)} %gather_tendency.1.tendency_ref), custom_call_target="tpu_custom_call" | custom-call | flops 2516582400 | bytes 9994240 | tf_op jit(solution)/shard_map/inverse_transform/pallas_call | solution.py:399
  (33 shorter events, 0.1 us)
Async XLA Ops:
  0.0 3.9 %copy-start.20 = (s32[256]{0:T(256)S(1)}, s32[256]{0:T(256)}, u32[]{:S(2)}) copy-start(s32[256]{0:T(256)} %param.7) | copy-start | bytes 3076
  28.0 50.2 %copy-start.21 = (f32[80]{0:T(128)S(1)}, f32[80]{0:T(128)}, u32[]{:S(2)}) copy-start(f32[80]{0:T(128)} %param.9) | copy-start | bytes 964
  28.0 50.4 %copy-start.19 = (bf16[80,1024]{1,0:T(8,128)(2,1)S(1)}, bf16[80,1024]{1,0:T(8,128)(2,1)}, u32[]{:S(2)}) copy-start(bf16[80,1024]{1,0:T(8,128)(2,1)} %param.10) | copy-start | bytes 491524
  28.1 127.6 %all-to-all-start = ((bf16[32,16,1920]{2,1,0:T(8,128)(2,1)}), bf16[32,16,1920]{2,1,0:T(8,128)(2,1)S(1)}, u32[]{:S(2)}, u32[]{:S(2)}) async-start(bf16[32,16,1920]{2,1,0:T(8,128)(2,1)} %get-tuple-element.67), calls=%async_computation | async-start | bytes 3932160 | tf_op jit(solution)/shard_map/all_to_all | solution.py:449
  34.1 22.6 %collective-permute-start = (bf16[10,5,24,128]{3,2,1,0:T(8,128)(2,1)}, bf16[10,5,24,128]{3,2,1,0:T(8,128)(2,1)S(1)}, u32[]{:S(2)}, u32[]{:S(2)}) collective-permute-start(bf16[10,5,24,128]{3,2,1,0:T(8,128)(2,1)} %get-tuple-element.50), channel_id=1, source_target_pairs={{0,4},{4,0},{8,12},{12,8},{16,20},{20,16},{24,28},{28,24},{1,5},{5... | collective-permute-start | bytes 921608 | tf_op jit(solution)/shard_map/ppermute | solution.py:94
  35.6 39.0 %collective-permute-start.1 = (bf16[10,5,24,128]{3,2,1,0:T(8,128)(2,1)}, bf16[10,5,24,128]{3,2,1,0:T(8,128)(2,1)S(1)}, u32[]{:S(2)}, u32[]{:S(2)}) collective-permute-start(bf16[10,5,24,128]{3,2,1,0:T(8,128)(2,1)} %get-tuple-element.51), channel_id=1, source_target_pairs={{0,8},{4,12},{8,0},{12,4},{16,24},{20,28},{24,16},{28,20},{1,9},{5... | collective-permute-start | bytes 921608 | tf_op jit(solution)/shard_map/ppermute | solution.py:94
  36.2 50.9 %collective-permute-start.2 = (bf16[10,5,24,128]{3,2,1,0:T(8,128)(2,1)}, bf16[10,5,24,128]{3,2,1,0:T(8,128)(2,1)S(1)}, u32[]{:S(2)}, u32[]{:S(2)}) collective-permute-start(bf16[10,5,24,128]{3,2,1,0:T(8,128)(2,1)} %get-tuple-element.52), channel_id=1, source_target_pairs={{0,12},{4,8},{8,4},{12,0},{16,28},{20,24},{24,20},{28,16},{1,13},{... | collective-permute-start | bytes 921608 | tf_op jit(solution)/shard_map/ppermute | solution.py:94
  37.6 72.9 %collective-permute-start.3 = (bf16[10,5,24,128]{3,2,1,0:T(8,128)(2,1)}, bf16[10,5,24,128]{3,2,1,0:T(8,128)(2,1)}, u32[]{:S(2)}, u32[]{:S(2)}) collective-permute-start(bf16[10,5,24,128]{3,2,1,0:T(8,128)(2,1)} %get-tuple-element.53), channel_id=1, source_target_pairs={{0,16},{4,20},{8,24},{12,28},{16,0},{20,4},{24,8},{28,12},{1,17},{... | collective-permute-start | bytes 921608 | tf_op jit(solution)/shard_map/ppermute | solution.py:94
  40.1 77.1 %collective-permute-start.4 = (bf16[10,5,24,128]{3,2,1,0:T(8,128)(2,1)}, bf16[10,5,24,128]{3,2,1,0:T(8,128)(2,1)}, u32[]{:S(2)}, u32[]{:S(2)}) collective-permute-start(bf16[10,5,24,128]{3,2,1,0:T(8,128)(2,1)} %get-tuple-element.54), channel_id=1, source_target_pairs={{0,20},{4,16},{8,28},{12,24},{16,4},{20,0},{24,12},{28,8},{1,21},{... | collective-permute-start | bytes 921608 | tf_op jit(solution)/shard_map/ppermute | solution.py:94
  56.6 69.0 %collective-permute-start.5 = (bf16[10,5,24,128]{3,2,1,0:T(8,128)(2,1)}, bf16[10,5,24,128]{3,2,1,0:T(8,128)(2,1)}, u32[]{:S(2)}, u32[]{:S(2)}) collective-permute-start(bf16[10,5,24,128]{3,2,1,0:T(8,128)(2,1)} %get-tuple-element.55), channel_id=1, source_target_pairs={{0,24},{4,28},{8,16},{12,20},{16,8},{20,12},{24,0},{28,4},{1,25},{... | collective-permute-start | bytes 921608 | tf_op jit(solution)/shard_map/ppermute | solution.py:94
  74.6 57.9 %collective-permute-start.6 = (bf16[10,5,24,128]{3,2,1,0:T(8,128)(2,1)}, bf16[10,5,24,128]{3,2,1,0:T(8,128)(2,1)}, u32[]{:S(2)}, u32[]{:S(2)}) collective-permute-start(bf16[10,5,24,128]{3,2,1,0:T(8,128)(2,1)} %get-tuple-element.56), channel_id=1, source_target_pairs={{0,28},{4,24},{8,20},{12,16},{16,12},{20,8},{24,4},{28,0},{1,29},{... | collective-permute-start | bytes 921608 | tf_op jit(solution)/shard_map/ppermute | solution.py:94
  79.3 53.2 %copy-start.1 = (bf16[10,5,24,128]{3,2,1,0:T(8,128)(2,1)S(1)}, bf16[10,5,24,128]{3,2,1,0:T(8,128)(2,1)}, u32[]{:S(2)}) copy-start(bf16[10,5,24,128]{3,2,1,0:T(8,128)(2,1)} %get-tuple-element.49.refs_0_) | copy-start | bytes 921604
  79.3 53.2 %copy-start.18 = (bf16[1024,80]{0,1:T(8,128)(2,1)S(1)}, bf16[1024,80]{0,1:T(8,128)(2,1)}, u32[]{:S(2)}) copy-start(bf16[1024,80]{0,1:T(8,128)(2,1)} %param.11) | copy-start | bytes 491524
  87.1 0.7 copy-start.2
  132.5 1.0 copy-start.3
  150.5 0.7 copy-start.4
  151.2 0.7 copy-start.6
  151.9 0.7 copy-start.8
  152.7 0.7 copy-start.10
  153.4 0.7 copy-start.12
  154.2 0.7 copy-start.14
  154.9 0.7 copy-start.16
  177.6 1.3 copy-start
  178.9 3.6 %copy-start.17 = (bf16[10,5,24,128]{3,2,1,0:T(8,128)(2,1)S(1)}, bf16[10,5,24,128]{3,2,1,0:T(8,128)(2,1)}, u32[]{:S(2)}) copy-start(bf16[10,5,24,128]{3,2,1,0:T(8,128)(2,1)} %copy-done.16) | copy-start | bytes 921604
  178.9 5.1 %copy-start.15 = (bf16[10,5,24,128]{3,2,1,0:T(8,128)(2,1)S(1)}, bf16[10,5,24,128]{3,2,1,0:T(8,128)(2,1)}, u32[]{:S(2)}) copy-start(bf16[10,5,24,128]{3,2,1,0:T(8,128)(2,1)} %copy-done.14) | copy-start | bytes 921604
  178.9 5.7 %copy-start.13 = (bf16[10,5,24,128]{3,2,1,0:T(8,128)(2,1)S(1)}, bf16[10,5,24,128]{3,2,1,0:T(8,128)(2,1)}, u32[]{:S(2)}) copy-start(bf16[10,5,24,128]{3,2,1,0:T(8,128)(2,1)} %copy-done.12) | copy-start | bytes 921604
  178.9 7.1 %copy-start.11 = (bf16[10,5,24,128]{3,2,1,0:T(8,128)(2,1)S(1)}, bf16[10,5,24,128]{3,2,1,0:T(8,128)(2,1)}, u32[]{:S(2)}) copy-start(bf16[10,5,24,128]{3,2,1,0:T(8,128)(2,1)} %copy-done.10) | copy-start | bytes 921604
  178.9 9.6 %copy-start.9 = (bf16[10,5,24,128]{3,2,1,0:T(8,128)(2,1)S(1)}, bf16[10,5,24,128]{3,2,1,0:T(8,128)(2,1)}, u32[]{:S(2)}) copy-start(bf16[10,5,24,128]{3,2,1,0:T(8,128)(2,1)} %copy-done.8) | copy-start | bytes 921604
  178.9 26.1 %copy-start.7 = (bf16[10,5,24,128]{3,2,1,0:T(8,128)(2,1)S(1)}, bf16[10,5,24,128]{3,2,1,0:T(8,128)(2,1)}, u32[]{:S(2)}) copy-start(bf16[10,5,24,128]{3,2,1,0:T(8,128)(2,1)} %copy-done.6) | copy-start | bytes 921604
  178.9 44.0 %copy-start.5 = (bf16[10,5,24,128]{3,2,1,0:T(8,128)(2,1)S(1)}, bf16[10,5,24,128]{3,2,1,0:T(8,128)(2,1)}, u32[]{:S(2)}) copy-start(bf16[10,5,24,128]{3,2,1,0:T(8,128)(2,1)} %copy-done.4) | copy-start | bytes 921604
  178.9 102.0 %all-to-all-start.1 = ((bf16[32,16,1920]{2,1,0:T(8,128)(2,1)}), bf16[32,16,1920]{2,1,0:T(8,128)(2,1)}, u32[]{:S(2)}, u32[]{:S(2)}) async-start(bf16[32,16,1920]{2,1,0:T(8,128)(2,1)} %copy-done), calls=%async_computation.1 | async-start | bytes 3932160 | tf_op jit(solution)/shard_map/all_to_all | solution.py:455
  182.4 22.5 %collective-permute-start.7 = (bf16[10,5,24,128]{3,2,1,0:T(8,128)(2,1)S(1)}, bf16[10,5,24,128]{3,2,1,0:T(8,128)(2,1)S(1)}, u32[]{:S(2)}, u32[]{:S(2)}) collective-permute-start(bf16[10,5,24,128]{3,2,1,0:T(8,128)(2,1)S(1)} %copy-done.17), channel_id=1, source_target_pairs={{0,4},{4,0},{8,12},{12,8},{16,20},{20,16},{24,28},{28,24},{1,5},{5... | collective-permute-start | bytes 921608 | tf_op jit(solution)/shard_map/ppermute | solution.py:94
  184.0 39.0 %collective-permute-start.8 = (bf16[10,5,24,128]{3,2,1,0:T(8,128)(2,1)S(1)}, bf16[10,5,24,128]{3,2,1,0:T(8,128)(2,1)S(1)}, u32[]{:S(2)}, u32[]{:S(2)}) collective-permute-start(bf16[10,5,24,128]{3,2,1,0:T(8,128)(2,1)S(1)} %copy-done.15), channel_id=1, source_target_pairs={{0,8},{4,12},{8,0},{12,4},{16,24},{20,28},{24,16},{28,20},{1,9},{5... | collective-permute-start | bytes 921608 | tf_op jit(solution)/shard_map/ppermute | solution.py:94
  184.5 47.1 %collective-permute-start.9 = (bf16[10,5,24,128]{3,2,1,0:T(8,128)(2,1)S(1)}, bf16[10,5,24,128]{3,2,1,0:T(8,128)(2,1)S(1)}, u32[]{:S(2)}, u32[]{:S(2)}) collective-permute-start(bf16[10,5,24,128]{3,2,1,0:T(8,128)(2,1)S(1)} %copy-done.13), channel_id=1, source_target_pairs={{0,12},{4,8},{8,4},{12,0},{16,28},{20,24},{24,20},{28,16},{1,13},{... | collective-permute-start | bytes 921608 | tf_op jit(solution)/shard_map/ppermute | solution.py:94
  186.0 72.8 %collective-permute-start.10 = (bf16[10,5,24,128]{3,2,1,0:T(8,128)(2,1)S(1)}, bf16[10,5,24,128]{3,2,1,0:T(8,128)(2,1)S(1)}, u32[]{:S(2)}, u32[]{:S(2)}) collective-permute-start(bf16[10,5,24,128]{3,2,1,0:T(8,128)(2,1)S(1)} %copy-done.11), channel_id=1, source_target_pairs={{0,16},{4,20},{8,24},{12,28},{16,0},{20,4},{24,8},{28,12},{1,17},{... | collective-permute-start | bytes 921608 | tf_op jit(solution)/shard_map/ppermute | solution.py:94
  188.5 76.9 %collective-permute-start.11 = (bf16[10,5,24,128]{3,2,1,0:T(8,128)(2,1)S(1)}, bf16[10,5,24,128]{3,2,1,0:T(8,128)(2,1)S(1)}, u32[]{:S(2)}, u32[]{:S(2)}) collective-permute-start(bf16[10,5,24,128]{3,2,1,0:T(8,128)(2,1)S(1)} %copy-done.9), channel_id=1, source_target_pairs={{0,20},{4,16},{8,28},{12,24},{16,4},{20,0},{24,12},{28,8},{1,21},{... | collective-permute-start | bytes 921608 | tf_op jit(solution)/shard_map/ppermute | solution.py:94
  205.0 68.8 %collective-permute-start.12 = (bf16[10,5,24,128]{3,2,1,0:T(8,128)(2,1)S(1)}, bf16[10,5,24,128]{3,2,1,0:T(8,128)(2,1)S(1)}, u32[]{:S(2)}, u32[]{:S(2)}) collective-permute-start(bf16[10,5,24,128]{3,2,1,0:T(8,128)(2,1)S(1)} %copy-done.7), channel_id=1, source_target_pairs={{0,24},{4,28},{8,16},{12,20},{16,8},{20,12},{24,0},{28,4},{1,25},{... | collective-permute-start | bytes 921608 | tf_op jit(solution)/shard_map/ppermute | solution.py:94
  222.9 57.8 %collective-permute-start.13 = (bf16[10,5,24,128]{3,2,1,0:T(8,128)(2,1)S(1)}, bf16[10,5,24,128]{3,2,1,0:T(8,128)(2,1)S(1)}, u32[]{:S(2)}, u32[]{:S(2)}) collective-permute-start(bf16[10,5,24,128]{3,2,1,0:T(8,128)(2,1)S(1)} %copy-done.5), channel_id=1, source_target_pairs={{0,28},{4,24},{8,20},{12,16},{16,12},{20,8},{24,4},{28,0},{1,29},{... | collective-permute-start | bytes 921608 | tf_op jit(solution)/shard_map/ppermute | solution.py:94

commit v4 on v3

--- a/solution.py
+++ b/solution.py
@@ -112,11 +112,20 @@
     return jnp.cos(fine), jnp.sin(fine), by_cos, by_sin
 
 
-def forward_kernel(owners, width, folds, state_ref, cos_ref, sin_ref, by_cos_ref, by_sin_ref,
-                   out_ref, high_ref, low_ref, state_high, state_low):
+def forward_kernel(owners, folds, half_ref, state_ref, cos_ref, sin_ref, by_cos_ref, by_sin_ref,
+                   near_ref, far_ref, high_ref, low_ref, state_high, state_low):
+    chans, lats, points = state_ref.shape
+    part = lats // 2
+    width = chans * part
+    half = half_ref[0]
+
     @pl.when(pl.program_id(0) == 0)
     def _():
-        state_high[...], state_low[...] = halves(state_ref[...])
+        for side in range(2):
+            at = slice(side * width, (side + 1) * width)
+            rows = pl.ds(pl.multiple_of((half ^ side) * part, ROWS), part)
+            block = state_ref[:, rows, :].reshape(width, points)
+            state_high[at, :], state_low[at, :] = halves(block)
 
     cosine, sine = cos_ref[...], sin_ref[...]
     for tile in range(by_cos_ref.shape[1]):
@@ -126,47 +135,128 @@
     found = mm(high_ref[...], state_low[...], NT)
     found += mm(low_ref[...], state_high[...], NT)
     found += mm(high_ref[...], state_high[...], NT)
-    rows = out_ref.shape[1]
-    for owner in range(owners):
-        for fold in range(folds):
-            start = (owner * folds + fold) * rows
-            out_ref[owner, :, fold * width : (fold + 1) * width] = found[start : start + rows].astype(BF16)
-
-
-def forward_transform(flat, tables, devices, folds, step_rows):
-    width, points = flat.shape
+    rows = near_ref.shape[1]
+
+    def put(out_ref, lane):
+        for owner in range(owners):
+            for fold in range(folds):
+                start = (owner * folds + fold) * rows
+                out_ref[owner, :, fold * width : (fold + 1) * width] = found[
+                    start : start + rows, lane : lane + width
+                ].astype(BF16)
+
+    put(near_ref, 0)
+
+    @pl.when(pl.program_id(0) // (pl.num_programs(0) // 2) == half)
+    def _():
+        put(far_ref, width)
+
+
+def forward_transform(state, half, tables, devices, folds, step_rows):
+    chans, lats, points = state.shape
+    width = chans * lats
     total = tables[0].shape[0]
     per_owner = total // devices
     rows = per_owner // folds
     owners = step_rows // per_owner
+    steps = total // step_rows
     coarse = points // LANES
+    wide = folds * width // 2
+
+    def own_half(i, half):
+        return (jnp.clip(i - half[0] * (steps // 2), 0, steps // 2 - 1), 0, 0)
+
     return pl.pallas_call(
-        functools.partial(forward_kernel, owners, width, folds),
-        grid=(total // step_rows,),
-        in_specs=[
-            pl.BlockSpec((width, points), lambda i: (0, 0)),
-            pl.BlockSpec((step_rows, LANES), lambda i: (i, 0)),
-            pl.BlockSpec((step_rows, LANES), lambda i: (i, 0)),
-            pl.BlockSpec((step_rows, coarse), lambda i: (i, 0)),
-            pl.BlockSpec((step_rows, coarse), lambda i: (i, 0)),
-        ],
-        out_specs=[
-            pl.BlockSpec((owners, rows, folds * width), lambda i: (i, 0, 0)),
-            pl.BlockSpec((step_rows, points), lambda i: (i, 0)),
-        ],
+        functools.partial(forward_kernel, owners, folds),
+        grid_spec=pltpu.PrefetchScalarGridSpec(
+            num_scalar_prefetch=1,
+            grid=(steps,),
+            in_specs=[
+                pl.BlockSpec((chans, lats, points), lambda i, half: (0, 0, 0)),
+                pl.BlockSpec((step_rows, LANES), lambda i, half: (i, 0)),
+                pl.BlockSpec((step_rows, LANES), lambda i, half: (i, 0)),
+                pl.BlockSpec((step_rows, coarse), lambda i, half: (i, 0)),
+                pl.BlockSpec((step_rows, coarse), lambda i, half: (i, 0)),
+            ],
+            out_specs=[
+                pl.BlockSpec((owners, rows, wide), lambda i, half: (i, 0, 0)),
+                pl.BlockSpec((owners, rows, wide), own_half),
+                pl.BlockSpec((step_rows, points), lambda i, half: (i, 0)),
+            ],
+            scratch_shapes=[
+                pltpu.VMEM((step_rows, points), BF16),
+                pltpu.VMEM((width, points), BF16),
+                pltpu.VMEM((width, points), BF16),
+            ],
+        ),
         out_shape=[
-            jax.ShapeDtypeStruct((devices, rows, folds * width), BF16),
+            jax.ShapeDtypeStruct((devices, rows, wide), BF16),
+            jax.ShapeDtypeStruct((devices // 2, rows, wide), BF16),
             jax.ShapeDtypeStruct((total, points), BF16),
-        ],
-        scratch_shapes=[
-            pltpu.VMEM((step_rows, points), BF16),
-            pltpu.VMEM((width, points), BF16),
-            pltpu.VMEM((width, points), BF16),
         ],
         compiler_params=params(56),
         cost_estimate=cost(6 * total * width * points, width * points * 4 + total * (points * 4 + width * 2)),
         name="forward_transform",
-    )(flat, *tables)
+    )(half, state, *tables)
+
+
+def cross_kernel(owners, mine_ref, *refs):
+    blocks, (basis_ref, far_ref, out_ref, columns) = refs[:-4], refs[-4:]
+    quads = len(blocks)
+    chans, tiles, rows, _ = blocks[0].shape
+    span = chans * rows
+    far_rows = far_ref.shape[1]
+    cross_rows = out_ref.shape[1] - far_rows
+    folds = out_ref.shape[2] // span
+    per_owner = basis_ref.shape[0] // owners
+
+    @pl.when(pl.program_id(0) == 0)
+    def _():
+        for offset, block in enumerate(blocks):
+            place = pl.ds(pl.multiple_of((mine_ref[0] % quads ^ offset) * span, 2 * ROWS), span)
+            for tile in range(tiles):
+                columns[place, tile * LANES : (tile + 1) * LANES] = block[:, tile].reshape(span, LANES)
+
+    found = mm(basis_ref[...], columns[...], NT)
+    per_quad = per_owner // cross_rows
+    for owner in range(owners):
+        out_ref[owner, cross_rows : cross_rows + far_rows, :] = far_ref[owner]
+        for fold in range(folds):
+            quad, start = fold // per_quad, owner * per_owner + fold % per_quad * cross_rows
+            out_ref[owner, 0:cross_rows, fold * span : (fold + 1) * span] = found[
+                start : start + cross_rows, quad * span : (quad + 1) * span
+            ].astype(BF16)
+
+
+def cross_transform(blocks, far, basis, mine, devices, lon_cuts, step_rows):
+    quads = len(blocks)
+    chans, tiles, rows, _ = blocks[0].shape
+    span = chans * rows
+    per_owner = basis.shape[0] // devices
+    owners = step_rows // per_owner
+    steps = devices // 2 // owners
+    cross_rows = quads * per_owner * span // far.shape[2]
+    out = (devices // 2, cross_rows + far.shape[1], far.shape[2])
+    return pl.pallas_call(
+        functools.partial(cross_kernel, owners),
+        grid_spec=pltpu.PrefetchScalarGridSpec(
+            num_scalar_prefetch=1,
+            grid=(steps,),
+            in_specs=[pl.BlockSpec(blocks[0].shape, lambda i, mine: (0, 0, 0, 0))] * quads
+            + [
+                pl.BlockSpec(
+                    (step_rows, tiles * LANES), lambda i, mine: (mine[0] // quads * steps + i, mine[0] % lon_cuts)
+                ),
+                pl.BlockSpec((owners,) + far.shape[1:], lambda i, mine: (i, 0, 0)),
+            ],
+            out_specs=pl.BlockSpec((owners,) + out[1:], lambda i, mine: (i, 0, 0)),
+            scratch_shapes=[pltpu.VMEM((quads * span, tiles * LANES), BF16)],
+        ),
+        out_shape=jax.ShapeDtypeStruct(out, BF16),
+        compiler_params=params(48),
+        cost_estimate=cost(steps * step_rows * quads * span * tiles * LANES * 2, 8 << 20),
+        name="cross_transform",
+    )(mine, *blocks, basis, far)
 
 
 def physics_kernel(groups, mine_ref, *refs):
@@ -247,9 +337,13 @@
     )(mine, *parts)
 
 
-def spectral_kernel(geometry, points, pairs_ref, got_ref, legendre_ref, diffusion_ref, out_ref,
-                    rows_ref, block_ref, high_ref, low_ref):
-    groups, bands, slots, per_group, lats, folds = geometry
+def spectral_kernel(geometry, points, pairs_ref, got_ref, more_ref, legendre_ref, diffusion_ref, out_ref,
+                    rows_ref, near_ref, far_ref, cross_ref, block_ref, high_ref, low_ref):
+    groups, bands, slots, per_group, lats, folds, lon_cuts = geometry
+    half = pairs_ref[slots]
+    quads = groups // 2
+    part = lats // 2
+    rows = part * lon_cuts // quads
     devices = groups * bands
     per_device = 4 * slots
     fold_rows = per_device // folds
@@ -262,29 +356,60 @@
     spans = [(tile, tile * LANES, min(LANES, width - tile * LANES)) for tile in range(rows_ref.shape[0])]
     fill = rows_ref.shape[0] * LANES - width
 
+    def unpack(target, source, past, count, wide, pack):
+        for device in range(source.shape[0]):
+            for fold in range(pack):
+                start = device * count * pack + fold * count
+                for tile in range(target.shape[0]):
+                    lanes = min(LANES, wide - tile * LANES)
+                    at = fold * wide + tile * LANES
+                    target[tile, start : start + count, 0:lanes] = source[
+                        device, past : past + count, at : at + lanes
+                    ].astype(F32)
+
+    near_rows = got_ref.shape[1]
+    cross_rows = more_ref.shape[1] - near_rows
+
     @pl.when(slot == 0)
     def _():
-        for device in range(devices):
-            for fold in range(folds):
-                start = device * per_device + fold * fold_rows
-                for tile, at, lanes in spans:
-                    rows_ref[tile, start : start + fold_rows, 0:lanes] = got_ref[
-                        device, :, fold * width + at : fold * width + at + lanes
-                    ].astype(F32)
+        near = per_group * part
+        unpack(near_ref, got_ref, 0, near_rows, near, got_ref.shape[2] // near)
+        unpack(far_ref, more_ref, cross_rows, near_rows, near, got_ref.shape[2] // near)
+        unpack(cross_ref, more_ref, 0, cross_rows, per_group * rows, got_ref.shape[2] // (per_group * rows))
         high_ref[...] = jnp.zeros_like(high_ref)
         low_ref[...] = jnp.zeros_like(low_ref)
 
     def rows_of(band, wave):
         return pl.ds(band * per_device + 4 * slot + wave, groups, stride=bands * per_device)
 
+    def read(ref, start, stride):
+        where = pl.ds(start, quads, stride=stride)
+        return jnp.concatenate([ref[tile, where, :] for tile in range(ref.shape[0])], axis=1)
+
+    stride = bands * per_device
     for wave in range(4):
         for band in range(bands):
-            piece = jnp.concatenate([rows_ref[tile, rows_of(band, wave), :] for tile, _, _ in spans], axis=1)
+            at = band * per_device + 4 * slot + wave
+            own = read(near_ref, half * (quads * stride) + at, stride)
+            other = read(near_ref, (1 - half) * (quads * stride) + at, stride)
+            far = read(far_ref, at, stride)
+            cross = []
+            for cut in range(quads // lon_cuts):
+                total = None
+                for lon in range(lon_cuts):
+                    source = (cut * lon_cuts + lon) * bands + band
+                    term = read(cross_ref, source * quads * per_device + 4 * slot + wave, per_device)
+                    total = term if total is None else total + term
+                cross.append(total)
             for chan in range(per_group):
+                lanes = slice(chan * part, (chan + 1) * part)
+                crossed = jnp.concatenate([cut[:, chan * rows : (chan + 1) * rows] for cut in cross], axis=1)
+                here = jnp.concatenate([own[:, lanes], crossed], axis=0)
+                there = jnp.concatenate([far[:, lanes], other[:, lanes]], axis=0)
                 row = (wave * per_group + chan) * groups
-                block_ref[row : row + groups, band * lats : (band + 1) * lats] = piece[
-                    :, chan * lats : (chan + 1) * lats
-                ]
+                first_lat = band * lats
+                block_ref[row : row + groups, first_lat : first_lat + part] = jnp.where(half == 0, here, there)
+                block_ref[row : row + groups, first_lat + part : first_lat + lats] = jnp.where(half == 0, there, here)
     high, low = halves(legendre_ref[0])
     high_ref[0:degrees, :] = high
     low_ref[0:degrees, :] = low
@@ -314,6 +439,7 @@
             if fill:
                 pieces.append(jnp.zeros((groups, fill), F32))
             line = jnp.concatenate(pieces, axis=1)
+            line = jnp.where(half == 0, line, jnp.concatenate([line[quads:], line[:quads]], axis=0))
             for tile, at, _ in spans:
                 rows_ref[tile, rows_of(band, wave), :] = line[:, at : at + LANES]
 
@@ -328,14 +454,20 @@
                     ].astype(BF16)
 
 
-def spectral_step(got, legendre, own_pairs, diffusion, groups, bands, folds, points):
+def spectral_step(got, more, half, legendre, own_pairs, diffusion, groups, bands, folds, lon_cuts, points):
     slots, degrees, lat_total = legendre.shape
     lats = lat_total // bands
     chans = diffusion.shape[0]
     per_group = chans // groups
     padded = -(-degrees // LANES) * LANES
-    by_row = diffusion.reshape(groups, per_group).T.reshape(chans, 1)
-    geometry = (groups, bands, slots, per_group, lats, folds)
+    by_half = diffusion.reshape(2, groups // 2, per_group)
+    by_half = jnp.where(half == 0, by_half, by_half[::-1])
+    by_row = by_half.reshape(groups, per_group).T.reshape(chans, 1)
+    geometry = (groups, bands, slots, per_group, lats, folds, lon_cuts)
+    devices = groups * bands
+    near_tiles = -(-per_group * lats // 2 // LANES)
+    cross_tiles = -(-per_group * lats * lon_cuts // groups // LANES)
+    out = (devices, 4 * slots // folds, per_group * lats * folds)
     whole = lambda i, pairs: (0, 0, 0)
     return pl.pallas_call(
         functools.partial(spectral_kernel, geometry, points),
@@ -344,22 +476,26 @@
             grid=(slots,),
             in_specs=[
                 pl.BlockSpec(got.shape, whole),
+                pl.BlockSpec(more.shape, whole),
                 pl.BlockSpec((1, degrees, lat_total), lambda i, pairs: (i, 0, 0)),
                 pl.BlockSpec((chans, 1), lambda i, pairs: (0, 0)),
             ],
-            out_specs=pl.BlockSpec(got.shape, whole),
+            out_specs=pl.BlockSpec(out, whole),
             scratch_shapes=[
-                pltpu.VMEM((-(-per_group * lats // LANES), groups * bands * 4 * slots, LANES), F32),
+                pltpu.VMEM((-(-per_group * lats // LANES), devices * 4 * slots, LANES), F32),
+                pltpu.VMEM((near_tiles, devices * 4 * slots, LANES), F32),
+                pltpu.VMEM((near_tiles, devices // 2 * 4 * slots, LANES), F32),
+                pltpu.VMEM((cross_tiles, devices // 2 * (groups // 2) * 4 * slots, LANES), F32),
                 pltpu.VMEM((4 * chans, lat_total), F32),
                 pltpu.VMEM((padded, lat_total), BF16),
                 pltpu.VMEM((padded, lat_total), BF16),
             ],
         ),
-        out_shape=jax.ShapeDtypeStruct(got.shape, BF16),
+        out_shape=jax.ShapeDtypeStruct(out, BF16),
         compiler_params=params(48),
         cost_estimate=cost(40 * slots * chans * degrees * lat_total, slots * degrees * lat_total * 4),
         name="spectral_step",
-    )(own_pairs, got, legendre, by_row)
+    )(jnp.concatenate([own_pairs, half]), got, more, legendre, by_row)
 
 
 def inverse_kernel(geometry, back_ref, basis_ref, tendency_ref, out_ref, rows_ref, turned):
@@ -428,30 +564,54 @@
     return folds if per_device % (folds * 2 * ROWS) == 0 else None
 
 
+def halves_fit(chans, lats, lons, slots, groups):
+    cuts = cuts_of(lats, lons, groups)
+    if cuts is None or groups & (groups - 1) or cuts[0] % 2 or lons % (2 * LANES):
+        return False
+    near, span, per_device = chans * lats // 2, chans * lats // cuts[0], 4 * slots
+    folds = LANES // math.gcd(near, LANES)
+    rows = groups // 2 * per_device * span
+    return (
+        folds_of(2 * near, per_device) is not None
+        and per_device % (folds * ROWS) == 0
+        and span % (2 * ROWS) == 0
+        and rows % (folds * near * 2 * ROWS) == 0
+        and per_device % (rows // (folds * near)) == 0
+    )
+
+
 def fast(state, pair_of_slot, legendre, diffusion, w_in, w_out):
     groups = lax.axis_size("grp")
     bands = lax.axis_size("band")
     devices = groups * bands
+    quads = groups // 2
     chans, lats, lons = state.shape
     slots, degrees, _ = legendre.shape
     waves = degrees - 1
     lat_cuts, lon_cuts = cuts_of(lats, lons, groups)
     folds = folds_of(chans * lats, 4 * slots)
+    near_folds = LANES // math.gcd(chans * lats // 2, LANES)
     mine = lax.axis_index("grp")
     device = mine * bands + lax.axis_index("band")
     mine = mine.reshape(1)
+    half = mine // quads
+    halves_of = [list(range(side * quads * bands, (side + 1) * quads * bands)) for side in range(2)]
     cut = cut_columns(state, mine, lat_cuts, lon_cuts)
     *cut, pairs = lax.optimization_barrier((*cut, pair_of_slot))
     columns = exchange(cut)
     tables = basis_tables(pairs, lons, waves)
-    step_rows = min(8, devices) * 4 * slots
-    spectra, basis = forward_transform(state.reshape(chans * lats, lons), tables, devices, folds, step_rows)
-    got = lax.all_to_all(spectra, ("grp", "band"), 0, 0, tiled=True)
+    step_rows = min(8, devices // 2) * 4 * slots
+    near, far, basis = forward_transform(state, half, tables, devices, near_folds, step_rows)
+    got = lax.all_to_all(near, ("grp", "band"), 0, 0, tiled=True)
+    crossed = cross_transform(columns[quads:], far, basis, mine, devices, lon_cuts, step_rows)
+    more = lax.all_to_all(crossed, ("grp", "band"), 0, 0, tiled=True, axis_index_groups=halves_of)
     tendency = physics(columns, mine, w_in, w_out)
     *tendency, pairs = lax.optimization_barrier((*tendency, pairs))
     tendency = exchange(tendency)
     own_pairs = lax.dynamic_slice_in_dim(pairs, device * slots, slots)
-    solved = spectral_step(got, legendre, own_pairs, diffusion, groups, bands, folds, lons)
+    solved = spectral_step(
+        got, more, half, legendre, own_pairs, diffusion, groups, bands, folds, lon_cuts, lons
+    )
     back = lax.all_to_all(solved, ("grp", "band"), 0, 0, tiled=True)
     tendency = gather_tendency(tendency, mine, lat_cuts, lon_cuts)
     return inverse_transform(back, basis, tendency, state.shape, 2 * LANES)
@@ -557,10 +717,7 @@
 
 def shards(state, pair_of_slot, legendre, diffusion, w_in, w_out):
     chans, lats, lons = state.shape
-    groups = lax.axis_size("grp")
-    fits = groups & (groups - 1) == 0 and lats % ROWS == 0 and lons % (2 * LANES) == 0
-    fits = fits and cuts_of(lats, lons, groups) is not None
-    fits = fits and folds_of(chans * lats, 4 * legendre.shape[0]) is not None
+    fits = halves_fit(chans, lats, lons, legendre.shape[0], lax.axis_size("grp"))
     if not fits:
         return plain(state, pair_of_slot, legendre, diffusion, w_in, w_out)
     return fast(state, pair_of_slot, legendre, diffusion, w_in, w_out)

time: 290 us -> 323 us (1.11)
  waiting for transfers between devices: 159 us -> 174 us
  Pallas kernels: 68.5 us -> 77.5 us
  local copies, waits for them, and re-layouts: 16.3 us -> 23.1 us
    ppermute x14, waiting for transfers between devices: 159 us -> 174 us  [exchange(): lax.ppermute(blocks[offset], 'grp', [(g, g ^ offset) for g in range(group...]
    unnamed x46 -> x62, local copies, waits for them, and re-layouts: 15.7 us -> 22.5 us
    pallas_call x1, Pallas kernels: 21.9 us -> 28 us  [spectral_step(): pl.pallas_call(functools.partial(spectral_kernel, geometry, points), grid...]
    ppermute x14, starting transfers between devices: 28.2 us -> 23.6 us  [exchange(): lax.ppermute(blocks[offset], 'grp', [(g, g ^ offset) for g in range(group...]
    all_to_all x1 -> x2, starting transfers between devices: 6 us -> 10.3 us  [the longest x1 6 us: fast(): got = lax.all_to_all(near, ('grp', 'band'), 0, 0, tiled=True)]
    pallas_call x1 -> x2, Pallas kernels: 17 us -> 20 us  [the longest x1 17.3 us: forward_transform(): pl.pallas_call(functools.partial(forward_kernel, owners, folds), grid_spe...]
  transfers between devices with their start and end apart: 16 -> 17, of which waited for: 13 -> 12; matrix products, arithmetic and copies ran while one was open for 3% -> 3% of each run, Pallas kernels for 6% -> 6%
where the time goes in v4:
time: 323 us; the launch traced here: 322 us
  waiting for transfers between devices  174 us (54%)
  Pallas kernels  77.5 us (24%)
  starting transfers between devices  39.6 us (12%)
  local copies, waits for them, and re-layouts  23.1 us (7%)
  other arithmetic  7.91 us (2%)
    ppermute x14, waiting for transfers between devices, exchange(): lax.ppermute(blocks[offset], 'grp', [(g, g ^ offset) for g in range(group...  174 us
    pallas_call x1, Pallas kernels, spectral_step(): pl.pallas_call(functools.partial(spectral_kernel, geometry, points), grid...  28 us
    ppermute x14, starting transfers between devices, exchange(): lax.ppermute(blocks[offset], 'grp', [(g, g ^ offset) for g in range(group...  23.6 us
    unnamed x62, local copies, waits for them, and re-layouts  22.5 us
    pallas_call x1, Pallas kernels, forward_transform(): pl.pallas_call(functools.partial(forward_kernel, owners, folds), grid_spe...  17.3 us
    pallas_call x1, Pallas kernels, physics(): pl.pallas_call(functools.partial(physics_kernel, groups), grid_spec=pltpu...  16.9 us
    pallas_call x1, Pallas kernels, inverse_transform(): pl.pallas_call(functools.partial(inverse_kernel, geometry), grid=(lons //...  8.5 us
  transfers between devices with their start and end apart: 17, of which 12 were waited for; matrix products, arithmetic and copies ran while one was open for 3% of the time, Pallas kernels for 6%

profile of v4, /device:TPU:12, one launch (start us, length us, event | category | flops | bytes accessed | tf_op | source)
XLA Modules:
  0.0 322.2 jit_solution(8511334939042232378)
XLA Ops:
  0.0 3.9 %cut_columns.1 = (bf16[10,5,24,128]{3,2,1,0:T(8,128)(2,1)}, bf16[10,5,24,128]{3,2,1,0:T(8,128)(2,1)}, bf16[10,5,24,128]{3,2,1,0:T(8,128)(2,1)}, bf16[10,5,24,128...) custom-call(s32[1]{0:T(128)} %bitcast.mine_ref, ...), custom_call_target="tpu_custom_call" | custom-call | bytes 7372800 | tf_op jit(solution)/shard_map/cut_columns/pallas_call | solution.py:69
  4.0 0.1 copy.18
  4.1 0.1 mul.66
  4.2 3.3 %fusion.10 = (f32[1024,128]{1,0:T(8,128)}, f32[1024,128]{1,0:T(8,128)}) fusion(s32[1024]{0:T(1024)S(1)} %mul.66), kind=kLoop, calls=%fused_computation.16 | loop fusion | flops 1179648 | bytes 1052672 | tf_op jit(solution)/shard_map/sin | solution.py:112
  7.5 3.5 %negate_select_fusion = (f32[1024,10]{1,0:T(8,128)}, f32[1024,10]{1,0:T(8,128)}) fusion(s32[10]{0:T(128)S(1)} %iota_multiply_fusion, s32[1024]{0:T(1024)S(1)} %mul.66, pred[1024]{0:T(1024)(128)(4,1)S(1)} %fusion.14), kind=kLoop, calls=%fused_computation.6 | loop fusion | flops 133120 | bytes 87080 | tf_op jit(solution)/shard_map/jit(_where)/select_n | solution.py:111
  11.1 17.3 %forward_transform.1 = (bf16[32,8,1920]{2,1,0:T(8,128)(2,1)}, bf16[16,8,1920]{2,1,0:T(8,128)(2,1)}, bf16[1024,1280]{1,0:T(8,128)(2,1)}) custom-call(s32[1]{0:T(128)S(6)} %select_n.45.half_ref, f32[10,96,1280]{2,1,0:T(8,128)} %state_ref.3, f32[1024,128]{1,0:T(8,128)} %get-tuple-element.82.cos_ref, f32[1024,128]{1,0:T(8,128)} %get-tuple-element.81.sin_ref, ...), custom_call_target="tpu_custom_call" | custom-call | flops 7549747200 | bytes 12124160 | tf_op jit(solution)/shard_map/forward_transform/pallas_call | solution.py:169
  28.3 6.0 %all-to-all-start = ((bf16[32,8,1920]{2,1,0:T(8,128)(2,1)}), bf16[32,8,1920]{2,1,0:T(8,128)(2,1)S(1)}, u32[]{:S(2)}, u32[]{:S(2)}) async-start(bf16[32,8,1920]{2,1,0:T(8,128)(2,1)} %get-tuple-element.68), calls=%async_computation | async-start | bytes 1966080 | tf_op jit(solution)/shard_map/all_to_all | solution.py:605
  34.4 2.5 collective-permute-start.3
  36.9 1.4 collective-permute-start.4
  38.2 1.5 collective-permute-start.5
  39.7 0.5 collective-permute-start.6
  40.3 49.1 %collective-permute-done.3.refs_4_.refs_0_ = bf16[10,5,24,128]{3,2,1,0:T(8,128)(2,1)S(1)} collective-permute-done((bf16[10,5,24,128]{3,2,1,0:T(8,128)(2,1)S(1)}, bf16[10,5,24,128]{3,2,1,0:T(8,128)(2,1)S(1)}, u32[]{:S(2)}, u32[]{:S(2)}) %collective-permute-start.3) | collective-permute-done | bytes 307232 | tf_op jit(solution)/shard_map/ppermute | solution.py:94
  89.4 6.6 %collective-permute-done.4.refs_5_.refs_1_ = bf16[10,5,24,128]{3,2,1,0:T(8,128)(2,1)S(1)} collective-permute-done((bf16[10,5,24,128]{3,2,1,0:T(8,128)(2,1)S(1)}, bf16[10,5,24,128]{3,2,1,0:T(8,128)(2,1)S(1)}, u32[]{:S(2)}, u32[]{:S(2)}) %collective-permute-start.4) | collective-permute-done | bytes 307232 | tf_op jit(solution)/shard_map/ppermute | solution.py:94
  95.9 8.7 %collective-permute-done.5.refs_6_.refs_2_ = bf16[10,5,24,128]{3,2,1,0:T(8,128)(2,1)S(1)} collective-permute-done((bf16[10,5,24,128]{3,2,1,0:T(8,128)(2,1)S(1)}, bf16[10,5,24,128]{3,2,1,0:T(8,128)(2,1)S(1)}, u32[]{:S(2)}, u32[]{:S(2)}) %collective-permute-start.5) | collective-permute-done | bytes 307232 | tf_op jit(solution)/shard_map/ppermute | solution.py:94
  104.6 6.9 %collective-permute-done.6.refs_7_.refs_3_ = bf16[10,5,24,128]{3,2,1,0:T(8,128)(2,1)S(1)} collective-permute-done((bf16[10,5,24,128]{3,2,1,0:T(8,128)(2,1)S(1)}, bf16[10,5,24,128]{3,2,1,0:T(8,128)(2,1)S(1)}, u32[]{:S(2)}, u32[]{:S(2)}) %collective-permute-start.6) | collective-permute-done | bytes 307232 | tf_op jit(solution)/shard_map/ppermute | solution.py:94
  111.5 1.7 copy-done
  113.3 1.0 copy-done.1
  114.3 2.7 cross_transform.1
  117.0 0.7 copy-done.4
  117.7 4.4 %all-to-all-start.1 = ((bf16[16,24,1920]{2,1,0:T(8,128)(2,1)}), bf16[16,24,1920]{2,1,0:T(8,128)(2,1)S(1)}, u32[]{:S(2)}, u32[]{:S(2)}) async-start(bf16[16,24,1920]{2,1,0:T(8,128)(2,1)} %cross_transform.1), calls=%async_computation.1 | async-start | bytes 2949120 | tf_op jit(solution)/shard_map/all_to_all | solution.py:607
  122.1 1.5 collective-permute-start
  123.6 0.6 collective-permute-start.1
  124.2 1.5 collective-permute-start.2
  125.6 0.1 reshape.34
  125.7 0.1 copy.19
  125.8 0.1 reshape.37.diffusion_ref
  125.9 1.8 copy.16
  127.7 6.7 %copy.20.legendre_ref = f32[8,513,384]{2,1,0:T(8,128)} copy(f32[8,513,384]{2,0,1:T(8,128)} %param.8) | data formatting | bytes 12607488 | tf_op args[2]
  134.4 1.0 multiply_bitcast_fusion.refs_8_
  135.3 18.5 %collective-permute-done.refs_1_ = bf16[10,5,24,128]{3,2,1,0:T(8,128)(2,1)S(1)} collective-permute-done((bf16[10,5,24,128]{3,2,1,0:T(8,128)(2,1)}, bf16[10,5,24,128]{3,2,1,0:T(8,128)(2,1)S(1)}, u32[]{:S(2)}, u32[]{:S(2)}) %collective-permute-start) | collective-permute-done | bytes 307232 | tf_op jit(solution)/shard_map/ppermute | solution.py:94
  153.8 0.7 copy-done.17
  154.5 1.0 copy-done.3
  155.5 1.0 copy-done.5
  156.5 1.0 copy-done.6
  157.4 1.0 copy-done.18
  158.4 0.9 copy-done.23
  159.3 16.9 %physics.1 = (bf16[10,5,24,128]{3,2,1,0:T(8,128)(2,1)S(1)}, bf16[10,5,24,128]{3,2,1,0:T(8,128)(2,1)S(1)}, bf16[10,5,24,128]{3,2,1,0:T(8,128)(2,1)S(1)}, bf16[10,...) custom-call(s32[1]{0:T(128)} %bitcast.mine_ref, ...), custom_call_target="tpu_custom_call" | custom-call | flops 5033164800 | bytes 4915200 | tf_op jit(solution)/shard_map/physics/pallas_call | solution.py:292
  176.3 0.7 copy-done.7
  177.0 0.7 copy-done.9
  177.7 0.7 copy-done.11
  178.4 0.7 copy-done.13
  179.2 0.7 copy-done.15
  179.9 0.7 copy-done.19
  180.6 0.7 copy-done.21
  181.3 0.1 dynamic_slice.3
  181.4 0.1 pad_add_fusion.1.pairs_ref
  181.5 28.0 %spectral_step.1 = bf16[32,16,1920]{2,1,0:T(8,128)(2,1)} custom-call(s32[9]{0:T(128)S(1)} %pad_add_fusion.1.pairs_ref, bf16[32,8,1920]{2,1,0:T(8,128)(2,1)S(1)} %all-to-all-done.got_ref, bf16[16,24,1920]{2,1,0:T(8,128)(2,1)S(1)} %all-to-all-done.1.more_ref, f32[8,513,384]{2,1,0:T(8,128)} %copy.20.legendre_ref, f32[80,1]{1,0:T(8,128)S(1)} %reshape.37.diffusion_ref), custom_call_target="tpu_custom_call" | custom-call | flops 5042995200 | bytes 6303744 | tf_op jit(solution)/shard_map/spectral_step/pallas_call | solution.py:472
  209.5 5.7 %all-to-all-start.2 = ((bf16[32,16,1920]{2,1,0:T(8,128)(2,1)}), bf16[32,16,1920]{2,1,0:T(8,128)(2,1)}, u32[]{:S(2)}, u32[]{:S(2)}) async-start(bf16[32,16,1920]{2,1,0:T(8,128)(2,1)} %spectral_step.1), calls=%async_computation.2 | async-start | bytes 3932160 | tf_op jit(solution)/shard_map/all_to_all | solution.py:615
  215.2 1.5 collective-permute-start.7
  216.7 0.6 collective-permute-start.8
  217.3 1.5 collective-permute-start.9
  218.7 2.4 collective-permute-start.10
  221.2 1.4 collective-permute-start.11
  222.6 15.1 %collective-permute-done.7.refs_1_ = bf16[10,5,24,128]{3,2,1,0:T(8,128)(2,1)S(1)} collective-permute-done((bf16[10,5,24,128]{3,2,1,0:T(8,128)(2,1)S(1)}, bf16[10,5,24,128]{3,2,1,0:T(8,128)(2,1)S(1)}, u32[]{:S(2)}, u32[]{:S(2)}) %collective-permute-start.7) | collective-permute-done | bytes 307232 | tf_op jit(solution)/shard_map/ppermute | solution.py:94
  237.7 3.2 collective-permute-start.12
  240.8 14.8 %collective-permute-done.8.refs_2_ = bf16[10,5,24,128]{3,2,1,0:T(8,128)(2,1)S(1)} collective-permute-done((bf16[10,5,24,128]{3,2,1,0:T(8,128)(2,1)S(1)}, bf16[10,5,24,128]{3,2,1,0:T(8,128)(2,1)S(1)}, u32[]{:S(2)}, u32[]{:S(2)}) %collective-permute-start.8) | collective-permute-done | bytes 307232 | tf_op jit(solution)/shard_map/ppermute | solution.py:94
  255.7 3.6 %collective-permute-start.13 = (bf16[10,5,24,128]{3,2,1,0:T(8,128)(2,1)S(1)}, bf16[10,5,24,128]{3,2,1,0:T(8,128)(2,1)S(1)}, u32[]{:S(2)}, u32[]{:S(2)}) collective-permute-start(bf16[10,5,24,128]{3,2,1,0:T(8,128)(2,1)S(1)} %copy-done.8), channel_id=1, source_target_pairs={{0,28},{4,24},{8,20},{12,16},{16,12},{20,8},{24,4},{28,0},{1,29},{... | collective-permute-start | bytes 921608 | tf_op jit(solution)/shard_map/ppermute | solution.py:94
  259.2 5.1 %collective-permute-done.9.refs_3_ = bf16[10,5,24,128]{3,2,1,0:T(8,128)(2,1)S(1)} collective-permute-done((bf16[10,5,24,128]{3,2,1,0:T(8,128)(2,1)S(1)}, bf16[10,5,24,128]{3,2,1,0:T(8,128)(2,1)S(1)}, u32[]{:S(2)}, u32[]{:S(2)}) %collective-permute-start.9) | collective-permute-done | bytes 307232 | tf_op jit(solution)/shard_map/ppermute | solution.py:94
  264.3 27.2 %collective-permute-done.10.refs_4_ = bf16[10,5,24,128]{3,2,1,0:T(8,128)(2,1)S(1)} collective-permute-done((bf16[10,5,24,128]{3,2,1,0:T(8,128)(2,1)S(1)}, bf16[10,5,24,128]{3,2,1,0:T(8,128)(2,1)S(1)}, u32[]{:S(2)}, u32[]{:S(2)}) %collective-permute-start.10) | collective-permute-done | bytes 307232 | tf_op jit(solution)/shard_map/ppermute | solution.py:94
  291.5 6.6 %collective-permute-done.11.refs_5_ = bf16[10,5,24,128]{3,2,1,0:T(8,128)(2,1)S(1)} collective-permute-done((bf16[10,5,24,128]{3,2,1,0:T(8,128)(2,1)S(1)}, bf16[10,5,24,128]{3,2,1,0:T(8,128)(2,1)S(1)}, u32[]{:S(2)}, u32[]{:S(2)}) %collective-permute-start.11) | collective-permute-done | bytes 307232 | tf_op jit(solution)/shard_map/ppermute | solution.py:94
  298.1 8.4 %collective-permute-done.12.refs_6_ = bf16[10,5,24,128]{3,2,1,0:T(8,128)(2,1)S(1)} collective-permute-done((bf16[10,5,24,128]{3,2,1,0:T(8,128)(2,1)S(1)}, bf16[10,5,24,128]{3,2,1,0:T(8,128)(2,1)S(1)}, u32[]{:S(2)}, u32[]{:S(2)}) %collective-permute-start.12) | collective-permute-done | bytes 307232 | tf_op jit(solution)/shard_map/ppermute | solution.py:94
  306.5 6.9 %collective-permute-done.13.refs_7_ = bf16[10,5,24,128]{3,2,1,0:T(8,128)(2,1)S(1)} collective-permute-done((bf16[10,5,24,128]{3,2,1,0:T(8,128)(2,1)S(1)}, bf16[10,5,24,128]{3,2,1,0:T(8,128)(2,1)S(1)}, u32[]{:S(2)}, u32[]{:S(2)}) %collective-permute-start.13) | collective-permute-done | bytes 307232 | tf_op jit(solution)/shard_map/ppermute | solution.py:94
  313.5 0.2 gather_tendency.1.tendency_ref
  313.7 8.5 %inverse_transform.1 = f32[10,96,1280]{2,1,0:T(8,128)} custom-call(bf16[32,16,1920]{2,1,0:T(8,128)(2,1)} %all-to-all-done.2.back_ref, bf16[1024,1280]{1,0:T(8,128)(2,1)} %get-tuple-element.69.refs_4_.basis_ref, bf16[10,4,10,24,128]{4,3,2,1,0:T(8,128)(2,1)S(1)} %gather_tendency.1.tendency_ref), custom_call_target="tpu_custom_call" | custom-call | flops 2516582400 | bytes 9994240 | tf_op jit(solution)/shard_map/inverse_transform/pallas_call | solution.py:535
  (54 shorter events, 0.1 us)
Async XLA Ops:
  0.0 3.9 %copy-start.24 = (s32[256]{0:T(256)S(1)}, s32[256]{0:T(256)}, u32[]{:S(2)}) copy-start(s32[256]{0:T(256)} %param.7) | copy-start | bytes 3076
  11.1 23.3 %copy-start.29 = (bf16[10,5,24,128]{3,2,1,0:T(8,128)(2,1)S(1)}, bf16[10,5,24,128]{3,2,1,0:T(8,128)(2,1)}, u32[]{:S(2)}) copy-start(bf16[10,5,24,128]{3,2,1,0:T(8,128)(2,1)} %get-tuple-element.54) | copy-start | bytes 921604
  11.1 25.8 %copy-start.28 = (bf16[10,5,24,128]{3,2,1,0:T(8,128)(2,1)S(1)}, bf16[10,5,24,128]{3,2,1,0:T(8,128)(2,1)}, u32[]{:S(2)}) copy-start(bf16[10,5,24,128]{3,2,1,0:T(8,128)(2,1)} %get-tuple-element.55) | copy-start | bytes 921604
  11.1 27.2 %copy-start.27 = (bf16[10,5,24,128]{3,2,1,0:T(8,128)(2,1)S(1)}, bf16[10,5,24,128]{3,2,1,0:T(8,128)(2,1)}, u32[]{:S(2)}) copy-start(bf16[10,5,24,128]{3,2,1,0:T(8,128)(2,1)} %get-tuple-element.56) | copy-start | bytes 921604
  11.1 28.7 %copy-start.26 = (bf16[10,5,24,128]{3,2,1,0:T(8,128)(2,1)S(1)}, bf16[10,5,24,128]{3,2,1,0:T(8,128)(2,1)}, u32[]{:S(2)}) copy-start(bf16[10,5,24,128]{3,2,1,0:T(8,128)(2,1)} %get-tuple-element.57) | copy-start | bytes 921604
  28.3 89.4 %all-to-all-start = ((bf16[32,8,1920]{2,1,0:T(8,128)(2,1)}), bf16[32,8,1920]{2,1,0:T(8,128)(2,1)S(1)}, u32[]{:S(2)}, u32[]{:S(2)}) async-start(bf16[32,8,1920]{2,1,0:T(8,128)(2,1)} %get-tuple-element.68), calls=%async_computation | async-start | bytes 1966080 | tf_op jit(solution)/shard_map/all_to_all | solution.py:605
  34.4 55.0 %collective-permute-start.3 = (bf16[10,5,24,128]{3,2,1,0:T(8,128)(2,1)S(1)}, bf16[10,5,24,128]{3,2,1,0:T(8,128)(2,1)S(1)}, u32[]{:S(2)}, u32[]{:S(2)}) collective-permute-start(bf16[10,5,24,128]{3,2,1,0:T(8,128)(2,1)S(1)} %copy-done.29), channel_id=1, source_target_pairs={{0,16},{4,20},{8,24},{12,28},{16,0},{20,4},{24,8},{28,12},{1,17},{... | collective-permute-start | bytes 921608 | tf_op jit(solution)/shard_map/ppermute | solution.py:94
  36.9 59.1 %collective-permute-start.4 = (bf16[10,5,24,128]{3,2,1,0:T(8,128)(2,1)S(1)}, bf16[10,5,24,128]{3,2,1,0:T(8,128)(2,1)S(1)}, u32[]{:S(2)}, u32[]{:S(2)}) collective-permute-start(bf16[10,5,24,128]{3,2,1,0:T(8,128)(2,1)S(1)} %copy-done.28), channel_id=1, source_target_pairs={{0,20},{4,16},{8,28},{12,24},{16,4},{20,0},{24,12},{28,8},{1,21},{... | collective-permute-start | bytes 921608 | tf_op jit(solution)/shard_map/ppermute | solution.py:94
  38.2 66.4 %collective-permute-start.5 = (bf16[10,5,24,128]{3,2,1,0:T(8,128)(2,1)S(1)}, bf16[10,5,24,128]{3,2,1,0:T(8,128)(2,1)S(1)}, u32[]{:S(2)}, u32[]{:S(2)}) collective-permute-start(bf16[10,5,24,128]{3,2,1,0:T(8,128)(2,1)S(1)} %copy-done.27), channel_id=1, source_target_pairs={{0,24},{4,28},{8,16},{12,20},{16,8},{20,12},{24,0},{28,4},{1,25},{... | collective-permute-start | bytes 921608 | tf_op jit(solution)/shard_map/ppermute | solution.py:94
  39.7 71.8 %collective-permute-start.6 = (bf16[10,5,24,128]{3,2,1,0:T(8,128)(2,1)S(1)}, bf16[10,5,24,128]{3,2,1,0:T(8,128)(2,1)S(1)}, u32[]{:S(2)}, u32[]{:S(2)}) collective-permute-start(bf16[10,5,24,128]{3,2,1,0:T(8,128)(2,1)S(1)} %copy-done.26), channel_id=1, source_target_pairs={{0,28},{4,24},{8,20},{12,16},{16,12},{20,8},{24,4},{28,0},{1,29},{... | collective-permute-start | bytes 921608 | tf_op jit(solution)/shard_map/ppermute | solution.py:94
  104.6 12.4 %copy-start.2 = (bf16[10,5,24,128]{3,2,1,0:T(8,128)(2,1)}, bf16[10,5,24,128]{3,2,1,0:T(8,128)(2,1)S(1)}, u32[]{:S(2)}) copy-start(bf16[10,5,24,128]{3,2,1,0:T(8,128)(2,1)S(1)} %collective-permute-done.5.refs_6_.refs_2_) | copy-start | bytes 921604
  111.5 1.7 copy-start
  113.3 1.0 copy-start.1
  117.0 0.7 copy-start.4
  117.7 7.9 %copy-start.25 = (f32[80]{0:T(128)S(1)}, f32[80]{0:T(128)}, u32[]{:S(2)}) copy-start(f32[80]{0:T(128)} %param.9) | copy-start | bytes 964
  117.7 63.8 %all-to-all-start.1 = ((bf16[16,24,1920]{2,1,0:T(8,128)(2,1)}), bf16[16,24,1920]{2,1,0:T(8,128)(2,1)S(1)}, u32[]{:S(2)}, u32[]{:S(2)}) async-start(bf16[16,24,1920]{2,1,0:T(8,128)(2,1)} %cross_transform.1), calls=%async_computation.1 | async-start | bytes 2949120 | tf_op jit(solution)/shard_map/all_to_all | solution.py:607
  122.1 31.7 %collective-permute-start = (bf16[10,5,24,128]{3,2,1,0:T(8,128)(2,1)}, bf16[10,5,24,128]{3,2,1,0:T(8,128)(2,1)S(1)}, u32[]{:S(2)}, u32[]{:S(2)}) collective-permute-start(bf16[10,5,24,128]{3,2,1,0:T(8,128)(2,1)} %get-tuple-element.51), channel_id=1, source_target_pairs={{0,4},{4,0},{8,12},{12,8},{16,20},{20,16},{24,28},{28,24},{1,5},{5... | collective-permute-start | bytes 921608 | tf_op jit(solution)/shard_map/ppermute | solution.py:94
  123.6 30.9 %collective-permute-start.1 = (bf16[10,5,24,128]{3,2,1,0:T(8,128)(2,1)}, bf16[10,5,24,128]{3,2,1,0:T(8,128)(2,1)}, u32[]{:S(2)}, u32[]{:S(2)}) collective-permute-start(bf16[10,5,24,128]{3,2,1,0:T(8,128)(2,1)} %get-tuple-element.52), channel_id=1, source_target_pairs={{0,8},{4,12},{8,0},{12,4},{16,24},{20,28},{24,16},{28,20},{1,9},{5... | collective-permute-start | bytes 921608 | tf_op jit(solution)/shard_map/ppermute | solution.py:94
  124.2 30.4 %collective-permute-start.2 = (bf16[10,5,24,128]{3,2,1,0:T(8,128)(2,1)}, bf16[10,5,24,128]{3,2,1,0:T(8,128)(2,1)}, u32[]{:S(2)}, u32[]{:S(2)}) collective-permute-start(bf16[10,5,24,128]{3,2,1,0:T(8,128)(2,1)} %get-tuple-element.53), channel_id=1, source_target_pairs={{0,12},{4,8},{8,4},{12,0},{16,28},{20,24},{24,20},{28,16},{1,13},{... | collective-permute-start | bytes 921608 | tf_op jit(solution)/shard_map/ppermute | solution.py:94
  153.8 0.7 copy-start.17
  154.5 1.0 copy-start.3
  155.5 1.0 copy-start.5
  156.5 1.0 copy-start.6
  157.4 1.0 copy-start.18
  158.4 0.9 copy-start.23
  176.3 0.7 copy-start.7
  177.0 0.7 copy-start.9
  177.7 0.7 copy-start.11
  178.4 0.7 copy-start.13
  179.2 0.7 copy-start.15
  179.9 0.7 copy-start.19
  180.6 0.7 copy-start.21
  209.4 5.7 %copy-start.22 = (bf16[10,5,24,128]{3,2,1,0:T(8,128)(2,1)S(1)}, bf16[10,5,24,128]{3,2,1,0:T(8,128)(2,1)}, u32[]{:S(2)}) copy-start(bf16[10,5,24,128]{3,2,1,0:T(8,128)(2,1)} %copy-done.21) | copy-start | bytes 921604
  209.4 7.3 %copy-start.20 = (bf16[10,5,24,128]{3,2,1,0:T(8,128)(2,1)S(1)}, bf16[10,5,24,128]{3,2,1,0:T(8,128)(2,1)}, u32[]{:S(2)}) copy-start(bf16[10,5,24,128]{3,2,1,0:T(8,128)(2,1)} %copy-done.19) | copy-start | bytes 921604
  209.4 7.8 %copy-start.16 = (bf16[10,5,24,128]{3,2,1,0:T(8,128)(2,1)S(1)}, bf16[10,5,24,128]{3,2,1,0:T(8,128)(2,1)}, u32[]{:S(2)}) copy-start(bf16[10,5,24,128]{3,2,1,0:T(8,128)(2,1)} %copy-done.15) | copy-start | bytes 921604
  209.4 9.3 %copy-start.14 = (bf16[10,5,24,128]{3,2,1,0:T(8,128)(2,1)S(1)}, bf16[10,5,24,128]{3,2,1,0:T(8,128)(2,1)}, u32[]{:S(2)}) copy-start(bf16[10,5,24,128]{3,2,1,0:T(8,128)(2,1)} %copy-done.13) | copy-start | bytes 921604
  209.4 11.7 %copy-start.12 = (bf16[10,5,24,128]{3,2,1,0:T(8,128)(2,1)S(1)}, bf16[10,5,24,128]{3,2,1,0:T(8,128)(2,1)}, u32[]{:S(2)}) copy-start(bf16[10,5,24,128]{3,2,1,0:T(8,128)(2,1)} %copy-done.11) | copy-start | bytes 921604
  209.5 28.2 %copy-start.10 = (bf16[10,5,24,128]{3,2,1,0:T(8,128)(2,1)S(1)}, bf16[10,5,24,128]{3,2,1,0:T(8,128)(2,1)}, u32[]{:S(2)}) copy-start(bf16[10,5,24,128]{3,2,1,0:T(8,128)(2,1)} %copy-done.9) | copy-start | bytes 921604
  209.5 46.2 %copy-start.8 = (bf16[10,5,24,128]{3,2,1,0:T(8,128)(2,1)S(1)}, bf16[10,5,24,128]{3,2,1,0:T(8,128)(2,1)}, u32[]{:S(2)}) copy-start(bf16[10,5,24,128]{3,2,1,0:T(8,128)(2,1)} %copy-done.7) | copy-start | bytes 921604
  209.5 104.2 %all-to-all-start.2 = ((bf16[32,16,1920]{2,1,0:T(8,128)(2,1)}), bf16[32,16,1920]{2,1,0:T(8,128)(2,1)}, u32[]{:S(2)}, u32[]{:S(2)}) async-start(bf16[32,16,1920]{2,1,0:T(8,128)(2,1)} %spectral_step.1), calls=%async_computation.2 | async-start | bytes 3932160 | tf_op jit(solution)/shard_map/all_to_all | solution.py:615
  215.2 22.5 %collective-permute-start.7 = (bf16[10,5,24,128]{3,2,1,0:T(8,128)(2,1)S(1)}, bf16[10,5,24,128]{3,2,1,0:T(8,128)(2,1)S(1)}, u32[]{:S(2)}, u32[]{:S(2)}) collective-permute-start(bf16[10,5,24,128]{3,2,1,0:T(8,128)(2,1)S(1)} %copy-done.22), channel_id=1, source_target_pairs={{0,4},{4,0},{8,12},{12,8},{16,20},{20,16},{24,28},{28,24},{1,5},{5... | collective-permute-start | bytes 921608 | tf_op jit(solution)/shard_map/ppermute | solution.py:94
  216.7 39.0 %collective-permute-start.8 = (bf16[10,5,24,128]{3,2,1,0:T(8,128)(2,1)S(1)}, bf16[10,5,24,128]{3,2,1,0:T(8,128)(2,1)S(1)}, u32[]{:S(2)}, u32[]{:S(2)}) collective-permute-start(bf16[10,5,24,128]{3,2,1,0:T(8,128)(2,1)S(1)} %copy-done.20), channel_id=1, source_target_pairs={{0,8},{4,12},{8,0},{12,4},{16,24},{20,28},{24,16},{28,20},{1,9},{5... | collective-permute-start | bytes 921608 | tf_op jit(solution)/shard_map/ppermute | solution.py:94
  217.3 47.1 %collective-permute-start.9 = (bf16[10,5,24,128]{3,2,1,0:T(8,128)(2,1)S(1)}, bf16[10,5,24,128]{3,2,1,0:T(8,128)(2,1)S(1)}, u32[]{:S(2)}, u32[]{:S(2)}) collective-permute-start(bf16[10,5,24,128]{3,2,1,0:T(8,128)(2,1)S(1)} %copy-done.16), channel_id=1, source_target_pairs={{0,12},{4,8},{8,4},{12,0},{16,28},{20,24},{24,20},{28,16},{1,13},{... | collective-permute-start | bytes 921608 | tf_op jit(solution)/shard_map/ppermute | solution.py:94
  218.7 72.8 %collective-permute-start.10 = (bf16[10,5,24,128]{3,2,1,0:T(8,128)(2,1)S(1)}, bf16[10,5,24,128]{3,2,1,0:T(8,128)(2,1)S(1)}, u32[]{:S(2)}, u32[]{:S(2)}) collective-permute-start(bf16[10,5,24,128]{3,2,1,0:T(8,128)(2,1)S(1)} %copy-done.14), channel_id=1, source_target_pairs={{0,16},{4,20},{8,24},{12,28},{16,0},{20,4},{24,8},{28,12},{1,17},{... | collective-permute-start | bytes 921608 | tf_op jit(solution)/shard_map/ppermute | solution.py:94
  221.2 76.9 %collective-permute-start.11 = (bf16[10,5,24,128]{3,2,1,0:T(8,128)(2,1)S(1)}, bf16[10,5,24,128]{3,2,1,0:T(8,128)(2,1)S(1)}, u32[]{:S(2)}, u32[]{:S(2)}) collective-permute-start(bf16[10,5,24,128]{3,2,1,0:T(8,128)(2,1)S(1)} %copy-done.12), channel_id=1, source_target_pairs={{0,20},{4,16},{8,28},{12,24},{16,4},{20,0},{24,12},{28,8},{1,21},{... | collective-permute-start | bytes 921608 | tf_op jit(solution)/shard_map/ppermute | solution.py:94
  237.7 68.8 %collective-permute-start.12 = (bf16[10,5,24,128]{3,2,1,0:T(8,128)(2,1)S(1)}, bf16[10,5,24,128]{3,2,1,0:T(8,128)(2,1)S(1)}, u32[]{:S(2)}, u32[]{:S(2)}) collective-permute-start(bf16[10,5,24,128]{3,2,1,0:T(8,128)(2,1)S(1)} %copy-done.10), channel_id=1, source_target_pairs={{0,24},{4,28},{8,16},{12,20},{16,8},{20,12},{24,0},{28,4},{1,25},{... | collective-permute-start | bytes 921608 | tf_op jit(solution)/shard_map/ppermute | solution.py:94
  255.7 57.8 %collective-permute-start.13 = (bf16[10,5,24,128]{3,2,1,0:T(8,128)(2,1)S(1)}, bf16[10,5,24,128]{3,2,1,0:T(8,128)(2,1)S(1)}, u32[]{:S(2)}, u32[]{:S(2)}) collective-permute-start(bf16[10,5,24,128]{3,2,1,0:T(8,128)(2,1)S(1)} %copy-done.8), channel_id=1, source_target_pairs={{0,28},{4,24},{8,20},{12,16},{16,12},{20,8},{24,4},{28,0},{1,29},{... | collective-permute-start | bytes 921608 | tf_op jit(solution)/shard_map/ppermute | solution.py:94

commit v5 on v3

--- a/solution.py
+++ b/solution.py
@@ -34,14 +34,14 @@
     return pltpu.CompilerParams(dimension_semantics=("arbitrary",), vmem_limit_bytes=mib << 20)
 
 
-def cut_kernel(lon_cuts, mine_ref, state_ref, *refs):
+def cut_kernel(lon_cuts, first, mine_ref, state_ref, *refs):
     groups = len(refs) - 4
     out_refs, (wide, narrow, arrived, left) = refs[:groups], refs[groups:]
     _, tiles, rows, _ = out_refs[0].shape
     lons = tiles * LANES
 
     def fetch(offset):
-        group = mine_ref[0] ^ offset
+        group = mine_ref[0] ^ (first + offset)
         lat = pl.multiple_of(group // lon_cuts * rows, ROWS)
         lon = pl.multiple_of(group % lon_cuts * lons, LANES)
         block = state_ref.at[:, pl.ds(lat, rows), pl.ds(lon, lons)]
@@ -61,13 +61,12 @@
         store(offset).wait()
 
 
-def cut_columns(state, mine, lat_cuts, lon_cuts):
+def cut_columns(state, mine, lat_cuts, lon_cuts, first, groups):
     chans, lats, lons = state.shape
     rows, tiles = lats // lat_cuts, lons // lon_cuts // LANES
-    groups = lat_cuts * lon_cuts
     block = (chans, tiles, rows, LANES)
     return pl.pallas_call(
-        functools.partial(cut_kernel, lon_cuts),
+        functools.partial(cut_kernel, lon_cuts, first),
         grid_spec=pltpu.PrefetchScalarGridSpec(
             num_scalar_prefetch=1,
             grid=(1,),
@@ -82,7 +81,7 @@
         ),
         out_shape=[jax.ShapeDtypeStruct(block, BF16)] * groups,
         compiler_params=params(60),
-        cost_estimate=cost(0, state.size * 6),
+        cost_estimate=cost(0, groups * math.prod(block) * 6),
         name="cut_columns",
     )(mine, state)
 
@@ -369,7 +368,6 @@
 
     @pl.when(pl.program_id(0) == 0)
     def _():
-        rows_ref[...] = jnp.zeros_like(rows_ref)
         for device in range(devices):
             for fold in range(folds):
                 start = (device * folds + fold) * fold_rows
@@ -407,7 +405,7 @@
         out_specs=pl.BlockSpec((chans, lats, step_lons), lambda i: (0, 0, i)),
         out_shape=jax.ShapeDtypeStruct(shape, F32),
         scratch_shapes=[pltpu.VMEM((total, padded), BF16), pltpu.VMEM((padded, total), BF16)],
-        compiler_params=params(48),
+        compiler_params=params(51),
         cost_estimate=cost(2 * total * width * lons, total * lons * 2 + width * lons * 6),
         name="inverse_transform",
     )(back, basis, tendency)
@@ -440,8 +438,9 @@
     mine = lax.axis_index("grp")
     device = mine * bands + lax.axis_index("band")
     mine = mine.reshape(1)
-    cut = cut_columns(state, mine, lat_cuts, lon_cuts)
-    *cut, pairs = lax.optimization_barrier((*cut, pair_of_slot))
+    cut_far = cut_columns(state, mine, lat_cuts, lon_cuts, groups // 2, groups - groups // 2)
+    cut = [*cut_columns(state, mine, lat_cuts, lon_cuts, 0, groups // 2), *cut_far]
+    cut[0], pairs = lax.optimization_barrier((cut[0], pair_of_slot))
     columns = exchange(cut)
     tables = basis_tables(pairs, lons, waves)
     step_rows = min(8, devices) * 4 * slots
@@ -454,7 +453,7 @@
     solved = spectral_step(got, legendre, own_pairs, diffusion, groups, bands, folds, lons)
     back = lax.all_to_all(solved, ("grp", "band"), 0, 0, tiled=True)
     tendency = gather_tendency(tendency, mine, lat_cuts, lon_cuts)
-    return inverse_transform(back, basis, tendency, state.shape, 2 * LANES)
+    return inverse_transform(back, basis, tendency, state.shape, lons // 2)
 
 
 def plain_basis(pair_index, points, waves):

time: 290 us -> 288 us (level)
  waiting for transfers between devices: 159 us -> 156 us
    unnamed x46 -> x42, local copies, waits for them, and re-layouts: 15.7 us -> 16.8 us
  transfers between devices with their start and end apart: 16 -> 16, of which waited for: 13 -> 13; matrix products, arithmetic and copies ran while one was open for 3% -> 3% of each run, Pallas kernels for 6% -> 7%
where the time goes in v5:
time: 288 us
  waiting for transfers between devices  156 us (54%)
  Pallas kernels  68.4 us (24%)
  starting transfers between devices  37.8 us (13%)
  local copies, waits for them, and re-layouts  17.4 us (6%)
  other arithmetic  7.87 us (3%)
    ppermute x14, waiting for transfers between devices, exchange(): lax.ppermute(blocks[offset], 'grp', [(g, g ^ offset) for g in range(group...  156 us
    ppermute x14, starting transfers between devices, exchange(): lax.ppermute(blocks[offset], 'grp', [(g, g ^ offset) for g in range(group...  28.3 us
    pallas_call x1, Pallas kernels, spectral_step(): pl.pallas_call(functools.partial(spectral_kernel, geometry, points), grid...  21.9 us
    pallas_call x1, Pallas kernels, forward_transform(): pl.pallas_call(functools.partial(forward_kernel, owners, width, folds), g...  17 us
    pallas_call x1, Pallas kernels, physics(): pl.pallas_call(functools.partial(physics_kernel, groups), grid_spec=pltpu...  16.9 us
    unnamed x42, local copies, waits for them, and re-layouts  16.8 us
    pallas_call x1, Pallas kernels, inverse_transform(): pl.pallas_call(functools.partial(inverse_kernel, geometry), grid=(lons //...  7.43 us
    all_to_all x1, starting transfers between devices, fast(): got = lax.all_to_all(spectra, ('grp', 'band'), 0, 0, tiled=True)  6 us
  transfers between devices with their start and end apart: 16, of which 13 were waited for; matrix products, arithmetic and copies ran while one was open for 3% of the time, Pallas kernels for 7%

profile of v5, /device:TPU:12, one launch (start us, length us, event | category | flops | bytes accessed | tf_op | source)
XLA Modules:
  0.0 288.0 jit_solution(3889908749006115603)
XLA Ops:
  0.0 2.5 cut_columns.2
  2.5 0.1 copy.18
  2.7 0.1 mul.66
  2.8 3.3 %fusion.10 = (f32[1024,128]{1,0:T(8,128)}, f32[1024,128]{1,0:T(8,128)}) fusion(s32[1024]{0:T(1024)S(1)} %mul.66), kind=kLoop, calls=%fused_computation.16 | loop fusion | flops 1179648 | bytes 1052672 | tf_op jit(solution)/shard_map/sin | solution.py:111
  6.1 3.6 %negate_select_fusion = (f32[1024,10]{1,0:T(8,128)}, f32[1024,10]{1,0:T(8,128)}) fusion(s32[10]{0:T(128)S(1)} %iota_multiply_fusion, s32[1024]{0:T(1024)S(1)} %mul.66, pred[1024]{0:T(1024)(128)(4,1)S(1)} %fusion.14), kind=kLoop, calls=%fused_computation.6 | loop fusion | flops 133120 | bytes 87080 | tf_op jit(solution)/shard_map/jit(_where)/select_n | solution.py:110
  9.7 17.0 %forward_transform.1 = (bf16[32,16,1920]{2,1,0:T(8,128)(2,1)}, bf16[1024,1280]{1,0:T(8,128)(2,1)}) custom-call(f32[960,1280]{1,0:T(8,128)} %bitcast.9, f32[1024,128]{1,0:T(8,128)} %get-tuple-element.66.cos_ref, f32[1024,128]{1,0:T(8,128)} %get-tuple-element.65.sin_ref, f32[1024,10]{1,0:T(8,128)} %get-tuple-element.64.by_cos_ref, ...), custom_call_target="tpu_custom_call" | custom-call | flops 7549747200 | bytes 12124160 | tf_op jit(solution)/shard_map/forward_transform/pallas_call | solution.py:142
  26.7 6.0 %all-to-all-start = ((bf16[32,16,1920]{2,1,0:T(8,128)(2,1)}), bf16[32,16,1920]{2,1,0:T(8,128)(2,1)S(1)}, u32[]{:S(2)}, u32[]{:S(2)}) async-start(bf16[32,16,1920]{2,1,0:T(8,128)(2,1)} %get-tuple-element.53), calls=%async_computation | async-start | bytes 3932160 | tf_op jit(solution)/shard_map/all_to_all | solution.py:448
  32.7 0.0 copy-start.19
  32.7 0.0 copy-start.17
  32.7 1.5 collective-permute-start
  34.2 0.6 collective-permute-start.1
  34.8 1.5 collective-permute-start.2
  36.2 2.5 cut_columns.3
  38.7 2.5 collective-permute-start.3
  41.2 1.4 collective-permute-start.4
  42.6 12.6 %collective-permute-done.refs_1_ = bf16[10,5,24,128]{3,2,1,0:T(8,128)(2,1)S(1)} collective-permute-done((bf16[10,5,24,128]{3,2,1,0:T(8,128)(2,1)}, bf16[10,5,24,128]{3,2,1,0:T(8,128)(2,1)S(1)}, u32[]{:S(2)}, u32[]{:S(2)}) %collective-permute-start) | collective-permute-done | bytes 307232 | tf_op jit(solution)/shard_map/ppermute | solution.py:93
  55.2 3.2 %collective-permute-start.5 = (bf16[10,5,24,128]{3,2,1,0:T(8,128)(2,1)}, bf16[10,5,24,128]{3,2,1,0:T(8,128)(2,1)}, u32[]{:S(2)}, u32[]{:S(2)}) collective-permute-start(bf16[10,5,24,128]{3,2,1,0:T(8,128)(2,1)} %get-tuple-element.41), channel_id=1, source_target_pairs={{0,24},{4,28},{8,16},{12,20},{16,8},{20,12},{24,0},{28,4},{1,25},{... | collective-permute-start | bytes 921608 | tf_op jit(solution)/shard_map/ppermute | solution.py:93
  58.4 14.8 %collective-permute-done.1.refs_2_ = bf16[10,5,24,128]{3,2,1,0:T(8,128)(2,1)S(1)} collective-permute-done((bf16[10,5,24,128]{3,2,1,0:T(8,128)(2,1)}, bf16[10,5,24,128]{3,2,1,0:T(8,128)(2,1)S(1)}, u32[]{:S(2)}, u32[]{:S(2)}) %collective-permute-start.1) | collective-permute-done | bytes 307232 | tf_op jit(solution)/shard_map/ppermute | solution.py:93
  73.2 3.6 %collective-permute-start.6 = (bf16[10,5,24,128]{3,2,1,0:T(8,128)(2,1)}, bf16[10,5,24,128]{3,2,1,0:T(8,128)(2,1)}, u32[]{:S(2)}, u32[]{:S(2)}) collective-permute-start(bf16[10,5,24,128]{3,2,1,0:T(8,128)(2,1)} %get-tuple-element.42), channel_id=1, source_target_pairs={{0,28},{4,24},{8,20},{12,16},{16,12},{20,8},{24,4},{28,0},{1,29},{... | collective-permute-start | bytes 921608 | tf_op jit(solution)/shard_map/ppermute | solution.py:93
  76.8 0.1 reshape.30
  76.9 0.1 copy.19
  77.0 0.1 reshape.32.diffusion_ref
  77.1 0.8 copy.16
  77.9 6.8 %copy.20.legendre_ref = f32[8,513,384]{2,1,0:T(8,128)} copy(f32[8,513,384]{2,0,1:T(8,128)} %param.8) | data formatting | bytes 12607488 | tf_op args[2]
  84.7 1.0 multiply_bitcast_fusion.refs_8_
  85.7 0.0 collective-permute-done.2.refs_3_
  85.7 23.5 %collective-permute-done.3.refs_4_ = bf16[10,5,24,128]{3,2,1,0:T(8,128)(2,1)S(1)} collective-permute-done((bf16[10,5,24,128]{3,2,1,0:T(8,128)(2,1)}, bf16[10,5,24,128]{3,2,1,0:T(8,128)(2,1)S(1)}, u32[]{:S(2)}, u32[]{:S(2)}) %collective-permute-start.3) | collective-permute-done | bytes 307232 | tf_op jit(solution)/shard_map/ppermute | solution.py:93
  109.2 0.7 copy-done.3
  109.9 5.9 %collective-permute-done.4.refs_5_ = bf16[10,5,24,128]{3,2,1,0:T(8,128)(2,1)} collective-permute-done((bf16[10,5,24,128]{3,2,1,0:T(8,128)(2,1)}, bf16[10,5,24,128]{3,2,1,0:T(8,128)(2,1)}, u32[]{:S(2)}, u32[]{:S(2)}) %collective-permute-start.4) | collective-permute-done | bytes 307232 | tf_op jit(solution)/shard_map/ppermute | solution.py:93
  115.7 8.4 %collective-permute-done.5.refs_6_ = bf16[10,5,24,128]{3,2,1,0:T(8,128)(2,1)} collective-permute-done((bf16[10,5,24,128]{3,2,1,0:T(8,128)(2,1)}, bf16[10,5,24,128]{3,2,1,0:T(8,128)(2,1)}, u32[]{:S(2)}, u32[]{:S(2)}) %collective-permute-start.5) | collective-permute-done | bytes 307232 | tf_op jit(solution)/shard_map/ppermute | solution.py:93
  124.2 6.9 %collective-permute-done.6.refs_7_ = bf16[10,5,24,128]{3,2,1,0:T(8,128)(2,1)} collective-permute-done((bf16[10,5,24,128]{3,2,1,0:T(8,128)(2,1)}, bf16[10,5,24,128]{3,2,1,0:T(8,128)(2,1)}, u32[]{:S(2)}, u32[]{:S(2)}) %collective-permute-start.6) | collective-permute-done | bytes 307232 | tf_op jit(solution)/shard_map/ppermute | solution.py:93
  131.1 1.0 copy-done.4
  132.1 0.9 copy-done.16
  133.0 16.9 %physics.1 = (bf16[10,5,24,128]{3,2,1,0:T(8,128)(2,1)S(1)}, bf16[10,5,24,128]{3,2,1,0:T(8,128)(2,1)S(1)}, bf16[10,5,24,128]{3,2,1,0:T(8,128)(2,1)S(1)}, bf16[10,...) custom-call(s32[1]{0:T(128)} %bitcast.mine_ref, ...), custom_call_target="tpu_custom_call" | custom-call | flops 5033164800 | bytes 4915200 | tf_op jit(solution)/shard_map/physics/pallas_call | solution.py:201
  149.9 0.7 copy-done.5
  150.7 0.7 copy-done.7
  151.4 0.7 copy-done.9
  152.1 0.7 copy-done.11
  152.8 0.7 copy-done.13
  153.5 0.1 copy-done.14
  153.7 0.1 copy-done.15
  153.8 0.1 dynamic_slice.3.pairs_ref
  153.8 0.0 all-to-all-done.got_ref
  153.8 21.9 %spectral_step.1 = bf16[32,16,1920]{2,1,0:T(8,128)(2,1)S(1)} custom-call(s32[8]{0:T(128)S(1)} %dynamic_slice.3.pairs_ref, bf16[32,16,1920]{2,1,0:T(8,128)(2,1)S(1)} %all-to-all-done.got_ref, f32[8,513,384]{2,1,0:T(8,128)} %copy.20.legendre_ref, f32[80,1]{1,0:T(8,128)S(1)} %reshape.32.diffusion_ref), custom_call_target="tpu_custom_call" | custom-call | flops 5042995200 | bytes 6303744 | tf_op jit(solution)/shard_map/spectral_step/pallas_call | solution.py:339
  175.8 0.0 copy-start.1
  175.8 1.3 copy-done.1
  177.0 3.5 %all-to-all-start.1 = ((bf16[32,16,1920]{2,1,0:T(8,128)(2,1)}), bf16[32,16,1920]{2,1,0:T(8,128)(2,1)S(1)}, u32[]{:S(2)}, u32[]{:S(2)}) async-start(bf16[32,16,1920]{2,1,0:T(8,128)(2,1)} %copy-done.1), calls=%async_computation.1 | async-start | bytes 3932160 | tf_op jit(solution)/shard_map/all_to_all | solution.py:454
  180.5 1.5 collective-permute-start.7
  182.0 0.6 collective-permute-start.8
  182.6 1.5 collective-permute-start.9
  184.1 2.4 collective-permute-start.10
  186.5 1.4 collective-permute-start.11
  187.9 15.2 %collective-permute-done.7.refs_1_ = bf16[10,5,24,128]{3,2,1,0:T(8,128)(2,1)S(1)} collective-permute-done((bf16[10,5,24,128]{3,2,1,0:T(8,128)(2,1)}, bf16[10,5,24,128]{3,2,1,0:T(8,128)(2,1)S(1)}, u32[]{:S(2)}, u32[]{:S(2)}) %collective-permute-start.7) | collective-permute-done | bytes 307232 | tf_op jit(solution)/shard_map/ppermute | solution.py:93
  203.1 3.2 %collective-permute-start.12 = (bf16[10,5,24,128]{3,2,1,0:T(8,128)(2,1)S(1)}, bf16[10,5,24,128]{3,2,1,0:T(8,128)(2,1)S(1)}, u32[]{:S(2)}, u32[]{:S(2)}) collective-permute-start(bf16[10,5,24,128]{3,2,1,0:T(8,128)(2,1)S(1)} %copy-done.8), channel_id=1, source_target_pairs={{0,24},{4,28},{8,16},{12,20},{16,8},{20,12},{24,0},{28,4},{1,25},{... | collective-permute-start | bytes 921608 | tf_op jit(solution)/shard_map/ppermute | solution.py:93
  206.2 14.8 %collective-permute-done.8.refs_2_ = bf16[10,5,24,128]{3,2,1,0:T(8,128)(2,1)S(1)} collective-permute-done((bf16[10,5,24,128]{3,2,1,0:T(8,128)(2,1)}, bf16[10,5,24,128]{3,2,1,0:T(8,128)(2,1)S(1)}, u32[]{:S(2)}, u32[]{:S(2)}) %collective-permute-start.8) | collective-permute-done | bytes 307232 | tf_op jit(solution)/shard_map/ppermute | solution.py:93
  221.1 3.6 %collective-permute-start.13 = (bf16[10,5,24,128]{3,2,1,0:T(8,128)(2,1)S(1)}, bf16[10,5,24,128]{3,2,1,0:T(8,128)(2,1)S(1)}, u32[]{:S(2)}, u32[]{:S(2)}) collective-permute-start(bf16[10,5,24,128]{3,2,1,0:T(8,128)(2,1)S(1)} %copy-done.6), channel_id=1, source_target_pairs={{0,28},{4,24},{8,20},{12,16},{16,12},{20,8},{24,4},{28,0},{1,29},{... | collective-permute-start | bytes 921608 | tf_op jit(solution)/shard_map/ppermute | solution.py:93
  224.7 5.2 %collective-permute-done.9.refs_3_ = bf16[10,5,24,128]{3,2,1,0:T(8,128)(2,1)S(1)} collective-permute-done((bf16[10,5,24,128]{3,2,1,0:T(8,128)(2,1)}, bf16[10,5,24,128]{3,2,1,0:T(8,128)(2,1)S(1)}, u32[]{:S(2)}, u32[]{:S(2)}) %collective-permute-start.9) | collective-permute-done | bytes 307232 | tf_op jit(solution)/shard_map/ppermute | solution.py:93
  229.8 27.1 %collective-permute-done.10.refs_4_ = bf16[10,5,24,128]{3,2,1,0:T(8,128)(2,1)S(1)} collective-permute-done((bf16[10,5,24,128]{3,2,1,0:T(8,128)(2,1)S(1)}, bf16[10,5,24,128]{3,2,1,0:T(8,128)(2,1)S(1)}, u32[]{:S(2)}, u32[]{:S(2)}) %collective-permute-start.10) | collective-permute-done | bytes 307232 | tf_op jit(solution)/shard_map/ppermute | solution.py:93
  256.9 6.6 %collective-permute-done.11.refs_5_ = bf16[10,5,24,128]{3,2,1,0:T(8,128)(2,1)S(1)} collective-permute-done((bf16[10,5,24,128]{3,2,1,0:T(8,128)(2,1)S(1)}, bf16[10,5,24,128]{3,2,1,0:T(8,128)(2,1)S(1)}, u32[]{:S(2)}, u32[]{:S(2)}) %collective-permute-start.11) | collective-permute-done | bytes 307232 | tf_op jit(solution)/shard_map/ppermute | solution.py:93
  263.5 8.4 %collective-permute-done.12.refs_6_ = bf16[10,5,24,128]{3,2,1,0:T(8,128)(2,1)S(1)} collective-permute-done((bf16[10,5,24,128]{3,2,1,0:T(8,128)(2,1)S(1)}, bf16[10,5,24,128]{3,2,1,0:T(8,128)(2,1)S(1)}, u32[]{:S(2)}, u32[]{:S(2)}) %collective-permute-start.12) | collective-permute-done | bytes 307232 | tf_op jit(solution)/shard_map/ppermute | solution.py:93
  271.9 6.9 %collective-permute-done.13.refs_7_ = bf16[10,5,24,128]{3,2,1,0:T(8,128)(2,1)S(1)} collective-permute-done((bf16[10,5,24,128]{3,2,1,0:T(8,128)(2,1)S(1)}, bf16[10,5,24,128]{3,2,1,0:T(8,128)(2,1)S(1)}, u32[]{:S(2)}, u32[]{:S(2)}) %collective-permute-start.13) | collective-permute-done | bytes 307232 | tf_op jit(solution)/shard_map/ppermute | solution.py:93
  278.9 0.2 gather_tendency.1.tendency_ref
  279.1 1.4 copy-done
  280.5 7.4 %inverse_transform.1 = f32[10,96,1280]{2,1,0:T(8,128)} custom-call(bf16[32,16,1920]{2,1,0:T(8,128)(2,1)S(1)} %all-to-all-done.1.back_ref, bf16[1024,1280]{1,0:T(8,128)(2,1)} %get-tuple-element.54.basis_ref, bf16[10,4,10,24,128]{4,3,2,1,0:T(8,128)(2,1)} %copy-done), custom_call_target="tpu_custom_call" | custom-call | flops 2516582400 | bytes 9994240 | tf_op jit(solution)/shard_map/inverse_transform/pallas_call | solution.py:397
  (30 shorter events, 0.1 us)
Async XLA Ops:
  0.0 2.5 copy-start.18
  26.7 127.2 %all-to-all-start = ((bf16[32,16,1920]{2,1,0:T(8,128)(2,1)}), bf16[32,16,1920]{2,1,0:T(8,128)(2,1)S(1)}, u32[]{:S(2)}, u32[]{:S(2)}) async-start(bf16[32,16,1920]{2,1,0:T(8,128)(2,1)} %get-tuple-element.53), calls=%async_computation | async-start | bytes 3932160 | tf_op jit(solution)/shard_map/all_to_all | solution.py:448
  32.7 44.1 %copy-start.19 = (f32[80]{0:T(128)S(1)}, f32[80]{0:T(128)}, u32[]{:S(2)}) copy-start(f32[80]{0:T(128)} %param.9) | copy-start | bytes 964
  32.7 44.4 %copy-start.17 = (bf16[80,1024]{1,0:T(8,128)(2,1)S(1)}, bf16[80,1024]{1,0:T(8,128)(2,1)}, u32[]{:S(2)}) copy-start(bf16[80,1024]{1,0:T(8,128)(2,1)} %param.10) | copy-start | bytes 491524
  32.7 22.5 %collective-permute-start = (bf16[10,5,24,128]{3,2,1,0:T(8,128)(2,1)}, bf16[10,5,24,128]{3,2,1,0:T(8,128)(2,1)S(1)}, u32[]{:S(2)}, u32[]{:S(2)}) collective-permute-start(bf16[10,5,24,128]{3,2,1,0:T(8,128)(2,1)} %get-tuple-element.36), channel_id=1, source_target_pairs={{0,4},{4,0},{8,12},{12,8},{16,20},{20,16},{24,28},{28,24},{1,5},{5... | collective-permute-start | bytes 921608 | tf_op jit(solution)/shard_map/ppermute | solution.py:93
  34.2 39.0 %collective-permute-start.1 = (bf16[10,5,24,128]{3,2,1,0:T(8,128)(2,1)}, bf16[10,5,24,128]{3,2,1,0:T(8,128)(2,1)S(1)}, u32[]{:S(2)}, u32[]{:S(2)}) collective-permute-start(bf16[10,5,24,128]{3,2,1,0:T(8,128)(2,1)} %get-tuple-element.37), channel_id=1, source_target_pairs={{0,8},{4,12},{8,0},{12,4},{16,24},{20,28},{24,16},{28,20},{1,9},{5... | collective-permute-start | bytes 921608 | tf_op jit(solution)/shard_map/ppermute | solution.py:93
  34.8 50.9 %collective-permute-start.2 = (bf16[10,5,24,128]{3,2,1,0:T(8,128)(2,1)}, bf16[10,5,24,128]{3,2,1,0:T(8,128)(2,1)S(1)}, u32[]{:S(2)}, u32[]{:S(2)}) collective-permute-start(bf16[10,5,24,128]{3,2,1,0:T(8,128)(2,1)} %get-tuple-element.38), channel_id=1, source_target_pairs={{0,12},{4,8},{8,4},{12,0},{16,28},{20,24},{24,20},{28,16},{1,13},{... | collective-permute-start | bytes 921608 | tf_op jit(solution)/shard_map/ppermute | solution.py:93
  38.7 70.4 %collective-permute-start.3 = (bf16[10,5,24,128]{3,2,1,0:T(8,128)(2,1)}, bf16[10,5,24,128]{3,2,1,0:T(8,128)(2,1)S(1)}, u32[]{:S(2)}, u32[]{:S(2)}) collective-permute-start(bf16[10,5,24,128]{3,2,1,0:T(8,128)(2,1)} %get-tuple-element.39), channel_id=1, source_target_pairs={{0,16},{4,20},{8,24},{12,28},{16,0},{20,4},{24,8},{28,12},{1,17},{... | collective-permute-start | bytes 921608 | tf_op jit(solution)/shard_map/ppermute | solution.py:93
  41.2 74.5 %collective-permute-start.4 = (bf16[10,5,24,128]{3,2,1,0:T(8,128)(2,1)}, bf16[10,5,24,128]{3,2,1,0:T(8,128)(2,1)}, u32[]{:S(2)}, u32[]{:S(2)}) collective-permute-start(bf16[10,5,24,128]{3,2,1,0:T(8,128)(2,1)} %get-tuple-element.40), channel_id=1, source_target_pairs={{0,20},{4,16},{8,28},{12,24},{16,4},{20,0},{24,12},{28,8},{1,21},{... | collective-permute-start | bytes 921608 | tf_op jit(solution)/shard_map/ppermute | solution.py:93
  55.2 69.0 %collective-permute-start.5 = (bf16[10,5,24,128]{3,2,1,0:T(8,128)(2,1)}, bf16[10,5,24,128]{3,2,1,0:T(8,128)(2,1)}, u32[]{:S(2)}, u32[]{:S(2)}) collective-permute-start(bf16[10,5,24,128]{3,2,1,0:T(8,128)(2,1)} %get-tuple-element.41), channel_id=1, source_target_pairs={{0,24},{4,28},{8,16},{12,20},{16,8},{20,12},{24,0},{28,4},{1,25},{... | collective-permute-start | bytes 921608 | tf_op jit(solution)/shard_map/ppermute | solution.py:93
  73.2 57.9 %collective-permute-start.6 = (bf16[10,5,24,128]{3,2,1,0:T(8,128)(2,1)}, bf16[10,5,24,128]{3,2,1,0:T(8,128)(2,1)}, u32[]{:S(2)}, u32[]{:S(2)}) collective-permute-start(bf16[10,5,24,128]{3,2,1,0:T(8,128)(2,1)} %get-tuple-element.42), channel_id=1, source_target_pairs={{0,28},{4,24},{8,20},{12,16},{16,12},{20,8},{24,4},{28,0},{1,29},{... | collective-permute-start | bytes 921608 | tf_op jit(solution)/shard_map/ppermute | solution.py:93
  77.9 53.2 %copy-start.2 = (bf16[10,5,24,128]{3,2,1,0:T(8,128)(2,1)S(1)}, bf16[10,5,24,128]{3,2,1,0:T(8,128)(2,1)}, u32[]{:S(2)}) copy-start(bf16[10,5,24,128]{3,2,1,0:T(8,128)(2,1)} %get-tuple-element.35.refs_0_) | copy-start | bytes 921604
  109.2 0.7 copy-start.3
  131.1 1.0 copy-start.4
  132.1 0.9 copy-start.16
  149.9 0.7 copy-start.5
  150.7 0.7 copy-start.7
  151.4 0.7 copy-start.9
  152.1 0.7 copy-start.11
  152.8 0.7 copy-start.13
  152.8 0.9 copy-start.14
  152.8 1.0 copy-start.15
  175.8 1.3 copy-start.1
  177.0 7.0 %copy-start.12 = (bf16[10,5,24,128]{3,2,1,0:T(8,128)(2,1)S(1)}, bf16[10,5,24,128]{3,2,1,0:T(8,128)(2,1)}, u32[]{:S(2)}) copy-start(bf16[10,5,24,128]{3,2,1,0:T(8,128)(2,1)} %copy-done.11) | copy-start | bytes 921604
  177.0 9.5 %copy-start.10 = (bf16[10,5,24,128]{3,2,1,0:T(8,128)(2,1)S(1)}, bf16[10,5,24,128]{3,2,1,0:T(8,128)(2,1)}, u32[]{:S(2)}) copy-start(bf16[10,5,24,128]{3,2,1,0:T(8,128)(2,1)} %copy-done.9) | copy-start | bytes 921604
  177.0 26.0 %copy-start.8 = (bf16[10,5,24,128]{3,2,1,0:T(8,128)(2,1)S(1)}, bf16[10,5,24,128]{3,2,1,0:T(8,128)(2,1)}, u32[]{:S(2)}) copy-start(bf16[10,5,24,128]{3,2,1,0:T(8,128)(2,1)} %copy-done.7) | copy-start | bytes 921604
  177.0 44.0 %copy-start.6 = (bf16[10,5,24,128]{3,2,1,0:T(8,128)(2,1)S(1)}, bf16[10,5,24,128]{3,2,1,0:T(8,128)(2,1)}, u32[]{:S(2)}) copy-start(bf16[10,5,24,128]{3,2,1,0:T(8,128)(2,1)} %copy-done.5) | copy-start | bytes 921604
  177.0 103.5 %all-to-all-start.1 = ((bf16[32,16,1920]{2,1,0:T(8,128)(2,1)}), bf16[32,16,1920]{2,1,0:T(8,128)(2,1)S(1)}, u32[]{:S(2)}, u32[]{:S(2)}) async-start(bf16[32,16,1920]{2,1,0:T(8,128)(2,1)} %copy-done.1), calls=%async_computation.1 | async-start | bytes 3932160 | tf_op jit(solution)/shard_map/all_to_all | solution.py:454
  180.5 22.6 %collective-permute-start.7 = (bf16[10,5,24,128]{3,2,1,0:T(8,128)(2,1)}, bf16[10,5,24,128]{3,2,1,0:T(8,128)(2,1)S(1)}, u32[]{:S(2)}, u32[]{:S(2)}) collective-permute-start(bf16[10,5,24,128]{3,2,1,0:T(8,128)(2,1)} %copy-done.15), channel_id=1, source_target_pairs={{0,4},{4,0},{8,12},{12,8},{16,20},{20,16},{24,28},{28,24},{1,5},{5... | collective-permute-start | bytes 921608 | tf_op jit(solution)/shard_map/ppermute | solution.py:93
  182.0 39.0 %collective-permute-start.8 = (bf16[10,5,24,128]{3,2,1,0:T(8,128)(2,1)}, bf16[10,5,24,128]{3,2,1,0:T(8,128)(2,1)S(1)}, u32[]{:S(2)}, u32[]{:S(2)}) collective-permute-start(bf16[10,5,24,128]{3,2,1,0:T(8,128)(2,1)} %copy-done.14), channel_id=1, source_target_pairs={{0,8},{4,12},{8,0},{12,4},{16,24},{20,28},{24,16},{28,20},{1,9},{5... | collective-permute-start | bytes 921608 | tf_op jit(solution)/shard_map/ppermute | solution.py:93
  182.6 47.2 %collective-permute-start.9 = (bf16[10,5,24,128]{3,2,1,0:T(8,128)(2,1)}, bf16[10,5,24,128]{3,2,1,0:T(8,128)(2,1)S(1)}, u32[]{:S(2)}, u32[]{:S(2)}) collective-permute-start(bf16[10,5,24,128]{3,2,1,0:T(8,128)(2,1)} %copy-done.13), channel_id=1, source_target_pairs={{0,12},{4,8},{8,4},{12,0},{16,28},{20,24},{24,20},{28,16},{1,13},{... | collective-permute-start | bytes 921608 | tf_op jit(solution)/shard_map/ppermute | solution.py:93
  184.1 72.8 %collective-permute-start.10 = (bf16[10,5,24,128]{3,2,1,0:T(8,128)(2,1)S(1)}, bf16[10,5,24,128]{3,2,1,0:T(8,128)(2,1)S(1)}, u32[]{:S(2)}, u32[]{:S(2)}) collective-permute-start(bf16[10,5,24,128]{3,2,1,0:T(8,128)(2,1)S(1)} %copy-done.12), channel_id=1, source_target_pairs={{0,16},{4,20},{8,24},{12,28},{16,0},{20,4},{24,8},{28,12},{1,17},{... | collective-permute-start | bytes 921608 | tf_op jit(solution)/shard_map/ppermute | solution.py:93
  186.5 77.0 %collective-permute-start.11 = (bf16[10,5,24,128]{3,2,1,0:T(8,128)(2,1)S(1)}, bf16[10,5,24,128]{3,2,1,0:T(8,128)(2,1)S(1)}, u32[]{:S(2)}, u32[]{:S(2)}) collective-permute-start(bf16[10,5,24,128]{3,2,1,0:T(8,128)(2,1)S(1)} %copy-done.10), channel_id=1, source_target_pairs={{0,20},{4,16},{8,28},{12,24},{16,4},{20,0},{24,12},{28,8},{1,21},{... | collective-permute-start | bytes 921608 | tf_op jit(solution)/shard_map/ppermute | solution.py:93
  203.1 68.8 %collective-permute-start.12 = (bf16[10,5,24,128]{3,2,1,0:T(8,128)(2,1)S(1)}, bf16[10,5,24,128]{3,2,1,0:T(8,128)(2,1)S(1)}, u32[]{:S(2)}, u32[]{:S(2)}) collective-permute-start(bf16[10,5,24,128]{3,2,1,0:T(8,128)(2,1)S(1)} %copy-done.8), channel_id=1, source_target_pairs={{0,24},{4,28},{8,16},{12,20},{16,8},{20,12},{24,0},{28,4},{1,25},{... | collective-permute-start | bytes 921608 | tf_op jit(solution)/shard_map/ppermute | solution.py:93
  221.1 57.8 %collective-permute-start.13 = (bf16[10,5,24,128]{3,2,1,0:T(8,128)(2,1)S(1)}, bf16[10,5,24,128]{3,2,1,0:T(8,128)(2,1)S(1)}, u32[]{:S(2)}, u32[]{:S(2)}) collective-permute-start(bf16[10,5,24,128]{3,2,1,0:T(8,128)(2,1)S(1)} %copy-done.6), channel_id=1, source_target_pairs={{0,28},{4,24},{8,20},{12,16},{16,12},{20,8},{24,4},{28,0},{1,29},{... | collective-permute-start | bytes 921608 | tf_op jit(solution)/shard_map/ppermute | solution.py:93
  279.1 1.5 copy-start
